TPU v7x, 32 devices: a whole 2x2x4 slice. The times are simulated.
32 devices in a mesh: rep: 2 (over x), shard: 16 (over z, y, core).
Axes of the slice: x: 2, y: 2, z: 4, core: 2. Of those that a mesh axis runs over, the one named last changes fastest.
Arguments:
- tokens: bfloat16 [32, 192, 2048], P(('rep', 'shard')), may hold values from -7 to 7
- segment_ids: int32 [32, 192], P(('rep', 'shard')), may hold values from 0 to 3, never falling along the last dimension, each value on 1 to 96 neighbouring positions
- norm_gain: bfloat16 [2048], P('shard'), may hold values from 0.25 to 1.75
- input_weight: bfloat16 [2048, 2048], P('shard'), may hold values from -0.125 to 0.125
- forget_weight: bfloat16 [2048, 2048], P('shard'), may hold values from -0.5 to 0.5
- gate_weight: bfloat16 [2048, 2048], P('shard'), may hold values from -0.125 to 0.125
- mixer_gain: bfloat16 [2048], P('shard'), may hold values from 0.25 to 1.75
- out_weight: bfloat16 [2048, 2048], P('shard'), may hold values from -0.1875 to 0.1875
- ffn_gain: bfloat16 [2048], P('shard'), may hold values from 0.25 to 1.75
- ffn_gate_weight: bfloat16 [2048, 5632], P('shard'), may hold values from -0.125 to 0.125
- ffn_up_weight: bfloat16 [2048, 5632], P('shard'), may hold values from -0.125 to 0.125
- ffn_down_weight: bfloat16 [5632, 2048], P('shard'), may hold values from -0.15625 to 0.15625
- cotangent: bfloat16 [32, 192, 2048], P(('rep', 'shard')), may hold values from -6 to 6
Outputs:
- block_output: bfloat16 [32, 192, 2048], P(('rep', 'shard'))
- input_grad: bfloat16 [32, 192, 2048], P(('rep', 'shard'))
- norm_gain_grad: float32 [2048], P('shard')
- input_weight_grad: float32 [2048, 2048], P('shard')
- forget_weight_grad: float32 [2048, 2048], P('shard')
- gate_weight_grad: float32 [2048, 2048], P('shard')
- mixer_gain_grad: float32 [2048], P('shard')
- out_weight_grad: float32 [2048, 2048], P('shard')
- ffn_gain_grad: float32 [2048], P('shard')
- ffn_gate_grad: float32 [2048, 5632], P('shard')
- ffn_up_grad: float32 [2048, 5632], P('shard')
- ffn_down_grad: float32 [5632, 2048], P('shard')
Inputs may be any that keep to these rules, and one draw needn't show every extreme that they name: `segment_ids`: document numbers never fall along a sequence; each document has 1 to 96 tokens, and one has exactly 96.
All inputs are finite; a program needn't handle non-finite values.
Results may differ from a plain program's by a relative error of at most 0.019.
Values may be sent and summed in bfloat16 or wider, within the bound.
No kernel may reach another device: no remote copies, remote signals or barrier semaphores. Data moves between devices by JAX's collectives and lax.ppermute only.
A program may use at most 640 MiB of HBM per device.

v0:
```python
import jax
import jax.numpy as jnp
from jax import lax
from jax.sharding import PartitionSpec as P

EPSILON = 1e-06


def normalize(values):
    scale = lax.rsqrt(jnp.mean(values * values, axis=-1, keepdims=True) + EPSILON)
    return (values * scale, scale)


def norm_back(grad_scaled, scaled, scale):
    inner = jnp.mean(grad_scaled * scaled, axis=-1, keepdims=True)
    return scale * (grad_scaled - scaled * inner)


def swish_pair(values):
    sigma = jax.nn.sigmoid(values)
    return (values * sigma, sigma * (1.0 + values * (1.0 - sigma)))


def combine_steps(earlier, later):
    return (earlier[0] * later[0], later[0] * earlier[1] + later[1])


def linear_scan(decay, update):
    return lax.associative_scan(combine_steps, (decay, update), axis=0)[1]


def contract_rows(left, piece):
    return lax.dot_general(
        left, piece, (((1,), (1,)), ((), ())), preferred_element_type=jnp.float32
    )


def gain_folder(scaled, carry, pieces):
    sums, fulls, gain_full = carry
    gain_piece = pieces[-1]
    matrices = pieces[:-1]
    columns = scaled * gain_piece.astype(jnp.float32)
    lowered = columns.astype(jnp.bfloat16)
    sums = tuple(
        (jnp.dot(lowered, piece, preferred_element_type=jnp.float32) for piece in matrices)
    )
    gain_full = gain_piece
    return (sums, fulls, gain_full)


def plain_folder(lowered_rows, carry, piece):
    total, full = carry
    total = jnp.dot(lowered_rows, piece, preferred_element_type=jnp.float32)
    return (total, full)


def start_carry(length, width, columns, number):
    sums = tuple((jnp.zeros((length, columns), jnp.float32) for index in range(number)))
    fulls = ()
    return (sums, fulls, jnp.zeros((width,), jnp.bfloat16))


def single_columns(left, piece):
    return contract_rows(left, piece)


def multi_columns(lefts, pieces):
    total = contract_rows(lefts[0], pieces[0])
    for left, piece in zip(lefts[1:], pieces[1:]):
        total = total + contract_rows(left, piece)
    return total


def row_grad(left, right):
    return lax.dot_general(
        left, right, (((0,), (0,)), ((), ())), preferred_element_type=jnp.float32
    )


def row_block(pairs, gains):
    pieces = [row_grad(left, right) for left, right in pairs]
    pieces = pieces + [vector[:, None] for vector in gains]
    return jnp.concatenate(pieces, axis=1)


def shards(
    tokens,
    segment_ids,
    norm_gain,
    input_weight,
    forget_weight,
    gate_weight,
    mixer_gain,
    out_weight,
    ffn_gain,
    ffn_gate_weight,
    ffn_up_weight,
    ffn_down_weight,
    cotangent,
):
    inputs = tokens[0].astype(jnp.float32)
    length, width = inputs.shape
    hidden_width = ffn_up_weight.shape[1]
    segments = segment_ids[0]
    same = jnp.concatenate(
        [jnp.zeros((1,), jnp.float32), (segments[1:] == segments[:-1]).astype(jnp.float32)]
    )
    scaled_in, scale_in = normalize(inputs)
    mixer_sums, mixer_full, gain_one = gain_folder(
        scaled_in,
        start_carry(length, width, width, 3),
        (
            lax.all_gather(input_weight, "shard", axis=0, tiled=True),
            lax.all_gather(forget_weight, "shard", axis=0, tiled=True),
            lax.all_gather(gate_weight, "shard", axis=0, tiled=True),
            lax.all_gather(norm_gain, "shard", axis=0, tiled=True),
        ),
    )
    input_pre, forget_pre, gate_pre = mixer_sums
    forget = jax.nn.sigmoid(forget_pre)
    input_act, input_slope = swish_pair(input_pre)
    update = input_act * (1.0 - forget)
    decay = forget * same[:, None]
    state = linear_scan(decay, update)
    state_scaled, state_scale = normalize(state)
    gate_act, gate_slope = swish_pair(gate_pre)
    mixed_pre = state_scaled * gate_act
    out_sums, out_full, gain_two = gain_folder(
        mixed_pre,
        start_carry(length, width, width, 1),
        (
            lax.all_gather(out_weight, "shard", axis=0, tiled=True),
            lax.all_gather(mixer_gain, "shard", axis=0, tiled=True),
        ),
    )
    resid = inputs + out_sums[0]
    scaled_mid, scale_mid = normalize(resid)
    ffn_sums, ffn_full, gain_three = gain_folder(
        scaled_mid,
        start_carry(length, width, hidden_width, 2),
        (
            lax.all_gather(ffn_gate_weight, "shard", axis=0, tiled=True),
            lax.all_gather(ffn_up_weight, "shard", axis=0, tiled=True),
            lax.all_gather(ffn_gain, "shard", axis=0, tiled=True),
        ),
    )
    ffn_gate, ffn_up = ffn_sums
    ffn_act, ffn_slope = swish_pair(ffn_gate)
    hidden = (ffn_act * ffn_up).astype(jnp.bfloat16)
    down_start = (jnp.zeros((length, width), jnp.float32), jnp.zeros((1, 1), jnp.bfloat16))
    ffn_out, down_full = plain_folder(
        hidden, down_start, lax.all_gather(ffn_down_weight, "shard", axis=0, tiled=True)
    )
    block_output = (resid + ffn_out).astype(jnp.bfloat16)
    grad_out = cotangent[0]
    grad_hidden = single_columns(
        grad_out, lax.all_gather(ffn_down_weight, "shard", axis=0, tiled=True)
    )
    grad_fgate = (grad_hidden * ffn_up * ffn_slope).astype(jnp.bfloat16)
    grad_fup = (grad_hidden * ffn_act).astype(jnp.bfloat16)
    grad_ffn_in = multi_columns(
        (grad_fgate, grad_fup),
        lax.all_gather((ffn_gate_weight, ffn_up_weight), "shard", axis=0, tiled=True),
    )
    gain_three_f = gain_three.astype(jnp.float32)
    mid_low = (scaled_mid * gain_three_f).astype(jnp.bfloat16)
    gain_three_grad = jnp.sum(grad_ffn_in * scaled_mid, axis=0)
    grad_resid = grad_out.astype(jnp.float32) + norm_back(
        grad_ffn_in * gain_three_f, scaled_mid, scale_mid
    )
    grad_branch = grad_resid.astype(jnp.bfloat16)
    grad_mixed = single_columns(
        grad_branch, lax.all_gather(out_weight, "shard", axis=0, tiled=True)
    )
    gain_two_f = gain_two.astype(jnp.float32)
    mixed_low = (mixed_pre * gain_two_f).astype(jnp.bfloat16)
    gain_two_grad = jnp.sum(grad_mixed * mixed_pre, axis=0)
    weighted = grad_mixed * gain_two_f
    grad_gate_pre = (weighted * state_scaled * gate_slope).astype(jnp.bfloat16)
    grad_state = norm_back(weighted * gate_act, state_scaled, state_scale)
    next_decay = jnp.concatenate([decay[1:], jnp.zeros((1, width), jnp.float32)])
    carried = jnp.flip(linear_scan(jnp.flip(next_decay, 0), jnp.flip(grad_state, 0)), 0)
    previous = jnp.concatenate([jnp.zeros((1, width), jnp.float32), state[:-1]])
    grad_forget = carried * previous * same[:, None] - carried * input_act
    grad_input_pre = (carried * (1.0 - forget) * input_slope).astype(jnp.bfloat16)
    grad_forget_pre = (grad_forget * forget * (1.0 - forget)).astype(jnp.bfloat16)
    triple = (grad_input_pre, grad_forget_pre, grad_gate_pre)
    grad_normed = multi_columns(
        triple,
        lax.all_gather((input_weight, forget_weight, gate_weight), "shard", axis=0, tiled=True),
    )
    gain_one_f = gain_one.astype(jnp.float32)
    in_low = (scaled_in * gain_one_f).astype(jnp.bfloat16)
    gain_one_grad = jnp.sum(grad_normed * scaled_in, axis=0)
    input_grad = (grad_resid + norm_back(grad_normed * gain_one_f, scaled_in, scale_in)).astype(
        jnp.bfloat16
    )
    triple_joined = jnp.concatenate(triple, axis=1)
    pair_joined = jnp.concatenate([grad_fgate, grad_fup], axis=1)
    pairs = ((in_low, triple_joined), (mixed_low, grad_branch), (mid_low, pair_joined))
    gains = (gain_one_grad, gain_two_grad, gain_three_grad)
    rows_term = lax.psum_scatter(
        row_block(pairs, gains).astype(jnp.bfloat16), "shard", scatter_dimension=0, tiled=True
    )
    down_term = lax.psum_scatter(
        row_grad(hidden, grad_out).astype(jnp.bfloat16), "shard", scatter_dimension=0, tiled=True
    )
    rows_total, down_total = (
        lax.psum(rows_term, "rep").astype(jnp.float32),
        lax.psum(down_term, "rep").astype(jnp.float32),
    )
    tail = 4 * width + 2 * hidden_width
    return (
        block_output[None],
        input_grad[None],
        rows_total[:, tail],
        rows_total[:, :width],
        rows_total[:, width : 2 * width],
        rows_total[:, 2 * width : 3 * width],
        rows_total[:, tail + 1],
        rows_total[:, 3 * width : 4 * width],
        rows_total[:, tail + 2],
        rows_total[:, 4 * width : 4 * width + hidden_width],
        rows_total[:, 4 * width + hidden_width : tail],
        down_total,
    )


def solution(mesh):
    placed = (
        P(("rep", "shard"), None, None),
        P(("rep", "shard"), None),
        P("shard"),
        P("shard", None),
        P("shard", None),
        P("shard", None),
        P("shard"),
        P("shard", None),
        P("shard"),
        P("shard", None),
        P("shard", None),
        P("shard", None),
        P(("rep", "shard"), None, None),
    )
    return jax.shard_map(
        shards,
        mesh=mesh,
        in_specs=placed,
        out_specs=(
            P(("rep", "shard"), None, None),
            P(("rep", "shard"), None, None),
            P("shard"),
            P("shard", None),
            P("shard", None),
            P("shard", None),
            P("shard"),
            P("shard", None),
            P("shard"),
            P("shard", None),
            P("shard", None),
            P("shard", None),
        ),
        check_vma=False,
    )
```

profile of v0, /device:TPU:0, one launch (start us, length us, event | category | flops | bytes accessed | tf_op | source)
XLA Modules:
  0.0 2012.6 jit_solution(17651145178794768228)
XLA Ops:
  12.0 23.2 %all-gather = bf16[16,1,128]{2,1,0:T(2,128)(2,1)S(1)} all-gather(bf16[1,1,128]{2,1,0:T(2,128)(2,1)S(1)} %bitcast.75), channel_id=1, replica_groups=mesh['rep'=2,'shard'=16] {'shard'}, dimensions={0}, use_global_device_ids=true | all-gather | bytes 4352 | tf_op jit(solution)/shard_map/all_gather | solution.py:116
  35.2 17.5 all-gather.1
  52.7 18.9 all-gather.2
  72.6 15.3 all-gather.11.cloned.1.call-done
  87.9 6.4 fusion.57
  94.3 69.0 %all-gather.13.cloned.1.call-done = bf16[2048,2048]{1,0:T(8,128)(2,1)} async-done(((bf16[128,2048]{1,0:T(8,128)(2,1)}), bf16[2048,2048]{1,0:T(8,128)(2,1)}) %all-gather.13.cloned.1.call-update) | async-done | bytes 8388624 | tf_op jit(solution)/shard_map/all_gather | solution.py:114
  163.3 7.8 broadcast_multiply_fusion
  171.4 2.2 slice.394
  173.6 2.2 slice.393
  177.4 4.4 slice.444
  181.9 2.1 slice.396
  184.0 2.1 slice.395
  186.2 1.6 fusion.62
  196.7 2.4 pad.101
  200.5 38.1 %all-gather.15.cloned.1.call-done = bf16[2048,2048]{1,0:T(8,128)(2,1)} async-done(((bf16[128,2048]{1,0:T(8,128)(2,1)}), bf16[2048,2048]{1,0:T(8,128)(2,1)}) %all-gather.15.cloned.1.call-update) | async-done | bytes 8388624 | tf_op jit(solution)/shard_map/all_gather | solution.py:115
  238.6 7.6 multiply_multiply_fusion.1
  246.2 67.6 %all-gather.17.cloned.1.call-done = bf16[2048,2048]{1,0:T(8,128)(2,1)} async-done(((bf16[128,2048]{1,0:T(8,128)(2,1)}), bf16[2048,2048]{1,0:T(8,128)(2,1)}) %all-gather.17.cloned.1.call-update) | async-done | bytes 8388624 | tf_op jit(solution)/shard_map/all_gather | solution.py:132
  313.8 5.9 multiply_reduce_fusion.4
  322.0 110.3 %all-gather.21.cloned.1.call-done = bf16[2048,5632]{1,0:T(8,128)(2,1)} async-done(((bf16[128,5632]{1,0:T(8,128)(2,1)}), bf16[2048,5632]{1,0:T(8,128)(2,1)}) %all-gather.21.cloned.1.call-update) | async-done | bytes 23068688 | tf_op jit(solution)/shard_map/all_gather | solution.py:143
  432.3 14.5 fusion.74
  446.8 105.7 %all-gather.19.cloned.1.call-done = bf16[2048,5632]{1,0:T(8,128)(2,1)} async-done(((bf16[128,5632]{1,0:T(8,128)(2,1)}), bf16[2048,5632]{1,0:T(8,128)(2,1)}) %all-gather.19.cloned.1.call-update) | async-done | bytes 23068688 | tf_op jit(solution)/shard_map/all_gather | solution.py:142
  552.4 14.7 fusion.73
  567.1 105.7 %all-gather.23.cloned.1.call-done = bf16[5632,2048]{1,0:T(8,128)(2,1)} async-done(((bf16[352,2048]{1,0:T(8,128)(2,1)}), bf16[5632,2048]{1,0:T(8,128)(2,1)}) %all-gather.23.cloned.1.call-update) | async-done | bytes 23068688 | tf_op jit(solution)/shard_map/all_gather | solution.py:152
  672.8 16.0 multiply_convert_fusion
  690.1 10.9 convolution_convert_fusion.1
  703.9 4.4 slice.456
  708.3 4.5 slice.449
  712.8 4.5 slice.447
  717.3 8.6 slice.457
  725.9 8.7 slice.448
  734.6 8.6 slice.450
  745.4 12.1 fusion.75
  757.6 14.4 multiply_reduce_fusion
  772.0 2.2 multiply_add_fusion
  775.2 8.6 multiply_reduce_fusion.1
  785.0 2.1 slice.503
  787.1 2.1 slice.453
  789.3 2.1 slice.451
  791.4 8.6 slice.452
  800.1 5.1 slice.454
  805.1 2.1 fusion.61
  821.1 1.8 broadcast_in_dim.19
  822.9 1.8 broadcast_in_dim.20
  824.8 5.5 slice.504
  836.3 2.3 pad.114
  838.6 5.2 pad.115
  843.8 2.8 add.313
  846.6 16.0 rev.6
  862.6 4.1 multiply_convert_fusion.4
  866.8 6.8 fusion.76
  873.7 2.9 convolution_add_fusion.1
  876.7 4.3 fusion.24
  882.1 5.8 convolution_convert_fusion.3
  887.9 12.3 copy.30
  900.2 13.6 convolution_convert_fusion.2
  913.7 20.9 %convolution_convert_fusion = bf16[2048,11264]{1,0:T(8,128)(2,1)} fusion(bf16[192,2048]{1,0:T(8,128)(2,1)} %multiply_convert_fusion.6, bf16[192,5632]{1,0:T(8,128)(2,1)} %get-tuple-element.29, bf16[192,5632]{1,0:T(8,128)(2,1)} %get-tuple-element.30), kind=kOutput, calls=%fused_computation | convolution fusion | flops 8890089472 | bytes 51249152 | tf_op jit(solution)/shard_map/dot_general | solution.py:75
  934.6 158.1 %concatenate.84 = bf16[2048,19459]{1,0:T(8,128)(2,1)} concatenate(bf16[2048,6144]{1,0:T(8,128)(2,1)} %convolution_convert_fusion.2, bf16[2048,2048]{1,0:T(8,128)(2,1)} %copy.30, bf16[2048,11264]{1,0:T(8,128)(2,1)} %convolution_convert_fusion, bf16[2048,1]{1,0:T(8,128)(2,1)} %broadcast_in_dim.18, bf16[2048,1]{1,0:T(8,128)(2,1)S(1)} %copy-done.24, bf16[2048,1]{1,0:T(8,128)(2,1)S(1)} %copy-done.25), dimensions={1} | concatenate | bytes 159408128 | tf_op jit(solution)/shard_map/concatenate | solution.py:83
  1092.8 743.0 %reduce-scatter.3.cloned.1.call-done = bf16[128,19459]{1,0:T(8,128)(2,1)} async-done(((bf16[2048,19459]{1,0:T(8,128)(2,1)}), bf16[128,19459]{1,0:T(8,128)(2,1)}) %reduce-scatter.3.cloned.1.call-update) | async-done | bytes 4981520 | tf_op jit(solution)/shard_map/reduce_scatter | solution.py:202
  1835.9 2.9 fusion.28
  1838.7 12.3 fusion.8
  1851.0 143.4 %all-reduce.33.cloned.1.call-done = (bf16[128,19459]{1,0:T(8,128)(2,1)}, bf16[352,2048]{1,0:T(8,128)(2,1)}) async-done(((bf16[128,19459]{1,0:T(8,128)(2,1)}, bf16[352,2048]{1,0:T(8,128)(2,1)}), (bf16[128,19459]{1,0:T(8,128)(2,1)}, bf16[352,2048]{1,0:T(8,128)(2,1)})) %all-reduce.33.cloned.1.call-update) | async-done | bytes 6423312 | tf_op jit(solution)/shard_map/psum | solution.py:209
  1994.4 3.8 fusion.60
  1998.3 3.2 fusion.59
  2002.9 1.9 convert_element_type.95
  (294 shorter events, 51.2 us)
Async XLA Ops:
  7.2 80.7 %all-gather.11.cloned.1.call-start = ((), (), s32[]{:S(2)}) async-start(), calls=%async_computation.2 | async-start | bytes 8912896 | tf_op jit(solution)/shard_map/all_gather | solution.py:113
  7.9 155.3 %all-gather.13.cloned.1.call-start = ((), (), s32[]{:S(2)}) async-start(), calls=%async_computation.3 | async-start | bytes 8912896 | tf_op jit(solution)/shard_map/all_gather | solution.py:114
  8.7 229.9 %all-gather.15.cloned.1.call-start = ((), (), s32[]{:S(2)}) async-start(), calls=%async_computation.4 | async-start | bytes 8912896 | tf_op jit(solution)/shard_map/all_gather | solution.py:115
  9.4 304.4 %all-gather.17.cloned.1.call-start = ((), (), s32[]{:S(2)}) async-start(), calls=%async_computation.5 | async-start | bytes 8912896 | tf_op jit(solution)/shard_map/all_gather | solution.py:132
  10.0 422.3 %all-gather.21.cloned.1.call-start = ((), (), s32[]{:S(2)}) async-start(), calls=%async_computation.7 | async-start | bytes 24510464 | tf_op jit(solution)/shard_map/all_gather | solution.py:143
  10.6 1.4 copy-start.45
  10.6 24.7 %copy-start.46 = (bf16[128]{0:T(256)(128)(2,1)S(1)}, bf16[128]{0:T(256)(128)(2,1)}, u32[]{:S(2)}) copy-start(bf16[128]{0:T(256)(128)(2,1)} %param.19) | copy-start | bytes 772
  10.6 42.1 %copy-start.47 = (bf16[128]{0:T(256)(128)(2,1)S(1)}, bf16[128]{0:T(256)(128)(2,1)}, u32[]{:S(2)}) copy-start(bf16[128]{0:T(256)(128)(2,1)} %param.21) | copy-start | bytes 772
  10.6 61.6 %copy-start.44 = (s32[1,192]{1,0:T(1,128)S(1)}, s32[1,192]{1,0:T(1,128)}, u32[]{:S(2)}) copy-start(s32[1,192]{1,0:T(1,128)} %param.14) | copy-start | bytes 2308
  10.6 61.8 %copy-start.1 = (bf16[1,192,2048]{2,1,0:T(8,128)(2,1)S(1)}, bf16[1,192,2048]{2,1,0:T(8,128)(2,1)}, u32[]{:S(2)}) copy-start(bf16[1,192,2048]{2,1,0:T(8,128)(2,1)} %param.13) | copy-start | bytes 2359300
  10.6 541.8 %all-gather.19.cloned.1.call-start = ((), (), s32[]{:S(2)}) async-start(), calls=%async_computation.6 | async-start | bytes 24510464 | tf_op jit(solution)/shard_map/all_gather | solution.py:142
  11.2 661.6 %all-gather.23.cloned.1.call-start = ((), (), s32[]{:S(2)}) async-start(), calls=%async_computation.8 | async-start | bytes 24510464 | tf_op jit(solution)/shard_map/all_gather | solution.py:152
  11.9 1080.8 %reduce-scatter.5.cloned.1.call-start = ((), (), s32[]{:S(2)}) async-start(), calls=%async_computation.10 | async-start | bytes 24510464 | tf_op jit(solution)/shard_map/reduce_scatter | solution.py:205
  72.4 90.9 %copy-start.42 = (f32[192]{0:T(256)}, f32[192]{0:T(256)S(1)}, u32[]{:S(2)}) copy-start(f32[192]{0:T(256)S(1)} %add_convert_fusion) | copy-start | bytes 2308
  72.6 90.6 %copy-start.32 = (f32[192]{0:T(256)}, f32[192]{0:T(256)S(1)}, u32[]{:S(2)}) copy-start(f32[192]{0:T(256)S(1)} %add_rsqrt_fusion.2) | copy-start | bytes 2308
  171.0 2.6 copy-start.3
  175.9 6.0 copy-start.10
  181.9 4.3 copy-start.13
  193.2 0.7 copy-start.38
  194.1 1.1 copy-start.17
  194.1 1.6 copy-start.18
  195.7 0.7 copy-start.36
  199.1 39.5 %copy-start.33 = (f32[192]{0:T(256)S(1)}, f32[192]{0:T(256)}, u32[]{:S(2)}) copy-start(f32[192]{0:T(256)} %copy-done.32) | copy-start | bytes 2308
  313.8 7.1 copy-start.31
  319.7 1.2 copy-start.5
  672.8 17.3 copy-start.20
  688.8 1.3 copy-start.8
  701.1 1134.7 %reduce-scatter.3.cloned.1.call-start = ((), (), s32[]{:S(2)}) async-start(), calls=%async_computation.9 | async-start | bytes 85229568 | tf_op jit(solution)/shard_map/reduce_scatter | solution.py:202
  743.2 2.2 copy-start.23
  745.4 12.2 copy-start.6
  772.0 2.2 copy-start.4
  772.0 2.7 copy-start.21
  772.0 3.2 copy-start.27
  791.4 8.7 copy-start.15
  810.3 3.6 copy-start.26
  819.0 5.8 copy-start.14
  822.9 7.7 copy-start.41
  830.3 0.7 copy-start.40
  830.8 0.7 copy-start.39
  831.5 1.0 copy-start.28
  831.5 1.1 copy-start.29
  831.6 1.0 copy-start.37
  832.9 1.4 copy-start.16
  832.9 1.7 copy-start.19
  834.6 0.7 copy-start.35
  846.6 16.0 copy-start.43
  862.6 11.0 slice-start
  866.8 6.9 copy-start.12
  866.8 6.9 slice-start.1
  866.8 9.8 slice-start.2
  873.7 2.9 copy-start.2
  873.7 2.9 slice-start.3
  873.7 2.9 copy-start.11
  873.7 2.9 copy-start.34
  876.6 5.4 copy-start.22
  913.7 20.9 %copy-start.24 = (bf16[2048,1]{1,0:T(8,128)(2,1)S(1)}, bf16[2048,1]{1,0:T(8,128)(2,1)}, u32[]{:S(2)}) copy-start(bf16[2048,1]{1,0:T(8,128)(2,1)} %broadcast_in_dim.19) | copy-start | bytes 12292
  913.7 20.9 %copy-start.25 = (bf16[2048,1]{1,0:T(8,128)(2,1)S(1)}, bf16[2048,1]{1,0:T(8,128)(2,1)}, u32[]{:S(2)}) copy-start(bf16[2048,1]{1,0:T(8,128)(2,1)} %broadcast_in_dim.20) | copy-start | bytes 12292
  1092.7 901.7 %all-reduce.33.cloned.1.call-start = ((), (), s32[]{:S(2)}) async-start(), calls=%async_computation.11 | async-start | bytes 12910592 | tf_op jit(solution)/shard_map/psum | solution.py:209
  1835.8 2.9 copy-start.7
  1835.9 2.9 copy-start.9
  1994.4 3.9 copy-start
  2001.5 1.4 copy-start.30
Sparse Core Ops, SparseCore 0:
  10.2 77.6 all-gather.10
  90.1 73.1 all-gather.12
  165.4 73.1 all-gather.14
  240.6 73.1 all-gather.16
  315.3 116.9 all-gather.20
  433.7 118.6 all-gather.18
  554.0 118.6 all-gather.22
  701.2 226.8 reduce-scatter.4
  1092.8 742.9 reduce-scatter.2
  1838.2 156.2 all-reduce.32
where the time goes:
time: 2030 us; the launch traced here: 2010 us
  waiting for transfers between devices  1400 us (69%)
  local copies, waits for them, and re-layouts  319 us (16%)
  matrix products  185 us (9%)
  blocking collectives  59.6 us (3%)
  other arithmetic  30.4 us (1%)
    reduce_scatter x1, waiting for transfers between devices, shards(): lax.psum_scatter(row_block(pairs, gains).astype(jnp.bfloat16), 'shard', s...  743 us
    concatenate x1, local copies, waits for them, and re-layouts, row_block(): return jnp.concatenate(pieces, axis=1)  158 us
    psum x1, waiting for transfers between devices, shards(): lax.psum(rows_term, 'rep').astype(jnp.float32)  143 us
    all_gather x1, waiting for transfers between devices, shards(): lax.all_gather(ffn_up_weight, 'shard', axis=0, tiled=True)  110 us
    all_gather x1, waiting for transfers between devices, shards(): lax.all_gather(ffn_gate_weight, 'shard', axis=0, tiled=True)  106 us
    all_gather x1, waiting for transfers between devices, shards(): lax.all_gather(ffn_down_weight, 'shard', axis=0, tiled=True)  106 us
    slice x90, local copies, waits for them, and re-layouts, linear_scan(): return lax.associative_scan(combine_steps, (decay, update), axis=0)[1]  96.4 us
    all_gather x1, waiting for transfers between devices, shards(): lax.all_gather(forget_weight, 'shard', axis=0, tiled=True)  69 us
  transfers between devices with their start and end apart: 10, of which 9 were waited for; matrix products, arithmetic and copies ran while one was open for 24% of the time, Pallas kernels for 0%

commit v1 on v0

v1 whole, which is shorter than its diff:
```python
import functools

import jax
import jax.numpy as jnp
from jax import lax
from jax.experimental import pallas as pl
from jax.experimental.pallas import tpu as pltpu
from jax.sharding import PartitionSpec as P

EPSILON = 1e-06
AXES = ("rep", "shard")
CORES = 2
F32 = jnp.float32
BF16 = jnp.bfloat16


def normalize(values):
    scale = lax.rsqrt(jnp.mean(values * values, axis=-1, keepdims=True) + EPSILON)
    return (values * scale, scale)


def norm_back(grad_scaled, scaled, scale):
    inner = jnp.mean(grad_scaled * scaled, axis=-1, keepdims=True)
    return scale * (grad_scaled - scaled * inner)


def swish_pair(values):
    sigma = jax.nn.sigmoid(values)
    return (values * sigma, sigma * (1.0 + values * (1.0 - sigma)))


def matmul(left, right, dims, out=F32):
    return lax.dot_general(left, right, ((dims[:1], dims[1:]), ((), ())), preferred_element_type=F32).astype(out)


TILE = 8


def scan_tile(decay, update, reverse):
    row = lax.broadcasted_iota(jnp.int32, decay.shape, 0)
    for step in (1, 2, 4):
        shift = TILE - step if reverse else step
        inside = row < TILE - step if reverse else row >= step
        earlier = jnp.where(inside, pltpu.roll(update, shift, 0), 0.0)
        product = jnp.where(inside, pltpu.roll(decay, shift, 0), 1.0)
        update = update + decay * earlier
        decay = decay * product
    return (decay, update)


def scan_forward_kernel(count, length, decay, update, state):
    def block(step, carries):
        out = []
        for n in range(count):
            rows = pl.ds(pl.multiple_of(n * length + step * TILE, TILE), TILE)
            product, local = scan_tile(decay[rows, :], update[rows, :], False)
            local = local + product * carries[n]
            state[rows, :] = local
            out.append(local[TILE - 1 :, :])
        return tuple(out)

    lax.fori_loop(0, length // TILE, block, (jnp.zeros((1, state.shape[1]), F32),) * count)


def scan_backward_kernel(count, length, decay, grad, carried):
    steps = length // TILE

    def block(step, pairs):
        out = []
        for n in range(count):
            carry, later = pairs[n]
            rows = pl.ds(pl.multiple_of(n * length + (steps - 1 - step) * TILE, TILE), TILE)
            own = decay[rows, :]
            row = lax.broadcasted_iota(jnp.int32, own.shape, 0)
            following = jnp.where(row < TILE - 1, pltpu.roll(own, TILE - 1, 0), later)
            product, local = scan_tile(following, grad[rows, :], True)
            local = local + product * carry
            carried[rows, :] = local
            out.append((local[:1, :], own[:1, :]))
        return tuple(out)

    zero = jnp.zeros((1, carried.shape[1]), F32)
    lax.fori_loop(0, steps, block, ((zero, zero),) * count)


def run_scan(kernel, name, count, length, left, right):
    size = left.size
    return pl.pallas_call(
        functools.partial(kernel, count, length),
        out_shape=jax.ShapeDtypeStruct(left.shape, F32),
        in_specs=[pl.BlockSpec(memory_space=pltpu.VMEM)] * 2,
        out_specs=pl.BlockSpec(memory_space=pltpu.VMEM),
        compiler_params=pltpu.CompilerParams(vmem_limit_bytes=32 * 2**20),
        cost_estimate=pl.CostEstimate(flops=2 * size, bytes_accessed=12 * size, transcendentals=0),
        name=name,
    )(left, right)


class Layout:
    def __init__(self, reps, shards):
        self.reps, self.shards = reps, shards
        self.chips = shards // CORES
        self.outer = 4 if self.chips % 4 == 0 else 1
        self.inner = self.chips // self.outer
        self.r = lax.axis_index("rep")
        place = lax.axis_index("shard")
        self.c = place % CORES
        self.i = (place // CORES) % self.inner
        self.o = place // (CORES * self.inner)
        self.members = reps * CORES

    def send(self, value, dr=0, do=0, di=0, dc=0):
        pairs = []
        for r in range(self.reps):
            for o in range(self.outer):
                for i in range(self.inner):
                    for c in range(CORES):
                        far = ((r + dr) % self.reps, (o + do) % self.outer, (i + di) % self.inner, (c + dc) % CORES)
                        pairs.append((self.number(r, o, i, c), self.number(*far)))
        return lax.ppermute(value, AXES, pairs)

    def number(self, r, o, i, c):
        return ((r * self.outer + o) * self.inner + i) * CORES + c

    def gather_members(self, value):
        both = [value] + [self.send(value, dr=k) for k in range(1, self.reps)]
        rows = jnp.concatenate(both, axis=0)
        return jnp.concatenate([rows, self.send(rows, dc=1)], axis=0)

    def sum_members(self, partial):
        half = partial.shape[0] // CORES
        rows = partial.shape[0] // self.members
        wire = partial.dtype
        total = partial[:half].astype(F32) + self.send(partial[half:], dc=1).astype(F32)
        own = total[:rows]
        for k in range(1, self.reps):
            block = total[k * rows : (k + 1) * rows].astype(wire)
            own = own + self.send(block, dr=-k).astype(F32)
        return own

    def scatter_plane(self, grad):
        rows = grad.shape[0] // self.chips
        grid = grad.reshape(self.outer, self.inner, rows, grad.shape[1])
        pick = lambda k: lax.dynamic_index_in_dim(grid, (self.i + k) % self.inner, 1, keepdims=False)
        total = pick(0).astype(F32)
        for k in range(1, self.inner):
            total = total + self.send(pick(k), di=k).astype(F32)
        line = total.astype(BF16)
        take = lambda k: lax.dynamic_index_in_dim(line, (self.o + k) % self.outer, 0, keepdims=False)
        own = take(0).astype(F32)
        for k in range(1, self.outer):
            own = own + self.send(take(k), do=k).astype(F32)
        return own

    def split_columns(self, weight):
        rows, columns = weight.shape
        small = columns // (self.chips * CORES * self.reps)
        grid = weight.reshape(rows, self.chips, CORES, self.reps, small)
        mine = lax.dynamic_index_in_dim(grid, self.r, 3, keepdims=False)
        return mine.transpose(0, 2, 1, 3).reshape(rows, CORES, self.chips * small)

    def own_columns(self, vector):
        columns = vector.shape[0]
        small = columns // (self.chips * CORES * self.reps)
        grid = vector.reshape(self.chips, CORES, self.reps, small)
        mine = lax.dynamic_index_in_dim(grid, self.c, 1, keepdims=False)
        return lax.dynamic_index_in_dim(mine, self.r, 1, keepdims=False).reshape(-1)

    def join_columns(self, own):
        rows, columns = own.shape[0] // CORES, own.shape[1]
        pair = own.reshape(CORES, rows, columns).astype(BF16)
        mine = lax.dynamic_index_in_dim(pair, self.c, 0, keepdims=False)
        other = self.send(lax.dynamic_index_in_dim(pair, 1 - self.c, 0, keepdims=False), dc=1)
        first = self.c == 0
        cores = jnp.stack([jnp.where(first, mine, other), jnp.where(first, other, mine)])
        return self.join_reps(cores)

    def join_reps(self, value):
        parts = [value] + [self.send(value, dr=k) for k in range(1, self.reps)]
        if self.reps == 2:
            first = self.r == 0
            return jnp.stack([jnp.where(first, parts[0], parts[1]), jnp.where(first, parts[1], parts[0])])
        stacked = jnp.stack(parts[::-1] + parts[::-1])
        return lax.dynamic_slice_in_dim(stacked, self.reps - 1 - self.r, self.reps, 0)

    def natural(self, joined):
        reps, cores, rows, columns = joined.shape
        small = columns // self.chips
        grid = joined.reshape(reps, cores, rows, self.chips, small).transpose(2, 3, 1, 0, 4)
        return grid.reshape(rows, self.chips * cores * reps * small).astype(F32)


def shards(
    reps,
    places,
    tokens,
    segment_ids,
    norm_gain,
    input_weight,
    forget_weight,
    gate_weight,
    mixer_gain,
    out_weight,
    ffn_gain,
    ffn_gate_weight,
    ffn_up_weight,
    ffn_down_weight,
    cotangent,
):
    at = Layout(reps, places)
    inputs = tokens[0].astype(F32)
    length, width = inputs.shape
    units = ffn_up_weight.shape[1]
    channels = width // at.members
    part = units // at.members
    count = at.members

    mix_local = jnp.stack([at.split_columns(w) for w in (input_weight, forget_weight, gate_weight)], axis=2)
    mix_local = mix_local.reshape(mix_local.shape[0], -1)
    pair_local = jnp.stack([at.split_columns(w) for w in (ffn_gate_weight, ffn_up_weight)], axis=2)
    pair_local = pair_local.reshape(pair_local.shape[0], -1)
    rep_rows = lambda w: lax.dynamic_index_in_dim(w.reshape(reps, w.shape[0] // reps, w.shape[1]), at.r, 0, keepdims=False)
    gather = lambda w: lax.all_gather(w, "shard", axis=0, tiled=True)
    core_columns = lambda w: lax.dynamic_index_in_dim(w.reshape(w.shape[0], CORES, -1), at.c, 1, keepdims=False)
    core_rows = lambda w, n: lax.dynamic_index_in_dim(w.reshape(at.chips, CORES, n, w.shape[1]), at.c, 1, keepdims=False).reshape(-1, w.shape[1])
    gains = lax.all_gather(jnp.stack([norm_gain, mixer_gain, ffn_gain]), "shard", axis=1, tiled=True).astype(F32)
    gain_one, gain_two, gain_three = gains[0], gains[1], gains[2]
    mix_weight = core_columns(gather(mix_local))
    out_rows = core_rows(gather(rep_rows(out_weight)), out_weight.shape[0] // reps)
    pair_weight = core_columns(gather(pair_local))
    down_rows = core_rows(gather(rep_rows(ffn_down_weight)), ffn_down_weight.shape[0] // reps)

    grad_out = cotangent[0]
    all_grad_out = at.gather_members(grad_out)
    segments = at.gather_members(segment_ids)
    starts = jnp.zeros((count, 1), F32)
    same = jnp.concatenate([starts, (segments[:, 1:] == segments[:, :-1]).astype(F32)], axis=1)
    same = same.reshape(count * length, 1)
    scaled_in, scale_in = normalize(inputs)
    normed = at.gather_members((scaled_in * gain_one).astype(BF16))
    pre = matmul(normed, mix_weight, (1, 0))
    input_pre, forget_pre, gate_pre = (pre[:, k * channels : (k + 1) * channels] for k in range(3))
    forget = jax.nn.sigmoid(forget_pre)
    input_act, input_slope = swish_pair(input_pre)
    decay = forget * same
    state = run_scan(scan_forward_kernel, "scan_forward", count, length, decay, input_act * (1.0 - forget))
    gate_act, gate_slope = swish_pair(gate_pre)
    gain_mix = at.own_columns(gain_two)
    mixed_raw = (state * gain_mix * gate_act).astype(BF16)
    squares = jnp.sum(state * state, axis=1).reshape(count, length)
    square_sum = at.sum_members(squares)
    branch_sum = at.sum_members(matmul(mixed_raw, out_rows, (1, 0), BF16))
    state_scale = lax.rsqrt(square_sum / width + EPSILON)
    branch = branch_sum * state_scale.reshape(length, 1)
    resid = inputs + branch

    scaled_mid, scale_mid = normalize(resid)
    ffn_in = at.gather_members((scaled_mid * gain_three).astype(BF16))
    pair = matmul(ffn_in, pair_weight, (1, 0))
    ffn_gate, ffn_up = pair[:, :part], pair[:, part:]
    ffn_act, ffn_slope = swish_pair(ffn_gate)
    hidden = (ffn_act * ffn_up).astype(BF16)
    down_grad = at.scatter_plane(matmul(hidden, all_grad_out, (0, 0), BF16))
    ffn_out = at.sum_members(matmul(hidden, down_rows, (1, 0), BF16))
    block_output = (resid + ffn_out).astype(BF16)
    grad_hidden = matmul(all_grad_out, down_rows, (1, 1))
    grad_fgate = (grad_hidden * ffn_up * ffn_slope).astype(BF16)
    grad_fup = (grad_hidden * ffn_act).astype(BF16)
    grad_pair = jnp.concatenate([grad_fgate, grad_fup], axis=1)
    grad_ffn_in = at.sum_members(matmul(grad_pair, pair_weight, (1, 1), BF16))
    gate_grad = at.scatter_plane(matmul(ffn_in, grad_fgate, (0, 0), BF16))
    up_grad = at.scatter_plane(matmul(ffn_in, grad_fup, (0, 0), BF16))
    grad_resid = grad_out.astype(F32) + norm_back(grad_ffn_in * gain_three, scaled_mid, scale_mid)
    grad_branch_own = grad_resid.astype(BF16)

    grad_branch = at.gather_members(grad_branch_own)
    inner_own = jnp.mean(grad_branch_own.astype(F32) * branch, axis=1)
    row_facts = at.gather_members(jnp.stack([state_scale.reshape(length), inner_own])[None])
    all_scale = row_facts[:, 0].reshape(count * length, 1)
    all_inner = row_facts[:, 1].reshape(count * length, 1)
    state_scaled = state * all_scale
    mixed = (state_scaled * gain_mix * gate_act).astype(BF16)
    weighted = matmul(grad_branch, out_rows, (1, 1)) * gain_mix
    out_grad = at.scatter_plane(matmul(mixed, grad_branch, (0, 0), BF16))
    grad_gate_pre = (weighted * state_scaled * gate_slope).astype(BF16)
    grad_state = all_scale * (weighted * gate_act - state_scaled * all_inner)
    carried = run_scan(scan_backward_kernel, "scan_backward", count, length, decay, grad_state)
    line = state.reshape(count, length, channels)
    previous = jnp.concatenate([jnp.zeros((count, 1, channels), F32), line[:, :-1]], axis=1).reshape(state.shape)
    grad_forget = carried * previous * same - carried * input_act
    grad_input_pre = (carried * (1.0 - forget) * input_slope).astype(BF16)
    grad_forget_pre = (grad_forget * forget * (1.0 - forget)).astype(BF16)
    triple = jnp.concatenate([grad_input_pre, grad_forget_pre, grad_gate_pre], axis=1)
    grad_normed = at.sum_members(matmul(triple, mix_weight, (1, 1), BF16))
    mix_grads = [at.scatter_plane(matmul(normed, g, (0, 0), BF16)) for g in (grad_input_pre, grad_forget_pre, grad_gate_pre)]
    input_grad = (grad_resid + norm_back(grad_normed * gain_one, scaled_in, scale_in)).astype(BF16)

    whole = lambda own: at.natural(at.join_columns(own))
    stacked = lambda own: at.join_reps(own.astype(BF16)).reshape(-1, own.shape[1]).astype(F32)
    down_total = stacked(down_grad)
    gate_total, up_total = whole(gate_grad), whole(up_grad)
    out_total = stacked(out_grad)
    mix_totals = [whole(g) for g in mix_grads]
    dotted = lambda w, g: jnp.sum(w.astype(F32) * g, axis=1)
    norm_gain_grad = sum(dotted(w, g) for w, g in zip((input_weight, forget_weight, gate_weight), mix_totals)) / norm_gain.astype(F32)
    mixer_gain_grad = dotted(out_weight, out_total) / mixer_gain.astype(F32)
    ffn_gain_grad = (dotted(ffn_gate_weight, gate_total) + dotted(ffn_up_weight, up_total)) / ffn_gain.astype(F32)
    return (
        block_output[None],
        input_grad[None],
        norm_gain_grad,
        *mix_totals,
        mixer_gain_grad,
        out_total,
        ffn_gain_grad,
        gate_total,
        up_total,
        down_total,
    )


def solution(mesh):
    tokens, vector, matrix = P(AXES, None, None), P("shard"), P("shard", None)
    placed = (tokens, P(AXES, None), vector, matrix, matrix, matrix, vector, matrix, vector, matrix, matrix, matrix, tokens)
    return jax.shard_map(
        functools.partial(shards, mesh.shape["rep"], mesh.shape["shard"]),
        mesh=mesh,
        in_specs=placed,
        out_specs=(tokens, tokens, vector, matrix, matrix, matrix, vector, matrix, vector, matrix, matrix, matrix),
        check_vma=False,
    )
```

time: 2030 us -> 1060 us (0.52)
  waiting for transfers between devices: 1400 us -> 657 us
  local copies, waits for them, and re-layouts: 319 us -> 76.3 us
  starting transfers between devices: 0.39 us -> 107 us
  matrix products: 185 us -> 105 us
  blocking collectives: 59.6 us -> 23.1 us
  other arithmetic: 30.4 us -> 62.7 us
    reduce_scatter x2 -> x0, waiting for transfers between devices: 743 us -> none  [the longest x1 743 us: shards(): lax.psum_scatter(row_block(pairs, gains).astype(jnp.bfloat16), 'shard', s...]
    ppermute x0 -> x62, waiting for transfers between devices: none -> 429 us  [send(): return lax.ppermute(value, AXES, pairs)]
    all_gather x7 -> x4, waiting for transfers between devices: 512 us -> 228 us  [shards(): gather = lambda w: lax.all_gather(w, 'shard', axis=0, tiled=True)]
    concatenate x2 -> x1, local copies, waits for them, and re-layouts: 159 us -> 1.37 us  [shards(): jnp.concatenate([jnp.zeros((count, 1, channels), F32), line[:, :-1]], axi...]
    psum x1 -> x0, waiting for transfers between devices: 143 us -> none  [shards(): lax.psum(rows_term, 'rep').astype(jnp.float32)]
    ppermute x0 -> x62, starting transfers between devices: none -> 107 us  [send(): return lax.ppermute(value, AXES, pairs)]
    slice x94 -> x15, local copies, waits for them, and re-layouts: 106 us -> 3.29 us  [the longest x6 1.82 us: sum_members(): partial[half:]]
    dot_general x18 -> x15, matrix products: 185 us -> 105 us  [matmul(): lax.dot_general(left, right, ((dims[:1], dims[1:]), ((), ())), preferred_...]
  transfers between devices with their start and end apart: 10 -> 66, of which waited for: 9 -> 32; matrix products, arithmetic and copies ran while one was open for 24% -> 18% of each run, Pallas kernels for 0% -> 0%
where the time goes in v1:
time: 1060 us; the launch traced here: 1050 us
  waiting for transfers between devices  657 us (62%)
  starting transfers between devices  107 us (10%)
  matrix products  105 us (10%)
  local copies, waits for them, and re-layouts  76.3 us (7%)
  other arithmetic  62.7 us (6%)
  blocking collectives  23.1 us (2%)
  between operations  15.9 us (2%)
    ppermute x62, waiting for transfers between devices, send(): return lax.ppermute(value, AXES, pairs)  429 us
    all_gather x4, waiting for transfers between devices, shards(): gather = lambda w: lax.all_gather(w, 'shard', axis=0, tiled=True)  228 us
    ppermute x62, starting transfers between devices, send(): return lax.ppermute(value, AXES, pairs)  107 us
    dot_general x15, matrix products, matmul(): lax.dot_general(left, right, ((dims[:1], dims[1:]), ((), ())), preferred_...  105 us
    unnamed x166, local copies, waits for them, and re-layouts  37.6 us
    all_gather x1, blocking collectives, shards(): lax.all_gather(jnp.stack([norm_gain, mixer_gain, ffn_gain]), 'shard', axi...  23.1 us
  transfers between devices with their start and end apart: 66, of which 32 were waited for; matrix products, arithmetic and copies ran while one was open for 18% of the time, Pallas kernels for 0%

profile of v1, /device:TPU:0, one launch (start us, length us, event | category | flops | bytes accessed | tf_op | source)
XLA Modules:
  0.0 1050.4 jit_solution(3468860039461205865)
XLA Ops:
  21.4 23.1 %all_gather.15 = bf16[3,2048]{1,0:T(4,128)(2,1)S(1)} all-gather(bf16[3,128]{1,0:T(4,128)(2,1)S(1)} %pad_maximum_fusion.23), channel_id=1, replica_groups=mesh['rep'=2,'shard'=16] {'shard'}, dimensions={1}, use_global_device_ids=true | all-gather | bytes 13056 | tf_op jit(solution)/shard_map/all_gather | solution.py:226
  46.7 18.3 %collective-permute-done = bf16[192,2048]{1,0:T(8,128)(2,1)S(1)} collective-permute-done((bf16[192,2048]{1,0:T(8,128)(2,1)S(1)}, bf16[192,2048]{1,0:T(8,128)(2,1)S(1)}, u32[]{:S(2)}, u32[]{:S(2)}) %collective-permute-start) | collective-permute-done | bytes 786464 | tf_op jit(solution)/shard_map/ppermute | solution.py:120
  70.3 3.2 constant_dynamic-slice_fusion.12
  73.5 97.9 %all-gather.7.cloned.1.call-done = bf16[2048,3072]{0,1:T(8,128)(2,1)} async-done(((bf16[128,3072]{0,1:T(8,128)(2,1)}), bf16[2048,3072]{0,1:T(8,128)(2,1)}) %all-gather.7.cloned.1.call-update) | async-done | bytes 12582928 | tf_op jit(solution)/shard_map/all_gather | solution.py:223
  171.4 7.9 fusion.8
  185.7 3.2 collective-permute-done.4
  194.7 16.3 %collective-permute-done.7 = f32[1,192]{1,0:T(1,128)S(1)} collective-permute-done((f32[1,192]{1,0:T(1,128)S(1)}, f32[1,192]{1,0:T(1,128)S(1)}, u32[]{:S(2)}, u32[]{:S(2)}) %collective-permute-start.7) | collective-permute-done | bytes 800 | tf_op jit(solution)/shard_map/ppermute | solution.py:120
  211.9 3.2 multiply_reduce_fusion.4
  216.6 16.8 %collective-permute-done.8 = bf16[192,2048]{1,0:T(8,128)(2,1)S(1)} collective-permute-done((bf16[192,2048]{1,0:T(8,128)(2,1)S(1)}, bf16[192,2048]{1,0:T(8,128)(2,1)S(1)}, u32[]{:S(2)}, u32[]{:S(2)}) %collective-permute-start.8) | collective-permute-done | bytes 786464 | tf_op jit(solution)/shard_map/ppermute | solution.py:120
  236.2 18.8 %collective-permute-done.12 = bf16[192,2048]{1,0:T(8,128)(2,1)} collective-permute-done((bf16[192,2048]{1,0:T(8,128)(2,1)}, bf16[192,2048]{1,0:T(8,128)(2,1)}, u32[]{:S(2)}, u32[]{:S(2)}) %collective-permute-start.12) | collective-permute-done | bytes 786464 | tf_op jit(solution)/shard_map/ppermute | solution.py:120
  255.0 2.7 pad_maximum_fusion.6
  257.7 9.0 all-gather.13.cloned.1.call-done
  266.8 6.1 constant_dynamic-slice_fusion.10
  272.9 120.9 %all-gather.9.cloned.1.call-done = bf16[2048,5632]{0,1:T(8,128)(2,1)} async-done(((bf16[128,5632]{0,1:T(8,128)(2,1)}), bf16[2048,5632]{0,1:T(8,128)(2,1)}) %all-gather.9.cloned.1.call-update) | async-done | bytes 23068688 | tf_op jit(solution)/shard_map/all_gather | solution.py:223
  393.8 16.1 %fusion.2 = f32[768,2816]{1,0:T(8,128)} fusion(bf16[2048,2,2816]{0,2,1:T(8,128)(2,1)} %bitcast.398, s32[]{:T(128)S(6)} %select_n.343, bf16[384,2048]{1,0:T(8,128)(2,1)} %collective-permute-done.9, bf16[192,2048]{1,0:T(8,128)(2,1)} %copy-done.43, bf16[192,2048]{1,0:T(8,128)(2,1)} %copy-done.37), kind=kOutput, calls=%fused_computation.2 | convolution fusion | flops 8867807232 | bytes 23330820 | tf_op jit(solution)/shard_map/dot_general | solution.py:33
  409.9 13.0 %multiply_convert_fusion.1 = (bf16[768,1408]{1,0:T(8,128)(2,1)}, bf16[768,1408]{1,0:T(8,128)(2,1)}, bf16[768,1408]{1,0:T(8,128)(2,1)S(1)}) fusion(f32[768,2816]{1,0:T(8,128)} %fusion.2, bf16[1408,2048]{1,0:T(8,128)(2,1)S(1)} %bitcast.343, bf16[384,2048]{1,0:T(8,128)(2,1)} %collective-permute-done.13, bf16[192,2048]{1,0:T(8,128)(2,1)} %collective-permute-done.12, ...), kind=kOutput, calls=%fused_computation.25 | convolution fusion | flops 4454842368 | bytes 24051712 | tf_op jit(solution)/shard_map/dot_general | solution.py:33
  422.9 5.2 convolution_convert_fusion.4
  428.2 13.8 %fusion.22 = bf16[768,2048]{1,0:T(8,128)(2,1)S(1)} fusion(bf16[2048,2,2816]{0,2,1:T(8,128)(2,1)} %bitcast.399, s32[]{:T(128)S(6)} %select_n.343, bf16[768,1408]{1,0:T(8,128)(2,1)S(1)} %copy-done.61, bf16[768,1408]{1,0:T(8,128)(2,1)} %get-tuple-element.45), kind=kOutput, calls=%fused_computation.31 | convolution fusion | flops 8868593664 | bytes 19005444 | tf_op jit(solution)/shard_map/dot_general | solution.py:33
  442.8 7.7 convolution_convert_fusion
  456.1 6.9 convolution_convert_fusion.2
  467.3 7.0 convolution_convert_fusion.1
  483.7 11.8 %collective-permute-done.15 = bf16[192,2048]{1,0:T(8,128)(2,1)S(1)} collective-permute-done((bf16[192,2048]{1,0:T(8,128)(2,1)S(1)}, bf16[192,2048]{1,0:T(8,128)(2,1)S(1)}, u32[]{:S(2)}, u32[]{:S(2)}) %collective-permute-start.15) | collective-permute-done | bytes 786464 | tf_op jit(solution)/shard_map/ppermute | solution.py:120
  496.0 15.4 %collective-permute-done.11 = bf16[192,2048]{1,0:T(8,128)(2,1)S(1)} collective-permute-done((bf16[192,2048]{1,0:T(8,128)(2,1)S(1)}, bf16[192,2048]{1,0:T(8,128)(2,1)S(1)}, u32[]{:S(2)}, u32[]{:S(2)}) %collective-permute-start.11) | collective-permute-done | bytes 786464 | tf_op jit(solution)/shard_map/ppermute | solution.py:120
  511.4 3.8 multiply_reduce_fusion.2
  522.1 4.0 fusion.10
  527.6 2.6 collective-permute-start.60
  530.3 51.8 %collective-permute-done.45 = bf16[4,256,1408]{2,1,0:T(8,128)(2,1)} collective-permute-done((bf16[4,256,1408]{2,1,0:T(8,128)(2,1)}, bf16[4,256,1408]{2,1,0:T(8,128)(2,1)}, u32[]{:S(2)}, u32[]{:S(2)}) %collective-permute-start.45) | collective-permute-done | bytes 2883616 | tf_op jit(solution)/shard_map/ppermute | solution.py:120
  583.2 2.5 fusion.12
  585.9 57.3 %collective-permute-done.51 = bf16[4,256,1408]{2,1,0:T(8,128)(2,1)} collective-permute-done((bf16[4,256,1408]{2,1,0:T(8,128)(2,1)}, bf16[4,256,1408]{2,1,0:T(8,128)(2,1)}, u32[]{:S(2)}, u32[]{:S(2)}) %collective-permute-start.51) | collective-permute-done | bytes 2883616 | tf_op jit(solution)/shard_map/ppermute | solution.py:120
  644.1 2.5 fusion.11
  648.9 2.9 collective-permute-start.48
  651.8 2.7 pad_maximum_fusion.7
  655.2 3.2 collective-permute-start.54
  658.9 5.3 collective-permute-done.46
  664.1 29.5 %collective-permute-start.53 = (bf16[256,1408]{1,0:T(8,128)(2,1)}, bf16[256,1408]{1,0:T(8,128)(2,1)}, u32[]{:S(2)}, u32[]{:S(2)}) collective-permute-start(bf16[256,1408]{1,0:T(8,128)(2,1)} %get-tuple-element.59), channel_id=1, source_target_pairs={{0,8},{1,9},{2,10},{3,11},{4,12},{5,13},{6,14},{7,15},{8,0},{9,1},... | collective-permute-start | bytes 2162696 | tf_op jit(solution)/shard_map/ppermute | solution.py:120
  693.7 32.3 %collective-permute-done.47 = bf16[256,1408]{1,0:T(8,128)(2,1)S(1)} collective-permute-done((bf16[256,1408]{1,0:T(8,128)(2,1)S(1)}, bf16[256,1408]{1,0:T(8,128)(2,1)S(1)}, u32[]{:S(2)}, u32[]{:S(2)}) %collective-permute-start.47) | collective-permute-done | bytes 720928 | tf_op jit(solution)/shard_map/ppermute | solution.py:120
  728.8 41.9 %collective-permute-done.53 = bf16[256,1408]{1,0:T(8,128)(2,1)} collective-permute-done((bf16[256,1408]{1,0:T(8,128)(2,1)}, bf16[256,1408]{1,0:T(8,128)(2,1)}, u32[]{:S(2)}, u32[]{:S(2)}) %collective-permute-start.53) | collective-permute-done | bytes 720928 | tf_op jit(solution)/shard_map/ppermute | solution.py:120
  784.9 12.5 %collective-permute-done.50 = bf16[2,128,1408]{1,2,0:T(8,128)(2,1)S(1)} collective-permute-done((bf16[2,128,1408]{1,2,0:T(8,128)(2,1)S(1)}, bf16[2,128,1408]{1,2,0:T(8,128)(2,1)S(1)}, u32[]{:S(2)}, u32[]{:S(2)}) %collective-permute-start.50) | collective-permute-done | bytes 720928 | tf_op jit(solution)/shard_map/ppermute | solution.py:120
  799.6 3.6 copy.102
  803.2 9.4 collective-permute-done.56
  815.9 3.5 copy.103
  819.4 2.7 multiply_reduce_fusion.1
  823.9 5.6 subtract_multiply_fusion
  831.1 3.9 convolution_convert_fusion.5
  838.4 3.4 convolution_convert_fusion.8
  843.2 5.5 fusion.19
  848.7 4.4 convolution_convert_fusion.6
  854.1 3.2 convolution_convert_fusion.7
  862.7 21.1 %collective-permute-done.22 = bf16[4,256,512]{2,1,0:T(8,128)(2,1)S(1)} collective-permute-done((bf16[4,256,512]{2,1,0:T(8,128)(2,1)S(1)}, bf16[4,256,512]{2,1,0:T(8,128)(2,1)S(1)}, u32[]{:S(2)}, u32[]{:S(2)}) %collective-permute-start.22) | collective-permute-done | bytes 1048608 | tf_op jit(solution)/shard_map/ppermute | solution.py:120
  884.2 22.0 %collective-permute-done.34 = bf16[4,256,512]{2,1,0:T(8,128)(2,1)S(1)} collective-permute-done((bf16[4,256,512]{2,1,0:T(8,128)(2,1)S(1)}, bf16[4,256,512]{2,1,0:T(8,128)(2,1)S(1)}, u32[]{:S(2)}, u32[]{:S(2)}) %collective-permute-start.34) | collective-permute-done | bytes 1048608 | tf_op jit(solution)/shard_map/ppermute | solution.py:120
  906.8 20.6 %collective-permute-done.28 = bf16[4,256,512]{2,1,0:T(8,128)(2,1)S(1)} collective-permute-done((bf16[4,256,512]{2,1,0:T(8,128)(2,1)S(1)}, bf16[4,256,512]{2,1,0:T(8,128)(2,1)S(1)}, u32[]{:S(2)}, u32[]{:S(2)}) %collective-permute-start.28) | collective-permute-done | bytes 1048608 | tf_op jit(solution)/shard_map/ppermute | solution.py:120
  929.7 2.7 collective-permute-start.42
  932.4 8.8 collective-permute-done.24
  941.2 9.5 collective-permute-start.35
  951.2 2.9 collective-permute-start.37
  954.7 6.8 collective-permute-done.42
  962.8 7.0 collective-permute-start.31
  969.8 8.0 collective-permute-start.30
  977.8 11.6 %collective-permute-done.36 = bf16[256,512]{1,0:T(8,128)(2,1)S(1)} collective-permute-done((bf16[256,512]{1,0:T(8,128)(2,1)}, bf16[256,512]{1,0:T(8,128)(2,1)S(1)}, u32[]{:S(2)}, u32[]{:S(2)}) %collective-permute-start.36) | collective-permute-done | bytes 262176 | tf_op jit(solution)/shard_map/ppermute | solution.py:120
  993.5 7.1 collective-permute-done.30
  1011.6 5.3 collective-permute-done.39
  1018.0 4.5 collective-permute-done.33
  1030.0 2.6 copy.100
  1040.7 2.7 fusion.72
  (405 shorter events, 146.7 us)
Async XLA Ops:
  7.2 63.1 %all-gather.11.cloned.1.call-start = ((), (), s32[]{:S(2)}) async-start(), calls=%async_computation.2 | async-start | bytes 4456448 | tf_op jit(solution)/shard_map/all_gather | solution.py:223
  9.1 162.3 %all-gather.7.cloned.1.call-start = ((), (), s32[]{:S(2)}) async-start(), calls=%async_computation | async-start | bytes 13369344 | tf_op jit(solution)/shard_map/all_gather | solution.py:223
  13.5 253.2 %all-gather.13.cloned.1.call-start = ((), (), s32[]{:S(2)}) async-start(), calls=%async_computation.3 | async-start | bytes 12255232 | tf_op jit(solution)/shard_map/all_gather | solution.py:223
  14.6 379.3 %all-gather.9.cloned.1.call-start = ((), (), s32[]{:S(2)}) async-start(), calls=%async_computation.1 | async-start | bytes 24510464 | tf_op jit(solution)/shard_map/all_gather | solution.py:223
  45.1 19.8 %collective-permute-start = (bf16[192,2048]{1,0:T(8,128)(2,1)S(1)}, bf16[192,2048]{1,0:T(8,128)(2,1)S(1)}, u32[]{:S(2)}, u32[]{:S(2)}) collective-permute-start(bf16[192,2048]{1,0:T(8,128)(2,1)S(1)} %fusion.39), channel_id=1, source_target_pairs={{0,16},{1,17},{2,18},{3,19},{4,20},{5,21},{6,22},{7,23},{8,24},{9,... | collective-permute-start | bytes 2359304 | tf_op jit(solution)/shard_map/ppermute | solution.py:120
  65.1 8.4 collective-permute-start.1
  65.2 3.6 collective-permute-start.2
  185.4 3.5 collective-permute-start.4
  191.1 19.8 %collective-permute-start.5 = (bf16[192,2048]{1,0:T(8,128)(2,1)S(1)}, bf16[192,2048]{1,0:T(8,128)(2,1)S(1)}, u32[]{:S(2)}, u32[]{:S(2)}) collective-permute-start(bf16[192,2048]{1,0:T(8,128)(2,1)S(1)} %slice.281), channel_id=1, source_target_pairs={{0,16},{1,17},{2,18},{3,19},{4,20},{5,21},{6,22},{7,23},{8,24},{9,... | collective-permute-start | bytes 2359304 | tf_op jit(solution)/shard_map/ppermute | solution.py:120
  194.1 16.8 %collective-permute-start.7 = (f32[1,192]{1,0:T(1,128)S(1)}, f32[1,192]{1,0:T(1,128)S(1)}, u32[]{:S(2)}, u32[]{:S(2)}) collective-permute-start(f32[1,192]{1,0:T(1,128)S(1)} %slice.172), channel_id=1, source_target_pairs={{0,16},{1,17},{2,18},{3,19},{4,20},{5,21},{6,22},{7,23},{8,24},{9,... | collective-permute-start | bytes 2312 | tf_op jit(solution)/shard_map/ppermute | solution.py:120
  215.3 18.0 %collective-permute-start.8 = (bf16[192,2048]{1,0:T(8,128)(2,1)S(1)}, bf16[192,2048]{1,0:T(8,128)(2,1)S(1)}, u32[]{:S(2)}, u32[]{:S(2)}) collective-permute-start(bf16[192,2048]{1,0:T(8,128)(2,1)S(1)} %multiply_convert_fusion.6), channel_id=1, source_target_pairs={{0,16},{1,17},{2,18},{3,19},{4,20},{5,21},{6,22},{7,23},{8,24},{9,... | collective-permute-start | bytes 2359304 | tf_op jit(solution)/shard_map/ppermute | solution.py:120
  234.8 38.1 %collective-permute-start.9 = (bf16[384,2048]{1,0:T(8,128)(2,1)}, bf16[384,2048]{1,0:T(8,128)(2,1)}, u32[]{:S(2)}, u32[]{:S(2)}) collective-permute-start(bf16[384,2048]{1,0:T(8,128)(2,1)} %pad_maximum_fusion.5), channel_id=1, source_target_pairs={{0,1},{1,0},{2,3},{3,2},{4,5},{5,4},{6,7},{7,6},{8,9},{9,8},{10,11... | collective-permute-start | bytes 4718600 | tf_op jit(solution)/shard_map/ppermute | solution.py:120
  234.8 20.3 %collective-permute-start.12 = (bf16[192,2048]{1,0:T(8,128)(2,1)}, bf16[192,2048]{1,0:T(8,128)(2,1)}, u32[]{:S(2)}, u32[]{:S(2)}) collective-permute-start(bf16[192,2048]{1,0:T(8,128)(2,1)} %bitcast.41), channel_id=1, source_target_pairs={{0,16},{1,17},{2,18},{3,19},{4,20},{5,21},{6,22},{7,23},{8,24},{9,... | collective-permute-start | bytes 2359304 | tf_op jit(solution)/shard_map/ppermute | solution.py:120
  257.7 152.2 %collective-permute-start.13 = (bf16[384,2048]{1,0:T(8,128)(2,1)}, bf16[384,2048]{1,0:T(8,128)(2,1)}, u32[]{:S(2)}, u32[]{:S(2)}) collective-permute-start(bf16[384,2048]{1,0:T(8,128)(2,1)} %pad_maximum_fusion.6), channel_id=1, source_target_pairs={{0,1},{1,0},{2,3},{3,2},{4,5},{5,4},{6,7},{7,6},{8,9},{9,8},{10,11... | collective-permute-start | bytes 4718600 | tf_op jit(solution)/shard_map/ppermute | solution.py:120
  442.2 34.4 %collective-permute-start.10 = (bf16[384,2048]{1,0:T(8,128)(2,1)S(1)}, bf16[384,2048]{1,0:T(8,128)(2,1)S(1)}, u32[]{:S(2)}, u32[]{:S(2)}) collective-permute-start(bf16[384,2048]{1,0:T(8,128)(2,1)S(1)} %slice.177), channel_id=1, source_target_pairs={{0,1},{1,0},{2,3},{3,2},{4,5},{5,4},{6,7},{7,6},{8,9},{9,8},{10,11... | collective-permute-start | bytes 4718600 | tf_op jit(solution)/shard_map/ppermute | solution.py:120
  442.6 31.7 %collective-permute-start.14 = (bf16[384,2048]{1,0:T(8,128)(2,1)S(1)}, bf16[384,2048]{1,0:T(8,128)(2,1)S(1)}, u32[]{:S(2)}, u32[]{:S(2)}) collective-permute-start(bf16[384,2048]{1,0:T(8,128)(2,1)S(1)} %slice.181), channel_id=1, source_target_pairs={{0,1},{1,0},{2,3},{3,2},{4,5},{5,4},{6,7},{7,6},{8,9},{9,8},{10,11... | collective-permute-start | bytes 4718600 | tf_op jit(solution)/shard_map/ppermute | solution.py:120
  454.7 67.4 %collective-permute-start.57 = (bf16[4,176,2048]{2,1,0:T(8,128)(2,1)}, bf16[4,176,2048]{2,1,0:T(8,128)(2,1)}, u32[]{:S(2)}, u32[]{:S(2)}) collective-permute-start(bf16[4,176,2048]{2,1,0:T(8,128)(2,1)} %dynamic-slice_bitcast_fusion), channel_id=1, source_target_pairs={{0,2},{1,3},{2,0},{3,1},{4,6},{5,7},{6,4},{7,5},{8,10},{9,11},{10,... | collective-permute-start | bytes 8650760 | tf_op jit(solution)/shard_map/ppermute | solution.py:120
  466.6 115.5 %collective-permute-start.45 = (bf16[4,256,1408]{2,1,0:T(8,128)(2,1)}, bf16[4,256,1408]{2,1,0:T(8,128)(2,1)}, u32[]{:S(2)}, u32[]{:S(2)}) collective-permute-start(bf16[4,256,1408]{2,1,0:T(8,128)(2,1)} %dynamic-slice_bitcast_fusion.2), channel_id=1, source_target_pairs={{0,2},{1,3},{2,0},{3,1},{4,6},{5,7},{6,4},{7,5},{8,10},{9,11},{10,... | collective-permute-start | bytes 8650760 | tf_op jit(solution)/shard_map/ppermute | solution.py:120
  475.1 20.5 %collective-permute-start.15 = (bf16[192,2048]{1,0:T(8,128)(2,1)S(1)}, bf16[192,2048]{1,0:T(8,128)(2,1)S(1)}, u32[]{:S(2)}, u32[]{:S(2)}) collective-permute-start(bf16[192,2048]{1,0:T(8,128)(2,1)S(1)} %slice.279), channel_id=1, source_target_pairs={{0,16},{1,17},{2,18},{3,19},{4,20},{5,21},{6,22},{7,23},{8,24},{9,... | collective-permute-start | bytes 2359304 | tf_op jit(solution)/shard_map/ppermute | solution.py:120
  479.0 32.4 %collective-permute-start.11 = (bf16[192,2048]{1,0:T(8,128)(2,1)S(1)}, bf16[192,2048]{1,0:T(8,128)(2,1)S(1)}, u32[]{:S(2)}, u32[]{:S(2)}) collective-permute-start(bf16[192,2048]{1,0:T(8,128)(2,1)S(1)} %slice.280), channel_id=1, source_target_pairs={{0,16},{1,17},{2,18},{3,19},{4,20},{5,21},{6,22},{7,23},{8,24},{9,... | collective-permute-start | bytes 2359304 | tf_op jit(solution)/shard_map/ppermute | solution.py:120
  482.4 160.8 %collective-permute-start.51 = (bf16[4,256,1408]{2,1,0:T(8,128)(2,1)}, bf16[4,256,1408]{2,1,0:T(8,128)(2,1)}, u32[]{:S(2)}, u32[]{:S(2)}) collective-permute-start(bf16[4,256,1408]{2,1,0:T(8,128)(2,1)} %dynamic-slice_bitcast_fusion.1), channel_id=1, source_target_pairs={{0,2},{1,3},{2,0},{3,1},{4,6},{5,7},{6,4},{7,5},{8,10},{9,11},{10,... | collective-permute-start | bytes 8650760 | tf_op jit(solution)/shard_map/ppermute | solution.py:120
  515.3 3.6 collective-permute-start.16
  518.9 3.0 collective-permute-start.17
  520.4 128.5 %collective-permute-start.18 = (bf16[192,2048]{1,0:T(8,128)(2,1)}, bf16[192,2048]{1,0:T(8,128)(2,1)}, u32[]{:S(2)}, u32[]{:S(2)}) collective-permute-start(bf16[192,2048]{1,0:T(8,128)(2,1)} %get-tuple-element.41), channel_id=1, source_target_pairs={{0,16},{1,17},{2,18},{3,19},{4,20},{5,21},{6,22},{7,23},{8,24},{9,... | collective-permute-start | bytes 2359304 | tf_op jit(solution)/shard_map/ppermute | solution.py:120
  526.4 125.4 %collective-permute-start.58 = (bf16[176,2048]{1,0:T(8,128)(2,1)S(1)}, bf16[176,2048]{1,0:T(8,128)(2,1)S(1)}, u32[]{:S(2)}, u32[]{:S(2)}) collective-permute-start(bf16[176,2048]{1,0:T(8,128)(2,1)S(1)} %get-tuple-element.54), channel_id=1, source_target_pairs={{0,4},{1,5},{2,6},{3,7},{4,8},{5,9},{6,10},{7,11},{8,12},{9,13},{1... | collective-permute-start | bytes 2162696 | tf_op jit(solution)/shard_map/ppermute | solution.py:120
  527.6 126.9 %collective-permute-start.60 = (bf16[176,2048]{1,0:T(8,128)(2,1)S(1)}, bf16[176,2048]{1,0:T(8,128)(2,1)S(1)}, u32[]{:S(2)}, u32[]{:S(2)}) collective-permute-start(bf16[176,2048]{1,0:T(8,128)(2,1)S(1)} %get-tuple-element.55), channel_id=1, source_target_pairs={{0,12},{1,13},{2,14},{3,15},{4,0},{5,1},{6,2},{7,3},{8,4},{9,5},{1... | collective-permute-start | bytes 2162696 | tf_op jit(solution)/shard_map/ppermute | solution.py:120
  582.1 73.1 %collective-permute-start.59 = (bf16[176,2048]{1,0:T(8,128)(2,1)S(1)}, bf16[176,2048]{1,0:T(8,128)(2,1)S(1)}, u32[]{:S(2)}, u32[]{:S(2)}) collective-permute-start(bf16[176,2048]{1,0:T(8,128)(2,1)S(1)} %get-tuple-element.56), channel_id=1, source_target_pairs={{0,8},{1,9},{2,10},{3,11},{4,12},{5,13},{6,14},{7,15},{8,0},{9,1},... | collective-permute-start | bytes 2162696 | tf_op jit(solution)/shard_map/ppermute | solution.py:120
  643.2 20.9 %collective-permute-start.46 = (bf16[256,1408]{1,0:T(8,128)(2,1)S(1)}, bf16[256,1408]{1,0:T(8,128)(2,1)S(1)}, u32[]{:S(2)}, u32[]{:S(2)}) collective-permute-start(bf16[256,1408]{1,0:T(8,128)(2,1)S(1)} %get-tuple-element.60), channel_id=1, source_target_pairs={{0,4},{1,5},{2,6},{3,7},{4,8},{5,9},{6,10},{7,11},{8,12},{9,13},{1... | collective-permute-start | bytes 2162696 | tf_op jit(solution)/shard_map/ppermute | solution.py:120
  648.9 44.7 %collective-permute-start.48 = (bf16[256,1408]{1,0:T(8,128)(2,1)S(1)}, bf16[256,1408]{1,0:T(8,128)(2,1)S(1)}, u32[]{:S(2)}, u32[]{:S(2)}) collective-permute-start(bf16[256,1408]{1,0:T(8,128)(2,1)S(1)} %get-tuple-element.61), channel_id=1, source_target_pairs={{0,12},{1,13},{2,14},{3,15},{4,0},{5,1},{6,2},{7,3},{8,4},{9,5},{1... | collective-permute-start | bytes 2162696 | tf_op jit(solution)/shard_map/ppermute | solution.py:120
  651.8 74.2 %collective-permute-start.47 = (bf16[256,1408]{1,0:T(8,128)(2,1)S(1)}, bf16[256,1408]{1,0:T(8,128)(2,1)S(1)}, u32[]{:S(2)}, u32[]{:S(2)}) collective-permute-start(bf16[256,1408]{1,0:T(8,128)(2,1)S(1)} %get-tuple-element.62), channel_id=1, source_target_pairs={{0,8},{1,9},{2,10},{3,11},{4,12},{5,13},{6,14},{7,15},{8,0},{9,1},... | collective-permute-start | bytes 2162696 | tf_op jit(solution)/shard_map/ppermute | solution.py:120
  654.5 74.3 %collective-permute-start.52 = (bf16[256,1408]{1,0:T(8,128)(2,1)}, bf16[256,1408]{1,0:T(8,128)(2,1)}, u32[]{:S(2)}, u32[]{:S(2)}) collective-permute-start(bf16[256,1408]{1,0:T(8,128)(2,1)} %get-tuple-element.57), channel_id=1, source_target_pairs={{0,4},{1,5},{2,6},{3,7},{4,8},{5,9},{6,10},{7,11},{8,12},{9,13},{1... | collective-permute-start | bytes 2162696 | tf_op jit(solution)/shard_map/ppermute | solution.py:120
  655.2 73.6 %collective-permute-start.54 = (bf16[256,1408]{1,0:T(8,128)(2,1)}, bf16[256,1408]{1,0:T(8,128)(2,1)}, u32[]{:S(2)}, u32[]{:S(2)}) collective-permute-start(bf16[256,1408]{1,0:T(8,128)(2,1)} %get-tuple-element.58), channel_id=1, source_target_pairs={{0,12},{1,13},{2,14},{3,15},{4,0},{5,1},{6,2},{7,3},{8,4},{9,5},{1... | collective-permute-start | bytes 2162696 | tf_op jit(solution)/shard_map/ppermute | solution.py:120
  664.1 106.6 %collective-permute-start.53 = (bf16[256,1408]{1,0:T(8,128)(2,1)}, bf16[256,1408]{1,0:T(8,128)(2,1)}, u32[]{:S(2)}, u32[]{:S(2)}) collective-permute-start(bf16[256,1408]{1,0:T(8,128)(2,1)} %get-tuple-element.59), channel_id=1, source_target_pairs={{0,8},{1,9},{2,10},{3,11},{4,12},{5,13},{6,14},{7,15},{8,0},{9,1},... | collective-permute-start | bytes 2162696 | tf_op jit(solution)/shard_map/ppermute | solution.py:120
  693.7 130.2 %collective-permute-start.19 = (bf16[384,2048]{1,0:T(8,128)(2,1)}, bf16[384,2048]{1,0:T(8,128)(2,1)}, u32[]{:S(2)}, u32[]{:S(2)}) collective-permute-start(bf16[384,2048]{1,0:T(8,128)(2,1)} %pad_maximum_fusion.7), channel_id=1, source_target_pairs={{0,1},{1,0},{2,3},{3,2},{4,5},{5,4},{6,7},{7,6},{8,9},{9,8},{10,11... | collective-permute-start | bytes 4718600 | tf_op jit(solution)/shard_map/ppermute | solution.py:120
  726.0 55.5 %collective-permute-start.61 = (bf16[176,2048]{1,0:T(8,128)(2,1)S(1)}, bf16[176,2048]{1,0:T(8,128)(2,1)}, u32[]{:S(2)}, u32[]{:S(2)}) collective-permute-start(bf16[176,2048]{1,0:T(8,128)(2,1)S(1)} %fusion.63), channel_id=1, source_target_pairs={{0,16},{1,17},{2,18},{3,19},{4,20},{5,21},{6,22},{7,23},{8,24},{9,... | collective-permute-start | bytes 2162696 | tf_op jit(solution)/shard_map/ppermute | solution.py:120
  728.8 48.4 %collective-permute-start.49 = (bf16[128,1408]{0,1:T(8,128)(2,1)}, bf16[128,1408]{0,1:T(8,128)(2,1)}, u32[]{:S(2)}, u32[]{:S(2)}) collective-permute-start(bf16[128,1408]{0,1:T(8,128)(2,1)} %bitcast.114), channel_id=1, source_target_pairs={{0,1},{1,0},{2,3},{3,2},{4,5},{5,4},{6,7},{7,6},{8,9},{9,8},{10,11... | collective-permute-start | bytes 1081352 | tf_op jit(solution)/shard_map/ppermute | solution.py:120
  777.1 2.8 collective-permute-start.55
  778.4 19.0 %collective-permute-start.50 = (bf16[2,128,1408]{1,2,0:T(8,128)(2,1)S(1)}, bf16[2,128,1408]{1,2,0:T(8,128)(2,1)S(1)}, u32[]{:S(2)}, u32[]{:S(2)}) collective-permute-start(bf16[2,128,1408]{1,2,0:T(8,128)(2,1)S(1)} %pad_maximum_fusion.15), channel_id=1, source_target_pairs={{0,16},{1,17},{2,18},{3,19},{4,20},{5,21},{6,22},{7,23},{8,24},{9,... | collective-permute-start | bytes 2162696 | tf_op jit(solution)/shard_map/ppermute | solution.py:120
  780.9 31.6 %collective-permute-start.56 = (bf16[2,128,1408]{1,2,0:T(8,128)(2,1)}, bf16[2,128,1408]{1,2,0:T(8,128)(2,1)}, u32[]{:S(2)}, u32[]{:S(2)}) collective-permute-start(bf16[2,128,1408]{1,2,0:T(8,128)(2,1)} %pad_maximum_fusion.16), channel_id=1, source_target_pairs={{0,16},{1,17},{2,18},{3,19},{4,20},{5,21},{6,22},{7,23},{8,24},{9,... | collective-permute-start | bytes 2162696 | tf_op jit(solution)/shard_map/ppermute | solution.py:120
  835.2 26.1 %collective-permute-start.40 = (bf16[4,64,2048]{2,1,0:T(8,128)(2,1)S(1)}, bf16[4,64,2048]{2,1,0:T(8,128)(2,1)S(1)}, u32[]{:S(2)}, u32[]{:S(2)}) collective-permute-start(bf16[4,64,2048]{2,1,0:T(8,128)(2,1)S(1)} %dynamic-slice_bitcast_fusion.3), channel_id=1, source_target_pairs={{0,2},{1,3},{2,0},{3,1},{4,6},{5,7},{6,4},{7,5},{8,10},{9,11},{10,... | collective-permute-start | bytes 3145736 | tf_op jit(solution)/shard_map/ppermute | solution.py:120
  841.9 41.9 %collective-permute-start.22 = (bf16[4,256,512]{2,1,0:T(8,128)(2,1)S(1)}, bf16[4,256,512]{2,1,0:T(8,128)(2,1)S(1)}, u32[]{:S(2)}, u32[]{:S(2)}) collective-permute-start(bf16[4,256,512]{2,1,0:T(8,128)(2,1)S(1)} %dynamic-slice_bitcast_fusion.6), channel_id=1, source_target_pairs={{0,2},{1,3},{2,0},{3,1},{4,6},{5,7},{6,4},{7,5},{8,10},{9,11},{10,... | collective-permute-start | bytes 3145736 | tf_op jit(solution)/shard_map/ppermute | solution.py:120
  853.2 53.1 %collective-permute-start.34 = (bf16[4,256,512]{2,1,0:T(8,128)(2,1)S(1)}, bf16[4,256,512]{2,1,0:T(8,128)(2,1)S(1)}, u32[]{:S(2)}, u32[]{:S(2)}) collective-permute-start(bf16[4,256,512]{2,1,0:T(8,128)(2,1)S(1)} %dynamic-slice_bitcast_fusion.4), channel_id=1, source_target_pairs={{0,2},{1,3},{2,0},{3,1},{4,6},{5,7},{6,4},{7,5},{8,10},{9,11},{10,... | collective-permute-start | bytes 3145736 | tf_op jit(solution)/shard_map/ppermute | solution.py:120
  857.4 70.0 %collective-permute-start.28 = (bf16[4,256,512]{2,1,0:T(8,128)(2,1)S(1)}, bf16[4,256,512]{2,1,0:T(8,128)(2,1)S(1)}, u32[]{:S(2)}, u32[]{:S(2)}) collective-permute-start(bf16[4,256,512]{2,1,0:T(8,128)(2,1)S(1)} %dynamic-slice_bitcast_fusion.5), channel_id=1, source_target_pairs={{0,2},{1,3},{2,0},{3,1},{4,6},{5,7},{6,4},{7,5},{8,10},{9,11},{10,... | collective-permute-start | bytes 3145736 | tf_op jit(solution)/shard_map/ppermute | solution.py:120
  860.0 146.1 %collective-permute-start.20 = (bf16[384,2048]{1,0:T(8,128)(2,1)}, bf16[384,2048]{1,0:T(8,128)(2,1)}, u32[]{:S(2)}, u32[]{:S(2)}) collective-permute-start(bf16[384,2048]{1,0:T(8,128)(2,1)} %slice.188), channel_id=1, source_target_pairs={{0,1},{1,0},{2,3},{3,2},{4,5},{5,4},{6,7},{7,6},{8,9},{9,8},{10,11... | collective-permute-start | bytes 4718600 | tf_op jit(solution)/shard_map/ppermute | solution.py:120
  862.6 88.5 %collective-permute-start.41 = (bf16[64,2048]{1,0:T(8,128)(2,1)}, bf16[64,2048]{1,0:T(8,128)(2,1)}, u32[]{:S(2)}, u32[]{:S(2)}) collective-permute-start(bf16[64,2048]{1,0:T(8,128)(2,1)} %get-tuple-element.70), channel_id=1, source_target_pairs={{0,4},{1,5},{2,6},{3,7},{4,8},{5,9},{6,10},{7,11},{8,12},{9,13},{1... | collective-permute-start | bytes 786440 | tf_op jit(solution)/shard_map/ppermute | solution.py:120
  884.1 45.3 %collective-permute-start.23 = (bf16[256,512]{1,0:T(8,128)(2,1)S(1)}, bf16[256,512]{1,0:T(8,128)(2,1)S(1)}, u32[]{:S(2)}, u32[]{:S(2)}) collective-permute-start(bf16[256,512]{1,0:T(8,128)(2,1)S(1)} %get-tuple-element.76), channel_id=1, source_target_pairs={{0,4},{1,5},{2,6},{3,7},{4,8},{5,9},{6,10},{7,11},{8,12},{9,13},{1... | collective-permute-start | bytes 786440 | tf_op jit(solution)/shard_map/ppermute | solution.py:120
  906.3 23.4 %collective-permute-start.25 = (bf16[256,512]{1,0:T(8,128)(2,1)S(1)}, bf16[256,512]{1,0:T(8,128)(2,1)S(1)}, u32[]{:S(2)}, u32[]{:S(2)}) collective-permute-start(bf16[256,512]{1,0:T(8,128)(2,1)S(1)} %get-tuple-element.77), channel_id=1, source_target_pairs={{0,12},{1,13},{2,14},{3,15},{4,0},{5,1},{6,2},{7,3},{8,4},{9,5},{1... | collective-permute-start | bytes 786440 | tf_op jit(solution)/shard_map/ppermute | solution.py:120
  927.4 13.8 %collective-permute-start.24 = (bf16[256,512]{1,0:T(8,128)(2,1)S(1)}, bf16[256,512]{1,0:T(8,128)(2,1)S(1)}, u32[]{:S(2)}, u32[]{:S(2)}) collective-permute-start(bf16[256,512]{1,0:T(8,128)(2,1)S(1)} %get-tuple-element.78), channel_id=1, source_target_pairs={{0,8},{1,9},{2,10},{3,11},{4,12},{5,13},{6,14},{7,15},{8,0},{9,1},... | collective-permute-start | bytes 786440 | tf_op jit(solution)/shard_map/ppermute | solution.py:120
  929.4 24.7 %collective-permute-start.43 = (bf16[64,2048]{1,0:T(8,128)(2,1)}, bf16[64,2048]{1,0:T(8,128)(2,1)}, u32[]{:S(2)}, u32[]{:S(2)}) collective-permute-start(bf16[64,2048]{1,0:T(8,128)(2,1)} %get-tuple-element.71), channel_id=1, source_target_pairs={{0,12},{1,13},{2,14},{3,15},{4,0},{5,1},{6,2},{7,3},{8,4},{9,5},{1... | collective-permute-start | bytes 786440 | tf_op jit(solution)/shard_map/ppermute | solution.py:120
  929.7 31.8 %collective-permute-start.42 = (bf16[64,2048]{1,0:T(8,128)(2,1)}, bf16[64,2048]{1,0:T(8,128)(2,1)}, u32[]{:S(2)}, u32[]{:S(2)}) collective-permute-start(bf16[64,2048]{1,0:T(8,128)(2,1)} %get-tuple-element.72), channel_id=1, source_target_pairs={{0,8},{1,9},{2,10},{3,11},{4,12},{5,13},{6,14},{7,15},{8,0},{9,1},... | collective-permute-start | bytes 786440 | tf_op jit(solution)/shard_map/ppermute | solution.py:120
  941.2 21.5 %collective-permute-start.35 = (bf16[256,512]{1,0:T(8,128)(2,1)}, bf16[256,512]{1,0:T(8,128)(2,1)}, u32[]{:S(2)}, u32[]{:S(2)}) collective-permute-start(bf16[256,512]{1,0:T(8,128)(2,1)} %get-tuple-element.79), channel_id=1, source_target_pairs={{0,4},{1,5},{2,6},{3,7},{4,8},{5,9},{6,10},{7,11},{8,12},{9,13},{1... | collective-permute-start | bytes 786440 | tf_op jit(solution)/shard_map/ppermute | solution.py:120
  951.2 18.6 %collective-permute-start.37 = (bf16[256,512]{1,0:T(8,128)(2,1)}, bf16[256,512]{1,0:T(8,128)(2,1)S(1)}, u32[]{:S(2)}, u32[]{:S(2)}) collective-permute-start(bf16[256,512]{1,0:T(8,128)(2,1)} %get-tuple-element.80), channel_id=1, source_target_pairs={{0,12},{1,13},{2,14},{3,15},{4,0},{5,1},{6,2},{7,3},{8,4},{9,5},{1... | collective-permute-start | bytes 786440 | tf_op jit(solution)/shard_map/ppermute | solution.py:120
  954.1 35.3 %collective-permute-start.36 = (bf16[256,512]{1,0:T(8,128)(2,1)}, bf16[256,512]{1,0:T(8,128)(2,1)S(1)}, u32[]{:S(2)}, u32[]{:S(2)}) collective-permute-start(bf16[256,512]{1,0:T(8,128)(2,1)} %get-tuple-element.81), channel_id=1, source_target_pairs={{0,8},{1,9},{2,10},{3,11},{4,12},{5,13},{6,14},{7,15},{8,0},{9,1},... | collective-permute-start | bytes 786440 | tf_op jit(solution)/shard_map/ppermute | solution.py:120
  961.5 31.5 %collective-permute-start.29 = (bf16[256,512]{1,0:T(8,128)(2,1)}, bf16[256,512]{1,0:T(8,128)(2,1)}, u32[]{:S(2)}, u32[]{:S(2)}) collective-permute-start(bf16[256,512]{1,0:T(8,128)(2,1)} %get-tuple-element.73), channel_id=1, source_target_pairs={{0,4},{1,5},{2,6},{3,7},{4,8},{5,9},{6,10},{7,11},{8,12},{9,13},{1... | collective-permute-start | bytes 786440 | tf_op jit(solution)/shard_map/ppermute | solution.py:120
  962.8 30.2 %collective-permute-start.31 = (bf16[256,512]{1,0:T(8,128)(2,1)S(1)}, bf16[256,512]{1,0:T(8,128)(2,1)S(1)}, u32[]{:S(2)}, u32[]{:S(2)}) collective-permute-start(bf16[256,512]{1,0:T(8,128)(2,1)S(1)} %get-tuple-element.74), channel_id=1, source_target_pairs={{0,12},{1,13},{2,14},{3,15},{4,0},{5,1},{6,2},{7,3},{8,4},{9,5},{1... | collective-permute-start | bytes 786440 | tf_op jit(solution)/shard_map/ppermute | solution.py:120
  969.8 30.7 %collective-permute-start.30 = (bf16[256,512]{1,0:T(8,128)(2,1)S(1)}, bf16[256,512]{1,0:T(8,128)(2,1)S(1)}, u32[]{:S(2)}, u32[]{:S(2)}) collective-permute-start(bf16[256,512]{1,0:T(8,128)(2,1)S(1)} %get-tuple-element.75), channel_id=1, source_target_pairs={{0,8},{1,9},{2,10},{3,11},{4,12},{5,13},{6,14},{7,15},{8,0},{9,1},... | collective-permute-start | bytes 786440 | tf_op jit(solution)/shard_map/ppermute | solution.py:120
  989.4 16.5 %collective-permute-start.44 = (bf16[64,2048]{1,0:T(8,128)(2,1)S(1)}, bf16[64,2048]{1,0:T(8,128)(2,1)S(1)}, u32[]{:S(2)}, u32[]{:S(2)}) collective-permute-start(bf16[64,2048]{1,0:T(8,128)(2,1)S(1)} %fusion.78), channel_id=1, source_target_pairs={{0,16},{1,17},{2,18},{3,19},{4,20},{5,21},{6,22},{7,23},{8,24},{9,... | collective-permute-start | bytes 786440 | tf_op jit(solution)/shard_map/ppermute | solution.py:120
  993.0 9.0 collective-permute-start.26
  993.0 10.6 %collective-permute-start.38 = (bf16[128,512]{0,1:T(8,128)(2,1)}, bf16[128,512]{0,1:T(8,128)(2,1)S(1)}, u32[]{:S(2)}, u32[]{:S(2)}) collective-permute-start(bf16[128,512]{0,1:T(8,128)(2,1)} %bitcast.88), channel_id=1, source_target_pairs={{0,1},{1,0},{2,3},{3,2},{4,5},{5,4},{6,7},{7,6},{8,9},{9,8},{10,11... | collective-permute-start | bytes 393224 | tf_op jit(solution)/shard_map/ppermute | solution.py:120
  1001.9 2.4 collective-permute-start.32
  1002.1 9.4 collective-permute-start.27
  1003.7 13.2 %collective-permute-start.39 = (bf16[2,128,512]{1,2,0:T(8,128)(2,1)S(1)}, bf16[2,128,512]{1,2,0:T(8,128)(2,1)S(1)}, u32[]{:S(2)}, u32[]{:S(2)}) collective-permute-start(bf16[2,128,512]{1,2,0:T(8,128)(2,1)S(1)} %pad_maximum_fusion.20), channel_id=1, source_target_pairs={{0,16},{1,17},{2,18},{3,19},{4,20},{5,21},{6,22},{7,23},{8,24},{9,... | collective-permute-start | bytes 786440 | tf_op jit(solution)/shard_map/ppermute | solution.py:120
  1004.3 18.1 %collective-permute-start.33 = (bf16[2,128,512]{1,2,0:T(8,128)(2,1)S(1)}, bf16[2,128,512]{1,2,0:T(8,128)(2,1)S(1)}, u32[]{:S(2)}, u32[]{:S(2)}) collective-permute-start(bf16[2,128,512]{1,2,0:T(8,128)(2,1)S(1)} %pad_maximum_fusion.19), channel_id=1, source_target_pairs={{0,16},{1,17},{2,18},{3,19},{4,20},{5,21},{6,22},{7,23},{8,24},{9,... | collective-permute-start | bytes 786440 | tf_op jit(solution)/shard_map/ppermute | solution.py:120
  1010.9 28.1 %collective-permute-start.21 = (bf16[192,2048]{1,0:T(8,128)(2,1)}, bf16[192,2048]{1,0:T(8,128)(2,1)}, u32[]{:S(2)}, u32[]{:S(2)}) collective-permute-start(bf16[192,2048]{1,0:T(8,128)(2,1)} %slice.278), channel_id=1, source_target_pairs={{0,16},{1,17},{2,18},{3,19},{4,20},{5,21},{6,22},{7,23},{8,24},{9,... | collective-permute-start | bytes 2359304 | tf_op jit(solution)/shard_map/ppermute | solution.py:120
  (75 other events, 1155.5 us)
Sparse Core Ops, SparseCore 0:
  10.8 53.4 all-gather.10
  67.0 104.4 all-gather.6
  174.3 92.4 all-gather.12
  268.7 125.0 all-gather.8

commit v2 on v1

v2 whole, which is shorter than its diff:
```python
import functools

import jax
import jax.numpy as jnp
from jax import lax
from jax.experimental import pallas as pl
from jax.experimental.pallas import tpu as pltpu
from jax.sharding import PartitionSpec as P

EPSILON = 1e-06
AXES = ("rep", "shard")
CORES = 2
F32 = jnp.float32
BF16 = jnp.bfloat16


def normalize(values):
    scale = lax.rsqrt(jnp.mean(values * values, axis=-1, keepdims=True) + EPSILON)
    return (values * scale, scale)


def norm_back(grad_scaled, scaled, scale):
    inner = jnp.mean(grad_scaled * scaled, axis=-1, keepdims=True)
    return scale * (grad_scaled - scaled * inner)


def swish_pair(values):
    sigma = jax.nn.sigmoid(values)
    return (values * sigma, sigma * (1.0 + values * (1.0 - sigma)))


def matmul(left, right, dims, out=F32):
    return lax.dot_general(left, right, ((dims[:1], dims[1:]), ((), ())), preferred_element_type=F32).astype(out)


TILE = 8


def scan_tile(decay, update, reverse):
    row = lax.broadcasted_iota(jnp.int32, decay.shape, 0)
    for step in (1, 2, 4):
        shift = TILE - step if reverse else step
        inside = row < TILE - step if reverse else row >= step
        earlier = jnp.where(inside, pltpu.roll(update, shift, 0), 0.0)
        product = jnp.where(inside, pltpu.roll(decay, shift, 0), 1.0)
        update = update + decay * earlier
        decay = decay * product
    return (decay, update)


def scan_forward_kernel(count, length, decay, update, state):
    def block(step, carries):
        out = []
        for n in range(count):
            rows = pl.ds(pl.multiple_of(n * length + step * TILE, TILE), TILE)
            product, local = scan_tile(decay[rows, :], update[rows, :], False)
            local = local + product * carries[n]
            state[rows, :] = local
            out.append(local[TILE - 1 :, :])
        return tuple(out)

    lax.fori_loop(0, length // TILE, block, (jnp.zeros((1, state.shape[1]), F32),) * count)


def scan_backward_kernel(count, length, decay, grad, carried):
    steps = length // TILE

    def block(step, pairs):
        out = []
        for n in range(count):
            carry, later = pairs[n]
            rows = pl.ds(pl.multiple_of(n * length + (steps - 1 - step) * TILE, TILE), TILE)
            own = decay[rows, :]
            row = lax.broadcasted_iota(jnp.int32, own.shape, 0)
            following = jnp.where(row < TILE - 1, pltpu.roll(own, TILE - 1, 0), later)
            product, local = scan_tile(following, grad[rows, :], True)
            local = local + product * carry
            carried[rows, :] = local
            out.append((local[:1, :], own[:1, :]))
        return tuple(out)

    zero = jnp.zeros((1, carried.shape[1]), F32)
    lax.fori_loop(0, steps, block, ((zero, zero),) * count)


def run_scan(kernel, name, count, length, left, right):
    size = left.size
    return pl.pallas_call(
        functools.partial(kernel, count, length),
        out_shape=jax.ShapeDtypeStruct(left.shape, F32),
        in_specs=[pl.BlockSpec(memory_space=pltpu.VMEM)] * 2,
        out_specs=pl.BlockSpec(memory_space=pltpu.VMEM),
        compiler_params=pltpu.CompilerParams(vmem_limit_bytes=32 * 2**20),
        cost_estimate=pl.CostEstimate(flops=2 * size, bytes_accessed=12 * size, transcendentals=0),
        name=name,
    )(left, right)


def move_kernel(blocks, source, value, out):
    wide = value.shape[1] // blocks
    for k in range(blocks):
        out[:, k * wide : (k + 1) * wide] = value[:, pl.ds(pl.multiple_of(source[k] * wide, 128), wide)]


def move_blocks(source, value):
    return pl.pallas_call(
        functools.partial(move_kernel, source.shape[0]),
        out_shape=jax.ShapeDtypeStruct(value.shape, value.dtype),
        in_specs=[pl.BlockSpec(memory_space=pltpu.SMEM), pl.BlockSpec(memory_space=pltpu.VMEM)],
        out_specs=pl.BlockSpec(memory_space=pltpu.VMEM),
        cost_estimate=pl.CostEstimate(flops=0, bytes_accessed=2 * value.size * value.dtype.itemsize, transcendentals=0),
        name="move_blocks",
    )(source, value)


class Place:
    def __init__(self, reps, shards):
        self.reps, self.shards = reps, shards
        self.chips = shards // CORES
        self.hi = self.chips // 4
        self.r = lax.axis_index("rep")
        self.s = lax.axis_index("shard")
        self.c = self.s % CORES
        self.core = ("shard", 1)
        self.low = ("shard", 2)
        self.lo = ("shard", 4)
        self.his = [("shard", 8 << k) for k in range(self.hi.bit_length() - 1)]
        self.rep_bits = [("rep", 1 << k) for k in range(reps.bit_length() - 1)]
        self.mixers = self.rep_bits + [self.core]
        self.feeders = self.rep_bits + [self.lo, self.core]

    def bit(self, which):
        axis, value = which
        return ((self.r if axis == "rep" else self.s) // value) % 2

    def swap(self, value, which):
        axis, flip = which
        flip = flip * self.shards if axis == "rep" else flip
        return lax.ppermute(value, AXES, [(n, n ^ flip) for n in range(self.reps * self.shards)])

    def merge(self, own, other, which, axis=0):
        first = self.bit(which) == 0
        return jnp.stack([jnp.where(first, own, other), jnp.where(first, other, own)], axis)

    def join(self, value, which, axis=0):
        return self.merge(value, self.swap(value, which), which, axis)

    def pick(self, value, which, axis, flipped=False):
        bit = self.bit(which)
        return lax.dynamic_index_in_dim(value, 1 - bit if flipped else bit, axis, keepdims=False)

    def trade(self, value, which, axis):
        other = self.swap(self.pick(value, which, axis, True), which)
        return self.merge(self.pick(value, which, axis), other, which)

    def reduce(self, value, which, axis):
        other = self.swap(self.pick(value, which, axis, True), which)
        return (self.pick(value, which, axis).astype(F32) + other.astype(F32)).astype(BF16)

    def extend(self, value, which):
        return jnp.concatenate([value, self.swap(value, which)], axis=0)

    def fold(self, value, which):
        half = value.shape[0] // 2
        other = self.swap(value[half:], which)
        return (value[:half].astype(F32) + other.astype(F32)).astype(BF16)

    def block_order(self, value, back=False):
        place = jnp.arange(self.chips, dtype=jnp.int32)
        here = self.s // CORES
        if back:
            other = place ^ (here & ~2)
            source = (other & 1) * (2 * self.hi) + (other >> 1)
        else:
            chip = (place % (2 * self.hi)) * 2 + place // (2 * self.hi)
            source = chip ^ (here & ~2)
        return move_blocks(source, value)

    def gather_members(self, value, bits):
        for which in bits:
            value = jnp.concatenate([value, self.swap(value, which)], axis=0)
        return value

    def sum_members(self, partial, bits):
        wire, total = partial.dtype, partial
        for which in bits[::-1]:
            half = total.shape[0] // 2
            total = total[:half].astype(F32) + self.swap(total[half:].astype(wire), which).astype(F32)
        return total

    def join_his(self, value):
        for which in self.his:
            value = self.join(value, which)
        return value.reshape((self.hi,) + value.shape[len(self.his) :])

    def reduce_his(self, value):
        value = value.reshape((2,) * len(self.his) + value.shape[1:])
        for which in self.his[::-1]:
            value = self.reduce(value, which, 0)
        return value

    def join_reps(self, value):
        for which in self.rep_bits:
            value = self.join(value, which)
        return value.reshape((self.reps,) + value.shape[len(self.rep_bits) :])

    def own_rep(self, weight):
        return lax.dynamic_index_in_dim(weight.reshape(self.reps, -1, weight.shape[1]), self.r, 0, keepdims=False)

    def groups(self, bits):
        flips = [value * self.shards if axis == "rep" else value for axis, value in bits]
        group = [0]
        for flip in flips:
            group = group + [n + flip for n in group]
        group = sorted(group)
        return [[base + n for n in group] for base in range(self.reps * self.shards) if not base & sum(flips)]

    def gather_group(self, value):
        return lax.all_gather(value, AXES, axis=0, tiled=True, axis_index_groups=self.groups(self.feeders))

    def sum_group(self, value):
        return lax.psum_scatter(value, AXES, scatter_dimension=0, tiled=True, axis_index_groups=self.groups(self.feeders)).astype(F32)


def fence(*values):
    return lax.optimization_barrier(values)


def late(value, *others):
    return fence(value, *others)[0]


def chooser(sources, targets, source_of):
    row = lax.broadcasted_iota(jnp.int32, (sources, targets), 0)
    column = lax.broadcasted_iota(jnp.int32, (sources, targets), 1)
    return (row == source_of(column)).astype(BF16)


def shards(
    reps,
    places,
    tokens,
    segment_ids,
    norm_gain,
    input_weight,
    forget_weight,
    gate_weight,
    mixer_gain,
    out_weight,
    ffn_gain,
    ffn_gate_weight,
    ffn_up_weight,
    ffn_down_weight,
    cotangent,
):
    at = Place(reps, places)
    inputs = tokens[0].astype(F32)
    length, width = inputs.shape
    units = ffn_up_weight.shape[1]
    count = 2 ** len(at.mixers)
    channels = width // count
    part = units // 2 ** len(at.feeders)
    rows = width // places
    small = rows // reps
    slim = units // (places * reps)
    chip_rows = CORES * rows

    def channel_source(position):
        core, chip, inner = position // channels, position % channels // small, position % small
        return ((chip * CORES + core) * reps + at.r) * small + inner

    triple_rows = jnp.concatenate([input_weight, forget_weight, gate_weight])
    picked = matmul(triple_rows, chooser(width, CORES * channels, channel_source), (1, 0), BF16)
    picked = picked.reshape(3, rows, CORES, channels).transpose(1, 2, 0, 3).reshape(rows, -1)
    mix_all = lax.all_gather(picked, "shard", axis=0, tiled=True)

    def unit_source(core):
        def source(position):
            hi, low, inner = position // (2 * slim), position % (2 * slim) // slim, position % slim
            return hi * (units // (2 * at.hi)) + ((low * CORES + core) * reps + at.r) * slim + inner

        return source

    pair_rows = jnp.concatenate([ffn_gate_weight, ffn_up_weight])
    strip = units // (2 * at.hi)
    strips = [pair_rows[:, k * strip : (k + 1) * strip] for k in range(2 * at.hi)]
    pair_lines = jnp.concatenate([jnp.concatenate(strips[k::2], axis=1) for k in range(2)])
    pick_units = lambda core: matmul(pair_lines, chooser(units // 2, part, unit_source(core)), (1, 0), BF16)
    kept, given = pick_units(at.c), pick_units(1 - at.c)

    grad_out = cotangent[0]
    all_tokens = at.gather_members(tokens[0], at.mixers)
    segments = at.gather_members(segment_ids, at.mixers)
    starts = jnp.zeros((count, 1), F32)
    same = jnp.concatenate([starts, (segments[:, 1:] == segments[:, :-1]).astype(F32)], axis=1)
    same = same.reshape(count * length, 1)
    out_rows = at.join(at.join_his(at.join(at.own_rep(out_weight), at.lo)), at.low, 2).reshape(channels, width)
    gains = lax.all_gather(jnp.stack([norm_gain, mixer_gain, ffn_gain]), "shard", axis=1, tiled=True).astype(F32)
    gain_one, gain_two, gain_three = gains[0], gains[1], gains[2]
    gain_grid = gain_two.reshape(at.chips, CORES, reps, small)
    gain_mix = lax.dynamic_index_in_dim(lax.dynamic_index_in_dim(gain_grid, at.c, 1, keepdims=False), at.r, 1, keepdims=False).reshape(-1)
    normed = (normalize(all_tokens.astype(F32))[0] * gain_one).astype(BF16)
    lines = lambda value: value.reshape(2 * CORES, rows, part)
    chip = at.merge(lines(kept), lines(at.swap(given, at.core)), at.core, 1).reshape(2, CORES * chip_rows, part)
    mix_all, normed, same, chip, out_rows, grad_out_sent, own_down = fence(
        mix_all, normed, same, chip, out_rows, grad_out, at.own_rep(ffn_down_weight)
    )

    all_grad_out = at.gather_group(grad_out_sent)
    own_pair = at.trade(chip, at.lo, 0)
    mix_weight = lax.dynamic_slice_in_dim(mix_all, at.c * (3 * channels), 3 * channels, 1)
    pre = matmul(normed, mix_weight, (1, 0))
    input_pre, forget_pre, gate_pre = (pre[:, k * channels : (k + 1) * channels] for k in range(3))
    forget = jax.nn.sigmoid(forget_pre)
    input_act, input_slope = swish_pair(input_pre)
    decay = forget * same
    state = run_scan(scan_forward_kernel, "scan_forward", count, length, decay, input_act * (1.0 - forget))
    gate_act, gate_slope = swish_pair(gate_pre)
    mixed_raw = (state * gain_mix * gate_act).astype(BF16)
    squares = jnp.sum(state * state, axis=1).reshape(count, length)
    out_part, squares, own_pair = fence(matmul(mixed_raw, out_rows, (1, 0), BF16), squares, own_pair)

    pair_grid = own_pair.reshape(2, 2, chip_rows, part)
    gate_half, up_half = pair_grid[:, 0].reshape(-1, part), pair_grid[:, 1].reshape(-1, part)
    for which in at.his:
        gate_half = at.extend(gate_half, which)
    square_sum = at.sum_members(squares, at.mixers)
    branch_sum = at.sum_members(out_part, at.mixers)
    branch_sum, square_sum, gate_half, up_half = fence(branch_sum, square_sum, gate_half, up_half)

    gate_columns = at.extend(gate_half, at.low)
    for which in at.his:
        up_half = at.extend(up_half, which)
    state_scale = lax.rsqrt(square_sum / width + EPSILON)
    branch = branch_sum * state_scale.reshape(length, 1)
    resid = inputs + branch
    scaled_mid, scale_mid = normalize(resid)
    ffn_in = at.gather_group(at.block_order((scaled_mid * gain_three).astype(BF16)))
    ffn_in, gate_columns, up_half, own_down, all_grad_out = fence(ffn_in, gate_columns, up_half, own_down, all_grad_out)
    up_columns = at.extend(up_half, at.low)
    down_lines = at.join_his(own_down)
    ffn_gate = matmul(ffn_in, gate_columns, (1, 0))
    ffn_gate, up_columns, down_lines, ffn_in = fence(ffn_gate, up_columns, down_lines, ffn_in)
    down_rows = at.join(down_lines, at.low, 1).reshape(part, width)
    ffn_up = matmul(ffn_in, up_columns, (1, 0))
    ffn_act, ffn_slope = swish_pair(ffn_gate)
    hidden = (ffn_act * ffn_up).astype(BF16)
    down_cut = matmul(hidden, all_grad_out, (0, 0), BF16)
    down_rows, down_cut, hidden = fence(down_rows, down_cut, hidden)
    down_grid = down_cut.reshape(at.hi, 2, -1, width)
    down_line = at.reduce(down_grid, at.low, 1)
    grad_hidden = matmul(all_grad_out, down_rows, (1, 1))
    grad_fgate = (grad_hidden * ffn_up * ffn_slope).astype(BF16)
    grad_fup = (grad_hidden * ffn_act).astype(BF16)
    grad_cut = (matmul(grad_fgate, gate_columns, (1, 1)) + matmul(grad_fup, up_columns, (1, 1))).astype(BF16)
    grad_cut, grad_fgate, grad_fup = fence(grad_cut, grad_fgate, grad_fup)

    grad_ffn_in = at.sum_group(grad_cut)
    gate_cut = matmul(ffn_in, grad_fgate, (0, 0), BF16)
    up_cut = matmul(ffn_in, grad_fup, (0, 0), BF16)
    ffn_part = matmul(hidden, down_rows, (1, 0), BF16)
    gate_line = at.fold(gate_cut, at.low)
    grad_ffn_in, gate_line, down_line, ffn_part, up_cut = fence(grad_ffn_in, gate_line, down_line, ffn_part, up_cut)
    up_line = at.fold(up_cut, at.low)
    down_own = at.reduce_his(down_line)
    grad_ffn_in = at.block_order(grad_ffn_in.astype(BF16), True).astype(F32)
    grad_resid = grad_out.astype(F32) + norm_back(grad_ffn_in * gain_three, scaled_mid, scale_mid)
    grad_branch_own = grad_resid.astype(BF16)
    inner_own = jnp.mean(grad_branch_own.astype(F32) * branch, axis=1)
    row_facts = at.gather_members(jnp.stack([state_scale.reshape(length), inner_own])[None], at.mixers)
    grad_branch = at.gather_members(grad_branch_own, at.mixers)
    grad_branch, row_facts, down_own, up_line, ffn_part, gate_line = fence(grad_branch, row_facts, down_own, up_line, ffn_part, gate_line)

    all_scale = row_facts[:, 0].reshape(count * length, 1)
    all_inner = row_facts[:, 1].reshape(count * length, 1)
    state_scaled = state * all_scale
    mixed = (state_scaled * gain_mix * gate_act).astype(BF16)
    weighted = matmul(grad_branch, out_rows, (1, 1)) * gain_mix

    def plane_grad(left, right, own_rows):
        cut = matmul(left, right, (0, 0), BF16).reshape(at.hi, 2, 2, own_rows, -1)
        return at.reduce(at.reduce_his(at.reduce(cut, at.low, 2)), at.lo, 0)

    out_own = plane_grad(mixed, grad_branch, small)
    grad_gate_pre = (weighted * state_scaled * gate_slope).astype(BF16)
    grad_state = all_scale * (weighted * gate_act - state_scaled * all_inner)
    carried = run_scan(scan_backward_kernel, "scan_backward", count, length, decay, grad_state)
    line = state.reshape(count, length, channels)
    previous = jnp.concatenate([jnp.zeros((count, 1, channels), F32), line[:, :-1]], axis=1).reshape(state.shape)
    grad_forget = carried * previous * same - carried * input_act
    grad_input_pre = (carried * (1.0 - forget) * input_slope).astype(BF16)
    grad_forget_pre = (grad_forget * forget * (1.0 - forget)).astype(BF16)
    triple = jnp.concatenate([grad_input_pre, grad_forget_pre, grad_gate_pre], axis=1)
    grad_normed = at.sum_members(matmul(triple, mix_weight, (1, 1), BF16), at.mixers)

    def channel_grad(right):
        return at.trade(plane_grad(normed, right, chip_rows).reshape(CORES, rows, channels), at.core, 0)

    mix_owns = [channel_grad(g) for g in (grad_input_pre, grad_forget_pre, grad_gate_pre)]

    def unit_grad(lines):
        for which in at.his[::-1]:
            lines = at.fold(lines, which)
        sets = at.trade(lines.reshape(2, chip_rows, part), at.lo, 0)
        return at.trade(sets.reshape(2, CORES, rows, part), at.core, 1)

    gate_own, up_own = unit_grad(gate_line), unit_grad(up_line)
    ffn_out = late(at.sum_group(ffn_part), triple)
    block_output = (resid + ffn_out).astype(BF16)
    scaled_in, scale_in = normalize(inputs)
    input_grad = (grad_resid + norm_back(grad_normed * gain_one, scaled_in, scale_in)).astype(BF16)

    def channel_place(column):
        chip, core = column // (CORES * reps * small), column // (reps * small) % CORES
        return ((column // small % reps * CORES + core) * at.chips + chip) * small + column % small

    def whole_channels(owns):
        joined = jnp.stack([at.join_reps(own) for own in owns])
        lines = joined.reshape(len(owns), reps * CORES, rows, channels).transpose(0, 2, 1, 3).reshape(-1, width)
        return jnp.split(matmul(lines, chooser(width, width, channel_place), (1, 0)), len(owns))

    def whole_units(own):
        grid = at.join_reps(own).reshape(reps, CORES, 2, rows, at.hi, 2, slim)
        return grid.transpose(3, 4, 2, 5, 1, 0, 6).reshape(rows, units).astype(F32)

    def whole_rows(own):
        return at.join_reps(own).reshape(-1, width).astype(F32)

    down_total = whole_rows(down_own)
    gate_total, up_total = whole_units(gate_own), whole_units(up_own)
    out_total = whole_rows(out_own)
    mix_totals = whole_channels(mix_owns)
    dotted = lambda w, g: jnp.sum(w.astype(F32) * g, axis=1)
    norm_gain_grad = sum(dotted(w, g) for w, g in zip((input_weight, forget_weight, gate_weight), mix_totals)) / norm_gain.astype(F32)
    mixer_gain_grad = dotted(out_weight, out_total) / mixer_gain.astype(F32)
    ffn_gain_grad = (dotted(ffn_gate_weight, gate_total) + dotted(ffn_up_weight, up_total)) / ffn_gain.astype(F32)
    return (
        block_output[None],
        input_grad[None],
        norm_gain_grad,
        *mix_totals,
        mixer_gain_grad,
        out_total,
        ffn_gain_grad,
        gate_total,
        up_total,
        down_total,
    )


def solution(mesh):
    tokens, vector, matrix = P(AXES, None, None), P("shard"), P("shard", None)
    placed = (tokens, P(AXES, None), vector, matrix, matrix, matrix, vector, matrix, vector, matrix, matrix, matrix, tokens)
    return jax.shard_map(
        functools.partial(shards, mesh.shape["rep"], mesh.shape["shard"]),
        mesh=mesh,
        in_specs=placed,
        out_specs=(tokens, tokens, vector, matrix, matrix, matrix, vector, matrix, vector, matrix, matrix, matrix),
        check_vma=False,
    )
```

time: 1060 us -> 797 us (0.75)
  waiting for transfers between devices: 657 us -> 379 us
  starting transfers between devices: 107 us -> 45 us
  other arithmetic: 62.7 us -> 107 us
  local copies, waits for them, and re-layouts: 76.3 us -> 96.4 us
  matrix products: 105 us -> 118 us
    all_gather x4 -> x3, waiting for transfers between devices: 228 us -> 25.6 us  [the longest x2 14.4 us: gather_group(): lax.all_gather(value, AXES, axis=0, tiled=True, axis_index_groups=self.gr...]
    ppermute x62 -> x57, waiting for transfers between devices: 429 us -> 353 us  [swap(): lax.ppermute(value, AXES, [(n, n ^ flip) for n in range(self.reps * self....]
    ppermute x62 -> x57, starting transfers between devices: 107 us -> 44.6 us  [swap(): lax.ppermute(value, AXES, [(n, n ^ flip) for n in range(self.reps * self....]
    another operation x16 -> x34, other arithmetic: 4 us -> 24.4 us  [the longest x33 23.1 us: merge(): jnp.stack([jnp.where(first, own, other), jnp.where(first, other, own)], a...]
    dot_general x15 -> x21, matrix products: 105 us -> 118 us  [matmul(): lax.dot_general(left, right, ((dims[:1], dims[1:]), ((), ())), preferred_...]
    convert_element_type x22 -> x24, other arithmetic: 21.9 us -> 34.4 us  [the longest x14 15.4 us: reduce(): (self.pick(value, which, axis).astype(F32) + other.astype(F32)).astype(BF16)]
    slice x12 -> x14, local copies, waits for them, and re-layouts: 3.21 us -> 14.2 us  [the longest x6 4.46 us: sum_members(): total[half:].astype(wire)]
    reshape x0 -> x7, local copies, waits for them, and re-layouts: none -> 10.9 us  [the longest x2 4.61 us: shards(): picked.reshape(3, rows, CORES, channels).transpose(1, 2, 0, 3)]
  transfers between devices with their start and end apart: 66 -> 62, of which waited for: 32 -> 30; matrix products, arithmetic and copies ran while one was open for 18% -> 33% of each run, Pallas kernels for 0% -> 1%
where the time goes in v2:
time: 797 us; the launch traced here: 790 us
  waiting for transfers between devices  379 us (48%)
  matrix products  118 us (15%)
  other arithmetic  107 us (13%)
  local copies, waits for them, and re-layouts  96.4 us (12%)
  starting transfers between devices  45 us (6%)
  blocking collectives  20.9 us (3%)
  between operations  16.4 us (2%)
    ppermute x57, waiting for transfers between devices, swap(): lax.ppermute(value, AXES, [(n, n ^ flip) for n in range(self.reps * self....  353 us
    dot_general x21, matrix products, matmul(): lax.dot_general(left, right, ((dims[:1], dims[1:]), ((), ())), preferred_...  118 us
    ppermute x57, starting transfers between devices, swap(): lax.ppermute(value, AXES, [(n, n ^ flip) for n in range(self.reps * self....  44.6 us
    unnamed x288, local copies, waits for them, and re-layouts  36.9 us
    another operation x33, other arithmetic, merge(): jnp.stack([jnp.where(first, own, other), jnp.where(first, other, own)], a...  23.1 us
    all_gather x1, blocking collectives, shards(): lax.all_gather(jnp.stack([norm_gain, mixer_gain, ffn_gain]), 'shard', axi...  20.9 us
  transfers between devices with their start and end apart: 62, of which 30 were waited for; matrix products, arithmetic and copies ran while one was open for 33% of the time, Pallas kernels for 1%

profile of v2, /device:TPU:0, one launch (start us, length us, event | category | flops | bytes accessed | tf_op | source)
XLA Modules:
  0.0 790.3 jit_solution(4889622930614295332)
XLA Ops:
  7.3 3.4 fusion.134
  12.2 3.2 copy.102
  16.2 3.0 collective-permute-start.5
  21.3 3.5 fusion.142
  27.0 20.9 %all_gather.13 = bf16[3,2048]{1,0:T(4,128)(2,1)S(1)} all-gather(bf16[3,128]{1,0:T(4,128)(2,1)S(1)} %pad_maximum_fusion.29), channel_id=1, replica_groups=mesh['rep'=2,'shard'=16] {'shard'}, dimensions={1}, use_global_device_ids=true | all-gather | bytes 13056 | tf_op jit(solution)/shard_map/all_gather | solution.py:298
  52.9 38.2 %collective-permute-done.6 = bf16[2,64,2048]{2,1,0:T(8,128)(2,1)} collective-permute-done((bf16[2,64,2048]{2,1,0:T(8,128)(2,1)S(1)}, bf16[2,64,2048]{2,1,0:T(8,128)(2,1)}, u32[]{:S(2)}, u32[]{:S(2)}) %collective-permute-start.6) | collective-permute-done | bytes 524320 | tf_op jit(solution)/shard_map/ppermute | solution.py:139
  94.9 4.8 broadcast_select_fusion.5
  104.2 2.7 pad_maximum_fusion.8
  106.9 28.6 %collective-permute-done.7 = bf16[2,2,64,2048]{3,2,1,0:T(8,128)(2,1)} collective-permute-done((bf16[2,2,64,2048]{3,2,1,0:T(8,128)(2,1)}, bf16[2,2,64,2048]{3,2,1,0:T(8,128)(2,1)}, u32[]{:S(2)}, u32[]{:S(2)}) %collective-permute-start.7) | collective-permute-done | bytes 1048608 | tf_op jit(solution)/shard_map/ppermute | solution.py:139
  140.4 5.2 fusion.54
  145.6 11.2 %all-gather.4.cloned.1.call-done = bf16[2048,3072]{0,1:T(8,128)(2,1)} async-done(((bf16[128,3072]{0,1:T(8,128)(2,1)}), bf16[2048,3072]{0,1:T(8,128)(2,1)}) %all-gather.4.cloned.1.call-update) | async-done | bytes 12582928 | tf_op jit(solution)/shard_map/all_gather | solution.py:275
  159.3 8.7 %fusion.57 = f32[768,1536]{1,0:T(8,128)S(1)} fusion(bf16[768,2048]{1,0:T(8,128)(2,1)} %fusion.54, bf16[2048,3072]{0,1:T(8,128)(2,1)} %all-gather.4.cloned.1.call-done, s32[]{:T(128)S(6)} %select_n.662), kind=kOutput, calls=%fused_computation.81 | convolution fusion | flops 4831838208 | bytes 14155780 | tf_op jit(solution)/shard_map/dot_general | solution.py:33
  173.0 4.0 convolution_convert_fusion.1
  177.0 9.6 %collective-permute-done.8 = bf16[512,704]{0,1:T(8,128)(2,1)} collective-permute-done((bf16[512,704]{0,1:T(8,128)(2,1)S(1)}, bf16[512,704]{0,1:T(8,128)(2,1)}, u32[]{:S(2)}, u32[]{:S(2)}) %collective-permute-start.8) | collective-permute-done | bytes 720928 | tf_op jit(solution)/shard_map/ppermute | solution.py:139
  190.4 3.5 reshape.261
  193.8 2.9 fusion.238
  211.3 14.2 %collective-permute-done.12 = f32[1,192]{1,0:T(1,128)S(1)} collective-permute-done((f32[1,192]{1,0:T(1,128)S(1)}, f32[1,192]{1,0:T(1,128)S(1)}, u32[]{:S(2)}, u32[]{:S(2)}) %collective-permute-start.12) | collective-permute-done | bytes 800 | tf_op jit(solution)/shard_map/ppermute | solution.py:139
  225.5 8.0 %collective-permute-done.13 = bf16[512,704]{0,1:T(8,128)(2,1)} collective-permute-done((bf16[512,704]{0,1:T(8,128)(2,1)}, bf16[512,704]{0,1:T(8,128)(2,1)}, u32[]{:S(2)}, u32[]{:S(2)}) %collective-permute-start.13) | collective-permute-done | bytes 720928 | tf_op jit(solution)/shard_map/ppermute | solution.py:139
  233.5 2.6 pad_maximum_fusion.12
  242.5 33.0 %collective-permute-done.15 = bf16[512,704]{0,1:T(8,128)(2,1)S(1)} collective-permute-done((bf16[512,704]{0,1:T(8,128)(2,1)}, bf16[512,704]{0,1:T(8,128)(2,1)S(1)}, u32[]{:S(2)}, u32[]{:S(2)}) %collective-permute-start.15) | collective-permute-done | bytes 720928 | tf_op jit(solution)/shard_map/ppermute | solution.py:139
  279.9 14.4 %all-gather.6.cloned.1.call-done = bf16[1536,2048]{1,0:T(8,128)(2,1)} async-done(((bf16[192,2048]{1,0:T(8,128)(2,1)}), bf16[1536,2048]{1,0:T(8,128)(2,1)}) %all-gather.6.cloned.1.call-update) | async-done | bytes 6291472 | tf_op jit(solution)/shard_map/all_gather | solution.py:219
  295.8 7.7 fusion.240
  303.5 25.7 %collective-permute-done.17 = bf16[176,2048]{1,0:T(8,128)(2,1)S(1)} collective-permute-done((bf16[176,2048]{1,0:T(8,128)(2,1)}, bf16[176,2048]{1,0:T(8,128)(2,1)S(1)}, u32[]{:S(2)}, u32[]{:S(2)}) %collective-permute-start.17) | collective-permute-done | bytes 720928 | tf_op jit(solution)/shard_map/ppermute | solution.py:139
  332.0 6.5 multiply_convert_fusion.2
  338.6 5.9 convolution_convert_fusion.4
  344.5 18.6 %collective-permute-done.18 = bf16[2,176,2048]{2,1,0:T(8,128)(2,1)S(1)} collective-permute-done((bf16[2,176,2048]{2,1,0:T(8,128)(2,1)S(1)}, bf16[2,176,2048]{2,1,0:T(8,128)(2,1)S(1)}, u32[]{:S(2)}, u32[]{:S(2)}) %collective-permute-start.18) | collective-permute-done | bytes 1441824 | tf_op jit(solution)/shard_map/ppermute | solution.py:139
  363.6 3.0 copy-done.127
  366.6 9.0 %multiply_convert_fusion = (bf16[1536,704]{0,1:T(8,128)(2,1)}, bf16[1536,704]{0,1:T(8,128)(2,1)S(1)}) fusion(f32[1536,704]{0,1:T(8,128)S(1)} %copy-done.127, f32[1536,704]{0,1:T(8,128)} %get-tuple-element.228, bf16[1536,2048]{1,0:T(8,128)(2,1)S(1)} %bitcast.421, bf16[704,2048]{1,0:T(8,128)(2,1)S(1)} %bitcast.371), kind=kOutput, calls=%fused_computation.83 | convolution fusion | flops 4443242496 | bytes 22151168 | tf_op jit(solution)/shard_map/dot_general | solution.py:33
  375.7 5.1 fusion.241
  380.8 7.1 add_convert_fusion
  388.5 2.7 dynamic-slice_bitcast_fusion
  392.7 8.3 %convolution_convert_fusion.3 = bf16[2048,704]{0,1:T(8,128)(2,1)S(1)} fusion(bf16[1536,704]{0,1:T(8,128)(2,1)S(1)} %copy-done.125, bf16[1536,2048]{1,0:T(8,128)(2,1)} %all-gather.6.cloned.1.call-done), kind=kOutput, calls=%fused_computation.130 | convolution fusion | flops 4430626816 | bytes 11337728 | tf_op jit(solution)/shard_map/dot_general | solution.py:33
  405.0 7.0 convolution_convert_fusion
  412.0 9.9 %convolution_convert_fusion.2 = bf16[2048,704]{0,1:T(8,128)(2,1)} fusion(bf16[1536,704]{0,1:T(8,128)(2,1)} %get-tuple-element.81, bf16[1536,2048]{1,0:T(8,128)(2,1)} %all-gather.6.cloned.1.call-done), kind=kOutput, calls=%fused_computation.129 | convolution fusion | flops 4430626816 | bytes 11337728 | tf_op jit(solution)/shard_map/dot_general | solution.py:33
  421.9 33.1 %collective-permute-done.19 = bf16[1024,704]{0,1:T(8,128)(2,1)} collective-permute-done((bf16[1024,704]{0,1:T(8,128)(2,1)}, bf16[1024,704]{0,1:T(8,128)(2,1)}, u32[]{:S(2)}, u32[]{:S(2)}) %collective-permute-start.19) | collective-permute-done | bytes 1441824 | tf_op jit(solution)/shard_map/ppermute | solution.py:139
  455.0 3.1 add_convert_fusion.2
  458.2 3.0 fusion.104
  475.5 9.3 %collective-permute-done.21 = bf16[192,2048]{1,0:T(8,128)(2,1)S(1)} collective-permute-done((bf16[192,2048]{1,0:T(8,128)(2,1)S(1)}, bf16[192,2048]{1,0:T(8,128)(2,1)S(1)}, u32[]{:S(2)}, u32[]{:S(2)}) %collective-permute-start.21) | collective-permute-done | bytes 786464 | tf_op jit(solution)/shard_map/ppermute | solution.py:139
  489.7 2.7 copy.115
  495.0 10.4 %collective-permute-done.25 = bf16[176,2048]{1,0:T(8,128)(2,1)} collective-permute-done((bf16[176,2048]{1,0:T(8,128)(2,1)}, bf16[176,2048]{1,0:T(8,128)(2,1)}, u32[]{:S(2)}, u32[]{:S(2)}) %collective-permute-start.25) | collective-permute-done | bytes 720928 | tf_op jit(solution)/shard_map/ppermute | solution.py:139
  509.8 4.0 pad_maximum_fusion.1
  514.9 4.6 convolution_convert_fusion.5
  519.6 5.5 subtract_multiply_fusion
  535.0 5.2 fusion.101
  540.3 3.2 convolution_convert_fusion.6
  545.8 2.9 collective-permute-start.48
  562.9 17.4 %collective-permute-done.48 = bf16[512,704]{0,1:T(8,128)(2,1)} collective-permute-done((bf16[512,704]{0,1:T(8,128)(2,1)}, bf16[512,704]{0,1:T(8,128)(2,1)}, u32[]{:S(2)}, u32[]{:S(2)}) %collective-permute-start.48) | collective-permute-done | bytes 720928 | tf_op jit(solution)/shard_map/ppermute | solution.py:139
  582.4 2.5 select_bitcast_fusion.5
  594.2 4.5 collective-permute-done.29
  605.6 15.5 %collective-permute-done.34 = bf16[2,2,256,512]{3,2,1,0:T(8,128)(2,1)} collective-permute-done((bf16[2,2,256,512]{3,2,1,0:T(8,128)(2,1)}, bf16[2,2,256,512]{3,2,1,0:T(8,128)(2,1)}, u32[]{:S(2)}, u32[]{:S(2)}) %collective-permute-start.34) | collective-permute-done | bytes 1048608 | tf_op jit(solution)/shard_map/ppermute | solution.py:139
  623.6 18.2 %collective-permute-done.39 = bf16[2,2,256,512]{3,2,1,0:T(8,128)(2,1)} collective-permute-done((bf16[2,2,256,512]{3,2,1,0:T(8,128)(2,1)}, bf16[2,2,256,512]{3,2,1,0:T(8,128)(2,1)}, u32[]{:S(2)}, u32[]{:S(2)}) %collective-permute-start.39) | collective-permute-done | bytes 1048608 | tf_op jit(solution)/shard_map/ppermute | solution.py:139
  645.4 2.6 collective-permute-start.35
  664.8 4.4 collective-permute-done.30
  669.2 3.3 collective-permute-start.46
  674.7 28.1 %collective-permute-done.35 = bf16[2,256,512]{2,1,0:T(8,128)(2,1)} collective-permute-done((bf16[2,256,512]{2,1,0:T(8,128)(2,1)}, bf16[2,256,512]{2,1,0:T(8,128)(2,1)}, u32[]{:S(2)}, u32[]{:S(2)}) %collective-permute-start.35) | collective-permute-done | bytes 524320 | tf_op jit(solution)/shard_map/ppermute | solution.py:139
  704.0 8.8 %collective-permute-done.40 = bf16[2,256,512]{2,1,0:T(8,128)(2,1)S(1)} collective-permute-done((bf16[2,256,512]{2,1,0:T(8,128)(2,1)S(1)}, bf16[2,256,512]{2,1,0:T(8,128)(2,1)S(1)}, u32[]{:S(2)}, u32[]{:S(2)}) %collective-permute-start.40) | collective-permute-done | bytes 524320 | tf_op jit(solution)/shard_map/ppermute | solution.py:139
  715.1 3.3 collective-permute-done.31
  719.1 5.0 collective-permute-done.36
  724.7 4.9 collective-permute-done.41
  735.6 9.0 %collective-permute-done.47 = bf16[64,2048]{1,0:T(8,128)(2,1)S(1)} collective-permute-done((bf16[64,2048]{1,0:T(8,128)(2,1)S(1)}, bf16[64,2048]{1,0:T(8,128)(2,1)S(1)}, u32[]{:S(2)}, u32[]{:S(2)}) %collective-permute-start.47) | collective-permute-done | bytes 262176 | tf_op jit(solution)/shard_map/ppermute | solution.py:139
  754.6 3.4 copy.128
  758.0 3.4 copy.127
  768.4 5.4 fusion.9
  779.4 4.2 fusion.150
  (577 shorter events, 200.9 us)
Async XLA Ops:
  7.2 149.6 %all-gather.4.cloned.1.call-start = ((), (), s32[]{:S(2)}) async-start(), calls=%async_computation.2 | async-start | bytes 13369344 | tf_op jit(solution)/shard_map/all_gather | solution.py:275
  15.4 264.5 %all-gather.8.cloned.1.call-start = ((), (), s32[]{:S(2)}) async-start(), calls=%async_computation.4 | async-start | bytes 7077888 | tf_op jit(solution)/shard_map/all_gather | solution.py:219
  16.2 32.8 %collective-permute-start.5 = (bf16[64,2048]{1,0:T(8,128)(2,1)}, bf16[64,2048]{1,0:T(8,128)(2,1)S(1)}, u32[]{:S(2)}, u32[]{:S(2)}) collective-permute-start(bf16[64,2048]{1,0:T(8,128)(2,1)} %dynamic-slice_bitcast_fusion.17), channel_id=1, source_target_pairs={{0,4},{1,5},{2,6},{3,7},{4,0},{5,1},{6,2},{7,3},{8,12},{9,13},{10,... | collective-permute-start | bytes 786440 | tf_op jit(solution)/shard_map/ppermute | solution.py:139
  24.8 70.0 %collective-permute-start.4 = (bf16[512,704]{0,1:T(8,128)(2,1)}, bf16[512,704]{0,1:T(8,128)(2,1)}, u32[]{:S(2)}, u32[]{:S(2)}) collective-permute-start(bf16[512,704]{0,1:T(8,128)(2,1)} %fusion.142), channel_id=1, source_target_pairs={{0,1},{1,0},{2,3},{3,2},{4,5},{5,4},{6,7},{7,6},{8,9},{9,8},{10,11... | collective-permute-start | bytes 2162696 | tf_op jit(solution)/shard_map/ppermute | solution.py:139
  24.9 68.6 %collective-permute-start = (bf16[192,2048]{1,0:T(8,128)(2,1)S(1)}, bf16[192,2048]{1,0:T(8,128)(2,1)S(1)}, u32[]{:S(2)}, u32[]{:S(2)}) collective-permute-start(bf16[192,2048]{1,0:T(8,128)(2,1)S(1)} %bitcast.355), channel_id=1, source_target_pairs={{0,16},{1,17},{2,18},{3,19},{4,20},{5,21},{6,22},{7,23},{8,24},{9,... | collective-permute-start | bytes 2359304 | tf_op jit(solution)/shard_map/ppermute | solution.py:139
  26.4 23.6 %collective-permute-start.2 = (s32[1,192]{1,0:T(1,128)}, s32[1,192]{1,0:T(1,128)}, u32[]{:S(2)}, u32[]{:S(2)}) collective-permute-start(s32[1,192]{1,0:T(1,128)} %param.14), channel_id=1, source_target_pairs={{0,16},{1,17},{2,18},{3,19},{4,20},{5,21},{6,22},{7,23},{8,24},{9,... | collective-permute-start | bytes 2312 | tf_op jit(solution)/shard_map/ppermute | solution.py:139
  47.9 92.4 %copy-start.81 = (f32[1,2048]{1,0:T(1,128)}, f32[1,2048]{1,0:T(1,128)S(1)}, u32[]{:S(2)}) copy-start(f32[1,2048]{1,0:T(1,128)S(1)} %get-tuple-element.226) | copy-start | bytes 24580
  50.0 41.1 %collective-permute-start.6 = (bf16[2,64,2048]{2,1,0:T(8,128)(2,1)S(1)}, bf16[2,64,2048]{2,1,0:T(8,128)(2,1)}, u32[]{:S(2)}, u32[]{:S(2)}) collective-permute-start(bf16[2,64,2048]{2,1,0:T(8,128)(2,1)S(1)} %pad_maximum_fusion.19), channel_id=1, source_target_pairs={{0,8},{1,9},{2,10},{3,11},{4,12},{5,13},{6,14},{7,15},{8,0},{9,1},... | collective-permute-start | bytes 1572872 | tf_op jit(solution)/shard_map/ppermute | solution.py:139
  50.8 1.2 collective-permute-start.3
  93.4 42.1 %collective-permute-start.7 = (bf16[2,2,64,2048]{3,2,1,0:T(8,128)(2,1)}, bf16[2,2,64,2048]{3,2,1,0:T(8,128)(2,1)}, u32[]{:S(2)}, u32[]{:S(2)}) collective-permute-start(bf16[2,2,64,2048]{3,2,1,0:T(8,128)(2,1)} %pad_maximum_fusion.16), channel_id=1, source_target_pairs={{0,2},{1,3},{2,0},{3,1},{4,6},{5,7},{6,4},{7,5},{8,10},{9,11},{10,... | collective-permute-start | bytes 3145736 | tf_op jit(solution)/shard_map/ppermute | solution.py:139
  94.7 43.8 %collective-permute-start.1 = (bf16[384,2048]{1,0:T(8,128)(2,1)}, bf16[384,2048]{1,0:T(8,128)(2,1)}, u32[]{:S(2)}, u32[]{:S(2)}) collective-permute-start(bf16[384,2048]{1,0:T(8,128)(2,1)} %pad_maximum_fusion.7), channel_id=1, source_target_pairs={{0,1},{1,0},{2,3},{3,2},{4,5},{5,4},{6,7},{7,6},{8,9},{9,8},{10,11... | collective-permute-start | bytes 4718600 | tf_op jit(solution)/shard_map/ppermute | solution.py:139
  156.8 137.5 %all-gather.6.cloned.1.call-start = ((), (), s32[]{:S(2)}) async-start(), calls=%async_computation.3 | async-start | bytes 7077888 | tf_op jit(solution)/shard_map/all_gather | solution.py:219
  158.9 27.8 %collective-permute-start.8 = (bf16[512,704]{0,1:T(8,128)(2,1)S(1)}, bf16[512,704]{0,1:T(8,128)(2,1)}, u32[]{:S(2)}, u32[]{:S(2)}) collective-permute-start(bf16[512,704]{0,1:T(8,128)(2,1)S(1)} %bitcast.403), channel_id=1, source_target_pairs={{0,4},{1,5},{2,6},{3,7},{4,0},{5,1},{6,2},{7,3},{8,12},{9,13},{10,... | collective-permute-start | bytes 2162696 | tf_op jit(solution)/shard_map/ppermute | solution.py:139
  190.4 10.3 %collective-permute-start.9 = (bf16[384,2048]{1,0:T(8,128)(2,1)}, bf16[384,2048]{1,0:T(8,128)(2,1)}, u32[]{:S(2)}, u32[]{:S(2)}) collective-permute-start(bf16[384,2048]{1,0:T(8,128)(2,1)} %slice.125), channel_id=1, source_target_pairs={{0,1},{1,0},{2,3},{3,2},{4,5},{5,4},{6,7},{7,6},{8,9},{9,8},{10,11... | collective-permute-start | bytes 4718600 | tf_op jit(solution)/shard_map/ppermute | solution.py:139
  198.8 34.7 %collective-permute-start.13 = (bf16[512,704]{0,1:T(8,128)(2,1)}, bf16[512,704]{0,1:T(8,128)(2,1)}, u32[]{:S(2)}, u32[]{:S(2)}) collective-permute-start(bf16[512,704]{0,1:T(8,128)(2,1)} %bitcast.149), channel_id=1, source_target_pairs={{0,8},{1,9},{2,10},{3,11},{4,12},{5,13},{6,14},{7,15},{8,0},{9,1},... | collective-permute-start | bytes 2162696 | tf_op jit(solution)/shard_map/ppermute | solution.py:139
  205.4 30.7 %collective-permute-start.10 = (bf16[192,2048]{1,0:T(8,128)(2,1)}, bf16[192,2048]{1,0:T(8,128)(2,1)}, u32[]{:S(2)}, u32[]{:S(2)}) collective-permute-start(bf16[192,2048]{1,0:T(8,128)(2,1)} %slice.232), channel_id=1, source_target_pairs={{0,16},{1,17},{2,18},{3,19},{4,20},{5,21},{6,22},{7,23},{8,24},{9,... | collective-permute-start | bytes 2359304 | tf_op jit(solution)/shard_map/ppermute | solution.py:139
  206.9 1.2 collective-permute-start.11
  208.1 17.4 %collective-permute-start.12 = (f32[1,192]{1,0:T(1,128)S(1)}, f32[1,192]{1,0:T(1,128)S(1)}, u32[]{:S(2)}, u32[]{:S(2)}) collective-permute-start(f32[1,192]{1,0:T(1,128)S(1)} %slice.164), channel_id=1, source_target_pairs={{0,16},{1,17},{2,18},{3,19},{4,20},{5,21},{6,22},{7,23},{8,24},{9,... | collective-permute-start | bytes 2312 | tf_op jit(solution)/shard_map/ppermute | solution.py:139
  241.9 219.3 %reduce-scatter.3.cloned.1.call-start = ((), (), s32[]{:S(2)}) async-start(), calls=%async_computation.5 | async-start | bytes 7077888 | tf_op jit(solution)/shard_map/reduce_scatter | solution.py:222
  242.1 35.9 %collective-permute-start.14 = (bf16[1024,704]{0,1:T(8,128)(2,1)}, bf16[1024,704]{0,1:T(8,128)(2,1)S(1)}, u32[]{:S(2)}, u32[]{:S(2)}) collective-permute-start(bf16[1024,704]{0,1:T(8,128)(2,1)} %pad_maximum_fusion.12), channel_id=1, source_target_pairs={{0,2},{1,3},{2,0},{3,1},{4,6},{5,7},{6,4},{7,5},{8,10},{9,11},{10,... | collective-permute-start | bytes 4325384 | tf_op jit(solution)/shard_map/ppermute | solution.py:139
  242.5 33.0 %collective-permute-start.15 = (bf16[512,704]{0,1:T(8,128)(2,1)}, bf16[512,704]{0,1:T(8,128)(2,1)S(1)}, u32[]{:S(2)}, u32[]{:S(2)}) collective-permute-start(bf16[512,704]{0,1:T(8,128)(2,1)} %bitcast.375), channel_id=1, source_target_pairs={{0,8},{1,9},{2,10},{3,11},{4,12},{5,13},{6,14},{7,15},{8,0},{9,1},... | collective-permute-start | bytes 2162696 | tf_op jit(solution)/shard_map/ppermute | solution.py:139
  294.3 34.9 %collective-permute-start.17 = (bf16[176,2048]{1,0:T(8,128)(2,1)}, bf16[176,2048]{1,0:T(8,128)(2,1)S(1)}, u32[]{:S(2)}, u32[]{:S(2)}) collective-permute-start(bf16[176,2048]{1,0:T(8,128)(2,1)} %dynamic-slice_bitcast_fusion.6), channel_id=1, source_target_pairs={{0,8},{1,9},{2,10},{3,11},{4,12},{5,13},{6,14},{7,15},{8,0},{9,1},... | collective-permute-start | bytes 2162696 | tf_op jit(solution)/shard_map/ppermute | solution.py:139
  294.3 35.1 %collective-permute-start.16 = (bf16[1024,704]{0,1:T(8,128)(2,1)}, bf16[1024,704]{0,1:T(8,128)(2,1)S(1)}, u32[]{:S(2)}, u32[]{:S(2)}) collective-permute-start(bf16[1024,704]{0,1:T(8,128)(2,1)} %pad_maximum_fusion.13), channel_id=1, source_target_pairs={{0,2},{1,3},{2,0},{3,1},{4,6},{5,7},{6,4},{7,5},{8,10},{9,11},{10,... | collective-permute-start | bytes 4325384 | tf_op jit(solution)/shard_map/ppermute | solution.py:139
  329.7 33.4 %collective-permute-start.18 = (bf16[2,176,2048]{2,1,0:T(8,128)(2,1)S(1)}, bf16[2,176,2048]{2,1,0:T(8,128)(2,1)S(1)}, u32[]{:S(2)}, u32[]{:S(2)}) collective-permute-start(bf16[2,176,2048]{2,1,0:T(8,128)(2,1)S(1)} %pad_maximum_fusion.14), channel_id=1, source_target_pairs={{0,2},{1,3},{2,0},{3,1},{4,6},{5,7},{6,4},{7,5},{8,10},{9,11},{10,... | collective-permute-start | bytes 4325384 | tf_op jit(solution)/shard_map/ppermute | solution.py:139
  387.9 390.0 %reduce-scatter.5.cloned.1.call-start = ((), (), s32[]{:S(2)}) async-start(), calls=%async_computation.6 | async-start | bytes 7077888 | tf_op jit(solution)/shard_map/reduce_scatter | solution.py:222
  391.3 66.9 %collective-permute-start.20 = (bf16[2,176,2048]{2,1,0:T(8,128)(2,1)}, bf16[2,176,2048]{2,1,0:T(8,128)(2,1)}, u32[]{:S(2)}, u32[]{:S(2)}) collective-permute-start(bf16[2,176,2048]{2,1,0:T(8,128)(2,1)} %dynamic-slice_bitcast_fusion), channel_id=1, source_target_pairs={{0,2},{1,3},{2,0},{3,1},{4,6},{5,7},{6,4},{7,5},{8,10},{9,11},{10,... | collective-permute-start | bytes 4325384 | tf_op jit(solution)/shard_map/ppermute | solution.py:139
  403.9 51.1 %collective-permute-start.19 = (bf16[1024,704]{0,1:T(8,128)(2,1)}, bf16[1024,704]{0,1:T(8,128)(2,1)}, u32[]{:S(2)}, u32[]{:S(2)}) collective-permute-start(bf16[1024,704]{0,1:T(8,128)(2,1)} %slice.169), channel_id=1, source_target_pairs={{0,2},{1,3},{2,0},{3,1},{4,6},{5,7},{6,4},{7,5},{8,10},{9,11},{10,... | collective-permute-start | bytes 4325384 | tf_op jit(solution)/shard_map/ppermute | solution.py:139
  467.2 17.6 %collective-permute-start.21 = (bf16[192,2048]{1,0:T(8,128)(2,1)S(1)}, bf16[192,2048]{1,0:T(8,128)(2,1)S(1)}, u32[]{:S(2)}, u32[]{:S(2)}) collective-permute-start(bf16[192,2048]{1,0:T(8,128)(2,1)S(1)} %get-tuple-element.153), channel_id=1, source_target_pairs={{0,16},{1,17},{2,18},{3,19},{4,20},{5,21},{6,22},{7,23},{8,24},{9,... | collective-permute-start | bytes 2359304 | tf_op jit(solution)/shard_map/ppermute | solution.py:139
  471.6 36.1 %collective-permute-start.26 = (bf16[1024,704]{0,1:T(8,128)(2,1)}, bf16[1024,704]{0,1:T(8,128)(2,1)}, u32[]{:S(2)}, u32[]{:S(2)}) collective-permute-start(bf16[1024,704]{0,1:T(8,128)(2,1)} %slice.138), channel_id=1, source_target_pairs={{0,2},{1,3},{2,0},{3,1},{4,6},{5,7},{6,4},{7,5},{8,10},{9,11},{10,... | collective-permute-start | bytes 4325384 | tf_op jit(solution)/shard_map/ppermute | solution.py:139
  474.0 31.5 %collective-permute-start.25 = (bf16[176,2048]{1,0:T(8,128)(2,1)}, bf16[176,2048]{1,0:T(8,128)(2,1)}, u32[]{:S(2)}, u32[]{:S(2)}) collective-permute-start(bf16[176,2048]{1,0:T(8,128)(2,1)} %dynamic-slice_bitcast_fusion.5), channel_id=1, source_target_pairs={{0,8},{1,9},{2,10},{3,11},{4,12},{5,13},{6,14},{7,15},{8,0},{9,1},... | collective-permute-start | bytes 2162696 | tf_op jit(solution)/shard_map/ppermute | solution.py:139
  486.1 23.6 %collective-permute-start.22 = (bf16[384,2048]{1,0:T(8,128)(2,1)}, bf16[384,2048]{1,0:T(8,128)(2,1)}, u32[]{:S(2)}, u32[]{:S(2)}) collective-permute-start(bf16[384,2048]{1,0:T(8,128)(2,1)} %pad_maximum_fusion.9), channel_id=1, source_target_pairs={{0,1},{1,0},{2,3},{3,2},{4,5},{5,4},{6,7},{7,6},{8,9},{9,8},{10,11... | collective-permute-start | bytes 4718600 | tf_op jit(solution)/shard_map/ppermute | solution.py:139
  486.2 7.6 collective-permute-start.23
  493.8 1.2 collective-permute-start.24
  514.7 42.9 %collective-permute-start.52 = (bf16[512,704]{0,1:T(8,128)(2,1)}, bf16[512,704]{0,1:T(8,128)(2,1)}, u32[]{:S(2)}, u32[]{:S(2)}) collective-permute-start(bf16[512,704]{0,1:T(8,128)(2,1)} %slice.149), channel_id=1, source_target_pairs={{0,8},{1,9},{2,10},{3,11},{4,12},{5,13},{6,14},{7,15},{8,0},{9,1},... | collective-permute-start | bytes 2162696 | tf_op jit(solution)/shard_map/ppermute | solution.py:139
  543.4 38.9 %collective-permute-start.56 = (bf16[176,2048]{1,0:T(8,128)(2,1)}, bf16[176,2048]{1,0:T(8,128)(2,1)}, u32[]{:S(2)}, u32[]{:S(2)}) collective-permute-start(bf16[176,2048]{1,0:T(8,128)(2,1)} %fusion.133), channel_id=1, source_target_pairs={{0,16},{1,17},{2,18},{3,19},{4,20},{5,21},{6,22},{7,23},{8,24},{9,... | collective-permute-start | bytes 2162696 | tf_op jit(solution)/shard_map/ppermute | solution.py:139
  545.8 34.5 %collective-permute-start.48 = (bf16[512,704]{0,1:T(8,128)(2,1)}, bf16[512,704]{0,1:T(8,128)(2,1)}, u32[]{:S(2)}, u32[]{:S(2)}) collective-permute-start(bf16[512,704]{0,1:T(8,128)(2,1)} %slice.147), channel_id=1, source_target_pairs={{0,8},{1,9},{2,10},{3,11},{4,12},{5,13},{6,14},{7,15},{8,0},{9,1},... | collective-permute-start | bytes 2162696 | tf_op jit(solution)/shard_map/ppermute | solution.py:139
  549.8 51.3 %collective-permute-start.44 = (bf16[2,2,64,2048]{3,2,1,0:T(8,128)(2,1)}, bf16[2,2,64,2048]{3,2,1,0:T(8,128)(2,1)}, u32[]{:S(2)}, u32[]{:S(2)}) collective-permute-start(bf16[2,2,64,2048]{3,2,1,0:T(8,128)(2,1)} %dynamic-slice_bitcast_fusion.1), channel_id=1, source_target_pairs={{0,2},{1,3},{2,0},{3,1},{4,6},{5,7},{6,4},{7,5},{8,10},{9,11},{10,... | collective-permute-start | bytes 3145736 | tf_op jit(solution)/shard_map/ppermute | solution.py:139
  551.4 47.3 %collective-permute-start.29 = (bf16[2,2,256,512]{3,2,1,0:T(8,128)(2,1)}, bf16[2,2,256,512]{3,2,1,0:T(8,128)(2,1)}, u32[]{:S(2)}, u32[]{:S(2)}) collective-permute-start(bf16[2,2,256,512]{3,2,1,0:T(8,128)(2,1)} %dynamic-slice_bitcast_fusion.4), channel_id=1, source_target_pairs={{0,2},{1,3},{2,0},{3,1},{4,6},{5,7},{6,4},{7,5},{8,10},{9,11},{10,... | collective-permute-start | bytes 3145736 | tf_op jit(solution)/shard_map/ppermute | solution.py:139
  557.6 63.6 %collective-permute-start.34 = (bf16[2,2,256,512]{3,2,1,0:T(8,128)(2,1)}, bf16[2,2,256,512]{3,2,1,0:T(8,128)(2,1)}, u32[]{:S(2)}, u32[]{:S(2)}) collective-permute-start(bf16[2,2,256,512]{3,2,1,0:T(8,128)(2,1)} %dynamic-slice_bitcast_fusion.3), channel_id=1, source_target_pairs={{0,2},{1,3},{2,0},{3,1},{4,6},{5,7},{6,4},{7,5},{8,10},{9,11},{10,... | collective-permute-start | bytes 3145736 | tf_op jit(solution)/shard_map/ppermute | solution.py:139
  580.3 61.5 %collective-permute-start.39 = (bf16[2,2,256,512]{3,2,1,0:T(8,128)(2,1)}, bf16[2,2,256,512]{3,2,1,0:T(8,128)(2,1)}, u32[]{:S(2)}, u32[]{:S(2)}) collective-permute-start(bf16[2,2,256,512]{3,2,1,0:T(8,128)(2,1)} %dynamic-slice_bitcast_fusion.2), channel_id=1, source_target_pairs={{0,2},{1,3},{2,0},{3,1},{4,6},{5,7},{6,4},{7,5},{8,10},{9,11},{10,... | collective-permute-start | bytes 3145736 | tf_op jit(solution)/shard_map/ppermute | solution.py:139
  582.3 77.1 %collective-permute-start.27 = (bf16[384,2048]{1,0:T(8,128)(2,1)}, bf16[384,2048]{1,0:T(8,128)(2,1)}, u32[]{:S(2)}, u32[]{:S(2)}) collective-permute-start(bf16[384,2048]{1,0:T(8,128)(2,1)} %slice.172), channel_id=1, source_target_pairs={{0,1},{1,0},{2,3},{3,2},{4,5},{5,4},{6,7},{7,6},{8,9},{9,8},{10,11... | collective-permute-start | bytes 4718600 | tf_op jit(solution)/shard_map/ppermute | solution.py:139
  598.7 46.7 %collective-permute-start.53 = (bf16[256,704]{0,1:T(8,128)(2,1)S(1)}, bf16[256,704]{0,1:T(8,128)(2,1)S(1)}, u32[]{:S(2)}, u32[]{:S(2)}) collective-permute-start(bf16[256,704]{0,1:T(8,128)(2,1)S(1)} %bitcast.404), channel_id=1, source_target_pairs={{0,4},{1,5},{2,6},{3,7},{4,0},{5,1},{6,2},{7,3},{8,12},{9,13},{10,... | collective-permute-start | bytes 1081352 | tf_op jit(solution)/shard_map/ppermute | solution.py:139
  601.1 52.3 %collective-permute-start.49 = (bf16[256,704]{0,1:T(8,128)(2,1)}, bf16[256,704]{0,1:T(8,128)(2,1)}, u32[]{:S(2)}, u32[]{:S(2)}) collective-permute-start(bf16[256,704]{0,1:T(8,128)(2,1)} %bitcast.351), channel_id=1, source_target_pairs={{0,4},{1,5},{2,6},{3,7},{4,0},{5,1},{6,2},{7,3},{8,12},{9,13},{10,... | collective-permute-start | bytes 1081352 | tf_op jit(solution)/shard_map/ppermute | solution.py:139
  621.2 40.9 %collective-permute-start.45 = (bf16[2,64,2048]{2,1,0:T(8,128)(2,1)}, bf16[2,64,2048]{2,1,0:T(8,128)(2,1)}, u32[]{:S(2)}, u32[]{:S(2)}) collective-permute-start(bf16[2,64,2048]{2,1,0:T(8,128)(2,1)} %dynamic-slice_bitcast_fusion.7), channel_id=1, source_target_pairs={{0,8},{1,9},{2,10},{3,11},{4,12},{5,13},{6,14},{7,15},{8,0},{9,1},... | collective-permute-start | bytes 1572872 | tf_op jit(solution)/shard_map/ppermute | solution.py:139
  641.8 27.4 %collective-permute-start.30 = (bf16[2,256,512]{2,1,0:T(8,128)(2,1)}, bf16[2,256,512]{2,1,0:T(8,128)(2,1)}, u32[]{:S(2)}, u32[]{:S(2)}) collective-permute-start(bf16[2,256,512]{2,1,0:T(8,128)(2,1)} %dynamic-slice_bitcast_fusion.10), channel_id=1, source_target_pairs={{0,8},{1,9},{2,10},{3,11},{4,12},{5,13},{6,14},{7,15},{8,0},{9,1},... | collective-permute-start | bytes 1572872 | tf_op jit(solution)/shard_map/ppermute | solution.py:139
  645.4 57.4 %collective-permute-start.35 = (bf16[2,256,512]{2,1,0:T(8,128)(2,1)}, bf16[2,256,512]{2,1,0:T(8,128)(2,1)}, u32[]{:S(2)}, u32[]{:S(2)}) collective-permute-start(bf16[2,256,512]{2,1,0:T(8,128)(2,1)} %dynamic-slice_bitcast_fusion.9), channel_id=1, source_target_pairs={{0,8},{1,9},{2,10},{3,11},{4,12},{5,13},{6,14},{7,15},{8,0},{9,1},... | collective-permute-start | bytes 1572872 | tf_op jit(solution)/shard_map/ppermute | solution.py:139
  653.4 3.4 collective-permute-start.54
  656.8 2.1 collective-permute-start.50
  658.9 53.9 %collective-permute-start.40 = (bf16[2,256,512]{2,1,0:T(8,128)(2,1)S(1)}, bf16[2,256,512]{2,1,0:T(8,128)(2,1)S(1)}, u32[]{:S(2)}, u32[]{:S(2)}) collective-permute-start(bf16[2,256,512]{2,1,0:T(8,128)(2,1)S(1)} %copy-done.78), channel_id=1, source_target_pairs={{0,8},{1,9},{2,10},{3,11},{4,12},{5,13},{6,14},{7,15},{8,0},{9,1},... | collective-permute-start | bytes 1572872 | tf_op jit(solution)/shard_map/ppermute | solution.py:139
  659.4 87.5 %collective-permute-start.55 = (bf16[2,2,128,704]{2,3,1,0:T(8,128)(2,1)S(1)}, bf16[2,2,128,704]{2,3,1,0:T(8,128)(2,1)S(1)}, u32[]{:S(2)}, u32[]{:S(2)}) collective-permute-start(bf16[2,2,128,704]{2,3,1,0:T(8,128)(2,1)S(1)} %pad_maximum_fusion.18), channel_id=1, source_target_pairs={{0,16},{1,17},{2,18},{3,19},{4,20},{5,21},{6,22},{7,23},{8,24},{9,... | collective-permute-start | bytes 2162696 | tf_op jit(solution)/shard_map/ppermute | solution.py:139
  662.0 83.2 %copy-start.9 = (f32[384,2048]{1,0:T(8,128)}, f32[384,2048]{1,0:T(8,128)S(1)}, u32[]{:S(2)}) copy-start(f32[384,2048]{1,0:T(8,128)S(1)} %convert_add_fusion) | copy-start | bytes 9437188
  662.0 87.0 %collective-permute-start.51 = (bf16[2,2,128,704]{2,3,1,0:T(8,128)(2,1)S(1)}, bf16[2,2,128,704]{2,3,1,0:T(8,128)(2,1)S(1)}, u32[]{:S(2)}, u32[]{:S(2)}) collective-permute-start(bf16[2,2,128,704]{2,3,1,0:T(8,128)(2,1)S(1)} %pad_maximum_fusion.17), channel_id=1, source_target_pairs={{0,16},{1,17},{2,18},{3,19},{4,20},{5,21},{6,22},{7,23},{8,24},{9,... | collective-permute-start | bytes 2162696 | tf_op jit(solution)/shard_map/ppermute | solution.py:139
  669.2 43.8 %collective-permute-start.46 = (bf16[64,2048]{1,0:T(8,128)(2,1)S(1)}, bf16[64,2048]{1,0:T(8,128)(2,1)S(1)}, u32[]{:S(2)}, u32[]{:S(2)}) collective-permute-start(bf16[64,2048]{1,0:T(8,128)(2,1)S(1)} %dynamic-slice_bitcast_fusion.13), channel_id=1, source_target_pairs={{0,4},{1,5},{2,6},{3,7},{4,0},{5,1},{6,2},{7,3},{8,12},{9,13},{10,... | collective-permute-start | bytes 786440 | tf_op jit(solution)/shard_map/ppermute | solution.py:139
  702.8 15.6 %collective-permute-start.31 = (bf16[256,512]{1,0:T(8,128)(2,1)S(1)}, bf16[256,512]{1,0:T(8,128)(2,1)S(1)}, u32[]{:S(2)}, u32[]{:S(2)}) collective-permute-start(bf16[256,512]{1,0:T(8,128)(2,1)S(1)} %dynamic-slice_bitcast_fusion.16), channel_id=1, source_target_pairs={{0,4},{1,5},{2,6},{3,7},{4,0},{5,1},{6,2},{7,3},{8,12},{9,13},{10,... | collective-permute-start | bytes 786440 | tf_op jit(solution)/shard_map/ppermute | solution.py:139
  712.8 11.2 %collective-permute-start.36 = (bf16[256,512]{1,0:T(8,128)(2,1)S(1)}, bf16[256,512]{1,0:T(8,128)(2,1)S(1)}, u32[]{:S(2)}, u32[]{:S(2)}) collective-permute-start(bf16[256,512]{1,0:T(8,128)(2,1)S(1)} %dynamic-slice_bitcast_fusion.15), channel_id=1, source_target_pairs={{0,4},{1,5},{2,6},{3,7},{4,0},{5,1},{6,2},{7,3},{8,12},{9,13},{10,... | collective-permute-start | bytes 786440 | tf_op jit(solution)/shard_map/ppermute | solution.py:139
  713.0 16.6 %collective-permute-start.41 = (bf16[256,512]{1,0:T(8,128)(2,1)S(1)}, bf16[256,512]{1,0:T(8,128)(2,1)S(1)}, u32[]{:S(2)}, u32[]{:S(2)}) collective-permute-start(bf16[256,512]{1,0:T(8,128)(2,1)S(1)} %dynamic-slice_bitcast_fusion.14), channel_id=1, source_target_pairs={{0,4},{1,5},{2,6},{3,7},{4,0},{5,1},{6,2},{7,3},{8,12},{9,13},{10,... | collective-permute-start | bytes 786440 | tf_op jit(solution)/shard_map/ppermute | solution.py:139
  718.4 57.8 %collective-permute-start.28 = (bf16[192,2048]{1,0:T(8,128)(2,1)}, bf16[192,2048]{1,0:T(8,128)(2,1)S(1)}, u32[]{:S(2)}, u32[]{:S(2)}) collective-permute-start(bf16[192,2048]{1,0:T(8,128)(2,1)} %slice.231), channel_id=1, source_target_pairs={{0,16},{1,17},{2,18},{3,19},{4,20},{5,21},{6,22},{7,23},{8,24},{9,... | collective-permute-start | bytes 2359304 | tf_op jit(solution)/shard_map/ppermute | solution.py:139
  724.0 20.6 %collective-permute-start.47 = (bf16[64,2048]{1,0:T(8,128)(2,1)S(1)}, bf16[64,2048]{1,0:T(8,128)(2,1)S(1)}, u32[]{:S(2)}, u32[]{:S(2)}) collective-permute-start(bf16[64,2048]{1,0:T(8,128)(2,1)S(1)} %fusion.156), channel_id=1, source_target_pairs={{0,16},{1,17},{2,18},{3,19},{4,20},{5,21},{6,22},{7,23},{8,24},{9,... | collective-permute-start | bytes 786440 | tf_op jit(solution)/shard_map/ppermute | solution.py:139
  729.5 1.3 collective-permute-start.32
  730.9 1.3 collective-permute-start.37
  732.2 1.3 collective-permute-start.42
  733.6 28.3 %collective-permute-start.33 = (bf16[2,128,512]{2,1,0:T(8,128)(2,1)}, bf16[2,128,512]{2,1,0:T(8,128)(2,1)}, u32[]{:S(2)}, u32[]{:S(2)}) collective-permute-start(bf16[2,128,512]{2,1,0:T(8,128)(2,1)} %pad_maximum_fusion.24), channel_id=1, source_target_pairs={{0,16},{1,17},{2,18},{3,19},{4,20},{5,21},{6,22},{7,23},{8,24},{9,... | collective-permute-start | bytes 786440 | tf_op jit(solution)/shard_map/ppermute | solution.py:139
  744.6 18.7 %collective-permute-start.38 = (bf16[2,128,512]{2,1,0:T(8,128)(2,1)}, bf16[2,128,512]{2,1,0:T(8,128)(2,1)}, u32[]{:S(2)}, u32[]{:S(2)}) collective-permute-start(bf16[2,128,512]{2,1,0:T(8,128)(2,1)} %pad_maximum_fusion.25), channel_id=1, source_target_pairs={{0,16},{1,17},{2,18},{3,19},{4,20},{5,21},{6,22},{7,23},{8,24},{9,... | collective-permute-start | bytes 786440 | tf_op jit(solution)/shard_map/ppermute | solution.py:139
  747.0 17.9 %collective-permute-start.43 = (bf16[2,128,512]{2,1,0:T(8,128)(2,1)}, bf16[2,128,512]{2,1,0:T(8,128)(2,1)}, u32[]{:S(2)}, u32[]{:S(2)}) collective-permute-start(bf16[2,128,512]{2,1,0:T(8,128)(2,1)} %pad_maximum_fusion.26), channel_id=1, source_target_pairs={{0,16},{1,17},{2,18},{3,19},{4,20},{5,21},{6,22},{7,23},{8,24},{9,... | collective-permute-start | bytes 786440 | tf_op jit(solution)/shard_map/ppermute | solution.py:139
  (136 other events, 1109.1 us)
Sparse Core Ops, SparseCore 0:
  15.5 141.2 all-gather.3
  158.4 45.8 all-gather.7
  242.0 52.2 all-gather.5
  388.0 67.4 reduce-scatter.2
  555.3 125.6 reduce-scatter.4

commit v3 on v2

--- a/solution.py
+++ b/solution.py
@@ -118,6 +118,7 @@
         self.reps, self.shards = reps, shards
         self.chips = shards // CORES
         self.hi = self.chips // 4
+        self.length = self.chips // 2
         self.r = lax.axis_index("rep")
         self.s = lax.axis_index("shard")
         self.c = self.s % CORES
@@ -127,7 +128,7 @@
         self.his = [("shard", 8 << k) for k in range(self.hi.bit_length() - 1)]
         self.rep_bits = [("rep", 1 << k) for k in range(reps.bit_length() - 1)]
         self.mixers = self.rep_bits + [self.core]
-        self.feeders = self.rep_bits + [self.lo, self.core]
+        self.feeders = self.rep_bits + [self.low, self.core]
 
     def bit(self, which):
         axis, value = which
@@ -157,6 +158,12 @@
         other = self.swap(self.pick(value, which, axis, True), which)
         return (self.pick(value, which, axis).astype(F32) + other.astype(F32)).astype(BF16)
 
+    def begin(self, value, which, axis):
+        return (self.pick(value, which, axis), self.swap(self.pick(value, which, axis, True), which))
+
+    def end(self, own, other):
+        return (own.astype(F32) + other.astype(F32)).astype(BF16)
+
     def extend(self, value, which):
         return jnp.concatenate([value, self.swap(value, which)], axis=0)
 
@@ -167,22 +174,20 @@
 
     def block_order(self, value, back=False):
         place = jnp.arange(self.chips, dtype=jnp.int32)
-        here = self.s // CORES
+        here = self.s // CORES & ~1
         if back:
-            other = place ^ (here & ~2)
-            source = (other & 1) * (2 * self.hi) + (other >> 1)
-        else:
-            chip = (place % (2 * self.hi)) * 2 + place // (2 * self.hi)
-            source = chip ^ (here & ~2)
-        return move_blocks(source, value)
+            other = place ^ here
+            return move_blocks(((other // 2 % 2) * self.hi + other // 4) * 2 + place % 2, value)
+        hi, lo = place // 2 % self.hi, place // (2 * self.hi)
+        return move_blocks((hi * 4 + lo * 2 + place % 2) ^ here, value)
 
     def gather_members(self, value, bits):
         for which in bits:
             value = jnp.concatenate([value, self.swap(value, which)], axis=0)
         return value
 
-    def sum_members(self, partial, bits):
-        wire, total = partial.dtype, partial
+    def sum_members(self, partial, bits, wire=None):
+        wire, total = wire or partial.dtype, partial
         for which in bits[::-1]:
             half = total.shape[0] // 2
             total = total[:half].astype(F32) + self.swap(total[half:].astype(wire), which).astype(F32)
@@ -274,18 +279,18 @@
     picked = picked.reshape(3, rows, CORES, channels).transpose(1, 2, 0, 3).reshape(rows, -1)
     mix_all = lax.all_gather(picked, "shard", axis=0, tiled=True)
 
-    def unit_source(core):
-        def source(position):
-            hi, low, inner = position // (2 * slim), position % (2 * slim) // slim, position % slim
-            return hi * (units // (2 * at.hi)) + ((low * CORES + core) * reps + at.r) * slim + inner
-
-        return source
-
     pair_rows = jnp.concatenate([ffn_gate_weight, ffn_up_weight])
-    strip = units // (2 * at.hi)
-    strips = [pair_rows[:, k * strip : (k + 1) * strip] for k in range(2 * at.hi)]
-    pair_lines = jnp.concatenate([jnp.concatenate(strips[k::2], axis=1) for k in range(2)])
-    pick_units = lambda core: matmul(pair_lines, chooser(units // 2, part, unit_source(core)), (1, 0), BF16)
+
+    def pick_units(core):
+        def column(low):
+            def source(position):
+                line, inner = position // slim, position % slim
+                return (((line * 2 + low) * CORES + core) * reps + at.r) * slim + inner
+
+            return source
+
+        return jnp.concatenate([matmul(pair_rows, chooser(units, part, column(low)), (1, 0), BF16) for low in range(2)])
+
     kept, given = pick_units(at.c), pick_units(1 - at.c)
 
     grad_out = cotangent[0]
@@ -294,20 +299,26 @@
     starts = jnp.zeros((count, 1), F32)
     same = jnp.concatenate([starts, (segments[:, 1:] == segments[:, :-1]).astype(F32)], axis=1)
     same = same.reshape(count * length, 1)
-    out_rows = at.join(at.join_his(at.join(at.own_rep(out_weight), at.lo)), at.low, 2).reshape(channels, width)
-    gains = lax.all_gather(jnp.stack([norm_gain, mixer_gain, ffn_gain]), "shard", axis=1, tiled=True).astype(F32)
+    out_lines = at.join_his(at.own_rep(out_weight))
+    out_lines, own_gains = fence(out_lines, jnp.stack([norm_gain, mixer_gain, ffn_gain]))
+    out_rows = at.join(at.join(out_lines, at.lo, 1), at.low, 2).reshape(channels, width)
+    gains = lax.all_gather(own_gains, "shard", axis=1, tiled=True).astype(F32)
     gain_one, gain_two, gain_three = gains[0], gains[1], gains[2]
     gain_grid = gain_two.reshape(at.chips, CORES, reps, small)
     gain_mix = lax.dynamic_index_in_dim(lax.dynamic_index_in_dim(gain_grid, at.c, 1, keepdims=False), at.r, 1, keepdims=False).reshape(-1)
     normed = (normalize(all_tokens.astype(F32))[0] * gain_one).astype(BF16)
     lines = lambda value: value.reshape(2 * CORES, rows, part)
     chip = at.merge(lines(kept), lines(at.swap(given, at.core)), at.core, 1).reshape(2, CORES * chip_rows, part)
-    mix_all, normed, same, chip, out_rows, grad_out_sent, own_down = fence(
-        mix_all, normed, same, chip, out_rows, grad_out, at.own_rep(ffn_down_weight)
+    own_pair = at.trade(chip, at.low, 0)
+    mix_all, normed, same, own_pair, out_rows, grad_out_sent, own_down = fence(
+        mix_all, normed, same, own_pair, out_rows, grad_out, at.own_rep(ffn_down_weight)
     )
 
     all_grad_out = at.gather_group(grad_out_sent)
-    own_pair = at.trade(chip, at.lo, 0)
+    pair_grid = own_pair.reshape(2, 2, chip_rows, part)
+    gate_half, up_half = pair_grid[:, 0].reshape(-1, part), pair_grid[:, 1].reshape(-1, part)
+    for which in at.his:
+        gate_half = at.extend(gate_half, which)
     mix_weight = lax.dynamic_slice_in_dim(mix_all, at.c * (3 * channels), 3 * channels, 1)
     pre = matmul(normed, mix_weight, (1, 0))
     input_pre, forget_pre, gate_pre = (pre[:, k * channels : (k + 1) * channels] for k in range(3))
@@ -318,70 +329,74 @@
     gate_act, gate_slope = swish_pair(gate_pre)
     mixed_raw = (state * gain_mix * gate_act).astype(BF16)
     squares = jnp.sum(state * state, axis=1).reshape(count, length)
-    out_part, squares, own_pair = fence(matmul(mixed_raw, out_rows, (1, 0), BF16), squares, own_pair)
-
-    pair_grid = own_pair.reshape(2, 2, chip_rows, part)
-    gate_half, up_half = pair_grid[:, 0].reshape(-1, part), pair_grid[:, 1].reshape(-1, part)
+    out_part, squares, gate_half, up_half = fence(matmul(mixed_raw, out_rows, (1, 0), BF16), squares, gate_half, up_half)
+
+    gate_columns = at.extend(gate_half, at.lo)
     for which in at.his:
-        gate_half = at.extend(gate_half, which)
+        up_half = at.extend(up_half, which)
     square_sum = at.sum_members(squares, at.mixers)
     branch_sum = at.sum_members(out_part, at.mixers)
-    branch_sum, square_sum, gate_half, up_half = fence(branch_sum, square_sum, gate_half, up_half)
-
-    gate_columns = at.extend(gate_half, at.low)
-    for which in at.his:
-        up_half = at.extend(up_half, which)
+    branch_sum, square_sum, gate_columns, up_half, own_down = fence(branch_sum, square_sum, gate_columns, up_half, own_down)
+
+    up_columns = at.extend(up_half, at.lo)
+    down_lines = at.join_his(own_down)
     state_scale = lax.rsqrt(square_sum / width + EPSILON)
     branch = branch_sum * state_scale.reshape(length, 1)
     resid = inputs + branch
     scaled_mid, scale_mid = normalize(resid)
     ffn_in = at.gather_group(at.block_order((scaled_mid * gain_three).astype(BF16)))
-    ffn_in, gate_columns, up_half, own_down, all_grad_out = fence(ffn_in, gate_columns, up_half, own_down, all_grad_out)
-    up_columns = at.extend(up_half, at.low)
-    down_lines = at.join_his(own_down)
+    ffn_in, up_columns, down_lines, all_grad_out = fence(ffn_in, up_columns, down_lines, all_grad_out)
+    down_rows = at.join(down_lines, at.lo, 1).reshape(part, width)
     ffn_gate = matmul(ffn_in, gate_columns, (1, 0))
-    ffn_gate, up_columns, down_lines, ffn_in = fence(ffn_gate, up_columns, down_lines, ffn_in)
-    down_rows = at.join(down_lines, at.low, 1).reshape(part, width)
     ffn_up = matmul(ffn_in, up_columns, (1, 0))
     ffn_act, ffn_slope = swish_pair(ffn_gate)
     hidden = (ffn_act * ffn_up).astype(BF16)
     down_cut = matmul(hidden, all_grad_out, (0, 0), BF16)
     down_rows, down_cut, hidden = fence(down_rows, down_cut, hidden)
-    down_grid = down_cut.reshape(at.hi, 2, -1, width)
-    down_line = at.reduce(down_grid, at.low, 1)
     grad_hidden = matmul(all_grad_out, down_rows, (1, 1))
     grad_fgate = (grad_hidden * ffn_up * ffn_slope).astype(BF16)
     grad_fup = (grad_hidden * ffn_act).astype(BF16)
     grad_cut = (matmul(grad_fgate, gate_columns, (1, 1)) + matmul(grad_fup, up_columns, (1, 1))).astype(BF16)
-    grad_cut, grad_fgate, grad_fup = fence(grad_cut, grad_fgate, grad_fup)
+    grad_cut, grad_fgate, grad_fup, down_cut = fence(grad_cut, grad_fgate, grad_fup, down_cut)
 
     grad_ffn_in = at.sum_group(grad_cut)
-    gate_cut = matmul(ffn_in, grad_fgate, (0, 0), BF16)
+    down_line = at.reduce(down_cut.reshape(at.hi, 2, -1, width), at.lo, 1)
+    gate_line = at.fold(matmul(ffn_in, grad_fgate, (0, 0), BF16), at.lo)
     up_cut = matmul(ffn_in, grad_fup, (0, 0), BF16)
     ffn_part = matmul(hidden, down_rows, (1, 0), BF16)
-    gate_line = at.fold(gate_cut, at.low)
-    grad_ffn_in, gate_line, down_line, ffn_part, up_cut = fence(grad_ffn_in, gate_line, down_line, ffn_part, up_cut)
-    up_line = at.fold(up_cut, at.low)
+    down_line, ffn_part, up_cut = fence(down_line, ffn_part, up_cut)
     down_own = at.reduce_his(down_line)
+    grad_ffn_in, gate_line, down_own, ffn_part, up_cut = fence(grad_ffn_in, gate_line, down_own, ffn_part, up_cut)
+
+    def fold_begin(lines, which):
+        half = lines.shape[0] // 2
+        return (lines[:half], at.swap(lines[half:], which))
+
+    def fold_rest(lines):
+        for which in at.his[-2::-1]:
+            lines = at.fold(lines, which)
+        return lines
+
+    mates = lambda lines: at.trade(lines.reshape(2, chip_rows, part), at.low, 0)
+    cores = lambda sets: at.trade(sets.reshape(-1, CORES, rows, sets.shape[-1]), at.core, 1)
+    up_line = at.fold(up_cut, at.lo)
+    ffn_out = at.sum_group(ffn_part)
     grad_ffn_in = at.block_order(grad_ffn_in.astype(BF16), True).astype(F32)
     grad_resid = grad_out.astype(F32) + norm_back(grad_ffn_in * gain_three, scaled_mid, scale_mid)
     grad_branch_own = grad_resid.astype(BF16)
     inner_own = jnp.mean(grad_branch_own.astype(F32) * branch, axis=1)
     row_facts = at.gather_members(jnp.stack([state_scale.reshape(length), inner_own])[None], at.mixers)
     grad_branch = at.gather_members(grad_branch_own, at.mixers)
-    grad_branch, row_facts, down_own, up_line, ffn_part, gate_line = fence(grad_branch, row_facts, down_own, up_line, ffn_part, gate_line)
-
+    grad_branch, row_facts, up_line, gate_line = fence(grad_branch, row_facts, up_line, gate_line)
+
+    gate_hi = fold_rest(at.end(*fold_begin(gate_line, at.his[-1])))
     all_scale = row_facts[:, 0].reshape(count * length, 1)
     all_inner = row_facts[:, 1].reshape(count * length, 1)
     state_scaled = state * all_scale
     mixed = (state_scaled * gain_mix * gate_act).astype(BF16)
     weighted = matmul(grad_branch, out_rows, (1, 1)) * gain_mix
-
-    def plane_grad(left, right, own_rows):
-        cut = matmul(left, right, (0, 0), BF16).reshape(at.hi, 2, 2, own_rows, -1)
-        return at.reduce(at.reduce_his(at.reduce(cut, at.low, 2)), at.lo, 0)
-
-    out_own = plane_grad(mixed, grad_branch, small)
+    plane = lambda cut: cut.reshape(at.hi, 2, 2, -1, cut.shape[1])
+    out_keep, out_other = at.begin(plane(matmul(mixed, grad_branch, (0, 0), BF16)), at.low, 2)
     grad_gate_pre = (weighted * state_scaled * gate_slope).astype(BF16)
     grad_state = all_scale * (weighted * gate_act - state_scaled * all_inner)
     carried = run_scan(scan_backward_kernel, "scan_backward", count, length, decay, grad_state)
@@ -390,22 +405,42 @@
     grad_forget = carried * previous * same - carried * input_act
     grad_input_pre = (carried * (1.0 - forget) * input_slope).astype(BF16)
     grad_forget_pre = (grad_forget * forget * (1.0 - forget)).astype(BF16)
+    cut_a, cut_b, cut_c = (plane(matmul(normed, g, (0, 0), BF16)) for g in (grad_gate_pre, grad_input_pre, grad_forget_pre))
+    out_keep, cut_a, cut_b, cut_c, up_line, gate_hi, ffn_out, down_own, grad_input_pre, grad_forget_pre = fence(
+        out_keep, cut_a, cut_b, cut_c, up_line, gate_hi, ffn_out, down_own, grad_input_pre, grad_forget_pre
+    )
+
+    sum_low = lambda cut: at.reduce(cut, at.low, 2)
+    sum_lo = lambda line: at.reduce(line, at.lo, 1)
     triple = jnp.concatenate([grad_input_pre, grad_forget_pre, grad_gate_pre], axis=1)
-    grad_normed = at.sum_members(matmul(triple, mix_weight, (1, 1), BF16), at.mixers)
-
-    def channel_grad(right):
-        return at.trade(plane_grad(normed, right, chip_rows).reshape(CORES, rows, channels), at.core, 0)
-
-    mix_owns = [channel_grad(g) for g in (grad_input_pre, grad_forget_pre, grad_gate_pre)]
-
-    def unit_grad(lines):
-        for which in at.his[::-1]:
-            lines = at.fold(lines, which)
-        sets = at.trade(lines.reshape(2, chip_rows, part), at.lo, 0)
-        return at.trade(sets.reshape(2, CORES, rows, part), at.core, 1)
-
-    gate_own, up_own = unit_grad(gate_line), unit_grad(up_line)
-    ffn_out = late(at.sum_group(ffn_part), triple)
+    normed_cut = matmul(triple, mix_weight, (1, 1), BF16)
+    gate_sets, out_low = mates(gate_hi), at.end(out_keep, out_other)
+    keep_a, other_a = at.begin(cut_a, at.low, 2)
+    up_keep, up_other = fold_begin(up_line, at.his[-1])
+    gate_sets, out_low, keep_a, cut_b, cut_c, up_keep, normed_cut, down_own = fence(
+        gate_sets, out_low, keep_a, cut_b, cut_c, up_keep, normed_cut, down_own
+    )
+    keep_b, other_b = at.begin(cut_b, at.low, 2)
+    normed_half = at.sum_members(normed_cut, [at.core])
+    low_a, out_lo, gate_cores, up_hi = at.end(keep_a, other_a), sum_lo(out_low), cores(gate_sets), fold_rest(at.end(up_keep, up_other))
+    low_a, out_lo, gate_cores, up_hi, keep_b, cut_c, normed_half, down_own = fence(
+        low_a, out_lo, gate_cores, up_hi, keep_b, cut_c, normed_half, down_own
+    )
+    grad_normed = at.sum_members(normed_half, at.rep_bits, BF16)
+    up_sets, gate_own = mates(up_hi), at.join_reps(gate_cores)
+    keep_c, other_c = at.begin(cut_c, at.low, 2)
+    low_b, lo_a, out_own = at.end(keep_b, other_b), sum_lo(low_a), at.reduce_his(out_lo)
+    low_b, lo_a, out_own, keep_c, up_sets, down_own = fence(low_b, lo_a, out_own, keep_c, up_sets, down_own)
+    down_own = at.join_reps(down_own)
+    low_c, lo_b, hi_a, up_cores = at.end(keep_c, other_c), sum_lo(low_b), at.reduce_his(lo_a), cores(up_sets)
+    low_c, lo_b, hi_a, up_cores = fence(low_c, lo_b, hi_a, up_cores)
+    up_own, lo_c, hi_b, own_a = at.join_reps(up_cores), sum_lo(low_c), at.reduce_his(lo_b), cores(hi_a)
+    lo_c, hi_b, own_a, out_own, gate_own, grad_normed = fence(lo_c, hi_b, own_a, out_own, gate_own, grad_normed)
+    hi_c, own_b, own_a, out_own = at.reduce_his(lo_c), cores(hi_b), at.join_reps(own_a), at.join_reps(out_own)
+    hi_c, own_b = fence(hi_c, own_b)
+    own_c, own_b = cores(hi_c), at.join_reps(own_b)
+    own_c, gate_own, up_own, out_own, down_own, grad_normed, ffn_out = fence(own_c, gate_own, up_own, out_own, down_own, grad_normed, ffn_out)
+    mix_owns = [own_b, at.join_reps(own_c), own_a]
     block_output = (resid + ffn_out).astype(BF16)
     scaled_in, scale_in = normalize(inputs)
     input_grad = (grad_resid + norm_back(grad_normed * gain_one, scaled_in, scale_in)).astype(BF16)
@@ -415,16 +450,15 @@
         return ((column // small % reps * CORES + core) * at.chips + chip) * small + column % small
 
     def whole_channels(owns):
-        joined = jnp.stack([at.join_reps(own) for own in owns])
-        lines = joined.reshape(len(owns), reps * CORES, rows, channels).transpose(0, 2, 1, 3).reshape(-1, width)
+        lines = jnp.stack(owns).reshape(len(owns), reps * CORES, rows, channels).transpose(0, 2, 1, 3).reshape(-1, width)
         return jnp.split(matmul(lines, chooser(width, width, channel_place), (1, 0)), len(owns))
 
     def whole_units(own):
-        grid = at.join_reps(own).reshape(reps, CORES, 2, rows, at.hi, 2, slim)
-        return grid.transpose(3, 4, 2, 5, 1, 0, 6).reshape(rows, units).astype(F32)
+        grid = own.reshape(reps, CORES, 2, rows, at.length, slim)
+        return grid.transpose(3, 4, 2, 1, 0, 5).reshape(rows, units).astype(F32)
 
     def whole_rows(own):
-        return at.join_reps(own).reshape(-1, width).astype(F32)
+        return own.reshape(-1, width).astype(F32)
 
     down_total = whole_rows(down_own)
     gate_total, up_total = whole_units(gate_own), whole_units(up_own)

time: 797 us -> 743 us (0.932)
  waiting for transfers between devices: 379 us -> 310 us
  local copies, waits for them, and re-layouts: 96.4 us -> 81.3 us
  matrix products: 118 us -> 129 us
  starting transfers between devices: 45 us -> 55.6 us
  blocking collectives: 20.9 us -> 29.2 us
    ppermute x57, waiting for transfers between devices: 353 us -> 309 us  [swap(): lax.ppermute(value, AXES, [(n, n ^ flip) for n in range(self.reps * self....]
    all_gather x2, waiting for transfers between devices: 14.4 us -> 0.01 us  [gather_group(): lax.all_gather(value, AXES, axis=0, tiled=True, axis_index_groups=self.gr...]
    unnamed x288 -> x214, local copies, waits for them, and re-layouts: 36.9 us -> 23.2 us
    convert_element_type x5 -> x11, other arithmetic: 4.08 us -> 17 us  [the longest x6 12.7 us: end(): return (own.astype(F32) + other.astype(F32)).astype(BF16)]
    all_gather x1, waiting for transfers between devices: 11.2 us -> 0.01 us  [shards(): mix_all = lax.all_gather(picked, 'shard', axis=0, tiled=True)]
    dot_general x21 -> x23, matrix products: 118 us -> 129 us  [matmul(): lax.dot_general(left, right, ((dims[:1], dims[1:]), ((), ())), preferred_...]
    ppermute x57, starting transfers between devices: 44.6 us -> 55 us  [swap(): lax.ppermute(value, AXES, [(n, n ^ flip) for n in range(self.reps * self....]
    all_gather x1, blocking collectives: 20.9 us -> 29.2 us  [shards(): gains = lax.all_gather(own_gains, 'shard', axis=1, tiled=True).astype(F32)]
  transfers between devices with their start and end apart: 62 -> 62, of which waited for: 30 -> 27; matrix products, arithmetic and copies ran while one was open for 33% -> 36% of each run, Pallas kernels for 1% -> 1%
where the time goes in v3:
time: 743 us; the launch traced here: 738 us
  waiting for transfers between devices  310 us (42%)
  matrix products  129 us (17%)
  other arithmetic  110 us (15%)
  local copies, waits for them, and re-layouts  81.3 us (11%)
  starting transfers between devices  55.6 us (7%)
  blocking collectives  29.2 us (4%)
  between operations  16.1 us (2%)
  Pallas kernels  7.72 us (1%)
    ppermute x57, waiting for transfers between devices, swap(): lax.ppermute(value, AXES, [(n, n ^ flip) for n in range(self.reps * self....  309 us
    dot_general x23, matrix products, matmul(): lax.dot_general(left, right, ((dims[:1], dims[1:]), ((), ())), preferred_...  129 us
    ppermute x57, starting transfers between devices, swap(): lax.ppermute(value, AXES, [(n, n ^ flip) for n in range(self.reps * self....  55 us
    all_gather x1, blocking collectives, shards(): gains = lax.all_gather(own_gains, 'shard', axis=1, tiled=True).astype(F32)  29.2 us
    another operation x43, other arithmetic, merge(): jnp.stack([jnp.where(first, own, other), jnp.where(first, other, own)], a...  23.6 us
    unnamed x214, local copies, waits for them, and re-layouts  23.2 us
  transfers between devices with their start and end apart: 62, of which 27 were waited for; matrix products, arithmetic and copies ran while one was open for 36% of the time, Pallas kernels for 1%

profile of v3, /device:TPU:0, one launch (start us, length us, event | category | flops | bytes accessed | tf_op | source)
XLA Modules:
  0.0 738.0 jit_solution(9072209973984046530)
XLA Ops:
  7.3 3.4 fusion.174
  12.2 3.2 copy.179
  16.3 4.0 collective-permute-start.2
  22.0 3.4 fusion.182
  25.4 3.4 fusion.188
  33.4 5.0 fusion.179
  38.5 3.4 fusion.185
  42.0 7.9 %collective-permute-done.3 = s32[1,192]{1,0:T(1,128)} collective-permute-done((s32[1,192]{1,0:T(1,128)}, s32[1,192]{1,0:T(1,128)}, u32[]{:S(2)}, u32[]{:S(2)}) %collective-permute-start.3) | collective-permute-done | bytes 800 | tf_op jit(solution)/shard_map/ppermute | solution.py:140
  55.4 29.2 %all_gather.13 = bf16[3,2048]{1,0:T(4,128)(2,1)S(1)} all-gather(bf16[3,128]{1,0:T(4,128)(2,1)S(1)} %pad_maximum_fusion.34), channel_id=1, replica_groups=mesh['rep'=2,'shard'=16] {'shard'}, dimensions={1}, use_global_device_ids=true | all-gather | bytes 13056 | tf_op jit(solution)/shard_map/all_gather | solution.py:305
  94.1 2.6 collective-permute-start.6
  102.5 22.0 %collective-permute-done.6 = bf16[512,704]{0,1:T(8,128)(2,1)} collective-permute-done((bf16[512,704]{0,1:T(8,128)(2,1)}, bf16[512,704]{0,1:T(8,128)(2,1)}, u32[]{:S(2)}, u32[]{:S(2)}) %collective-permute-start.6) | collective-permute-done | bytes 720928 | tf_op jit(solution)/shard_map/ppermute | solution.py:140
  127.1 19.7 %collective-permute-done.8 = bf16[2,2,64,2048]{3,2,1,0:T(8,128)(2,1)} collective-permute-done((bf16[2,2,64,2048]{3,2,1,0:T(8,128)(2,1)}, bf16[2,2,64,2048]{3,2,1,0:T(8,128)(2,1)}, u32[]{:S(2)}, u32[]{:S(2)}) %collective-permute-start.8) | collective-permute-done | bytes 1048608 | tf_op jit(solution)/shard_map/ppermute | solution.py:140
  151.7 5.1 fusion.118
  157.4 3.4 reshape.245
  167.4 8.2 %fusion.121 = f32[768,1536]{1,0:T(8,128)S(1)} fusion(bf16[768,2048]{1,0:T(8,128)(2,1)} %fusion.118, bf16[2048,3072]{0,1:T(8,128)(2,1)} %all-gather.4.cloned.1.call-done, s32[]{:T(128)S(6)} %select_n.686), kind=kOutput, calls=%fused_computation.142 | convolution fusion | flops 4831838208 | bytes 14155780 | tf_op jit(solution)/shard_map/dot_general | solution.py:33
  181.8 3.6 convolution_convert_fusion.1
  185.5 14.2 %collective-permute-done.9 = bf16[512,704]{0,1:T(8,128)(2,1)} collective-permute-done((bf16[512,704]{0,1:T(8,128)(2,1)}, bf16[512,704]{0,1:T(8,128)(2,1)}, u32[]{:S(2)}, u32[]{:S(2)}) %collective-permute-start.9) | collective-permute-done | bytes 720928 | tf_op jit(solution)/shard_map/ppermute | solution.py:140
  202.9 3.3 collective-permute-start.15
  211.6 17.3 %collective-permute-done.13 = f32[1,192]{1,0:T(1,128)S(1)} collective-permute-done((f32[1,192]{1,0:T(1,128)S(1)}, f32[1,192]{1,0:T(1,128)S(1)}, u32[]{:S(2)}, u32[]{:S(2)}) %collective-permute-start.13) | collective-permute-done | bytes 800 | tf_op jit(solution)/shard_map/ppermute | solution.py:140
  228.9 21.0 %collective-permute-done.15 = bf16[512,704]{0,1:T(8,128)(2,1)S(1)} collective-permute-done((bf16[512,704]{0,1:T(8,128)(2,1)}, bf16[512,704]{0,1:T(8,128)(2,1)S(1)}, u32[]{:S(2)}, u32[]{:S(2)}) %collective-permute-start.15) | collective-permute-done | bytes 720928 | tf_op jit(solution)/shard_map/ppermute | solution.py:140
  252.0 3.3 pad_maximum_fusion.2
  260.2 2.6 collective-permute-start.17
  264.1 30.6 %collective-permute-done.17 = bf16[176,2048]{1,0:T(8,128)(2,1)S(1)} collective-permute-done((bf16[176,2048]{1,0:T(8,128)(2,1)}, bf16[176,2048]{1,0:T(8,128)(2,1)S(1)}, u32[]{:S(2)}, u32[]{:S(2)}) %collective-permute-start.17) | collective-permute-done | bytes 720928 | tf_op jit(solution)/shard_map/ppermute | solution.py:140
  297.1 12.9 %collective-permute-done.16 = bf16[1024,704]{0,1:T(8,128)(2,1)S(1)} collective-permute-done((bf16[1024,704]{0,1:T(8,128)(2,1)}, bf16[1024,704]{0,1:T(8,128)(2,1)S(1)}, u32[]{:S(2)}, u32[]{:S(2)}) %collective-permute-start.16) | collective-permute-done | bytes 1441824 | tf_op jit(solution)/shard_map/ppermute | solution.py:140
  313.6 8.6 %fusion.286 = f32[1536,704]{0,1:T(8,128)S(1)} fusion(bf16[1536,2048]{1,0:T(8,128)(2,1)} %all-gather.6.cloned.1.call-done, bf16[2048,704]{0,1:T(8,128)(2,1)} %pad_maximum_fusion.2), kind=kOutput, calls=%fused_computation.542 | convolution fusion | flops 4429185024 | bytes 13500416 | tf_op jit(solution)/shard_map/dot_general | solution.py:33
  322.2 6.6 multiply_convert_fusion.2
  328.8 6.0 convolution_convert_fusion.4
  334.8 10.8 %collective-permute-done.18 = bf16[2,176,2048]{2,1,0:T(8,128)(2,1)S(1)} collective-permute-done((bf16[2,176,2048]{2,1,0:T(8,128)(2,1)}, bf16[2,176,2048]{2,1,0:T(8,128)(2,1)S(1)}, u32[]{:S(2)}, u32[]{:S(2)}) %collective-permute-start.18) | collective-permute-done | bytes 1441824 | tf_op jit(solution)/shard_map/ppermute | solution.py:140
  346.2 10.0 %multiply_convert_fusion.1 = (bf16[1536,704]{0,1:T(8,128)(2,1)}, bf16[1536,704]{0,1:T(8,128)(2,1)S(1)}) fusion(f32[1536,704]{0,1:T(8,128)S(1)} %fusion.286, f32[1536,704]{0,1:T(8,128)} %get-tuple-element.348, bf16[1536,2048]{1,0:T(8,128)(2,1)S(1)} %bitcast.455, bf16[704,2048]{1,0:T(8,128)(2,1)S(1)} %bitcast.411), kind=kOutput, calls=%fused_computation.145 | convolution fusion | flops 4443242496 | bytes 22151168 | tf_op jit(solution)/shard_map/dot_general | solution.py:33
  356.2 5.1 fusion.287
  361.3 8.7 %add_convert_fusion = bf16[1536,2048]{1,0:T(8,128)(2,1)} fusion(f32[1536,2048]{1,0:T(8,128)S(1)} %fusion.287, bf16[1536,704]{0,1:T(8,128)(2,1)} %get-tuple-element.129, bf16[2048,704]{0,1:T(8,128)(2,1)S(1)} %copy-done.47), kind=kOutput, calls=%fused_computation.56 | convolution fusion | flops 4435476480 | bytes 23920640 | tf_op jit(solution)/shard_map/dot_general | solution.py:33
  370.1 2.8 dynamic-slice_bitcast_fusion
  373.3 10.0 %convolution_convert_fusion.2 = bf16[2048,704]{0,1:T(8,128)(2,1)} fusion(bf16[1536,704]{0,1:T(8,128)(2,1)S(1)} %copy-done.91, bf16[1536,2048]{1,0:T(8,128)(2,1)} %all-gather.6.cloned.1.call-done), kind=kOutput, calls=%fused_computation.168 | convolution fusion | flops 4430626816 | bytes 11337728 | tf_op jit(solution)/shard_map/dot_general | solution.py:33
  383.3 4.8 convolution_convert_fusion.3
  392.4 7.0 convolution_convert_fusion
  399.4 8.3 %collective-permute-done.20 = bf16[2,176,2048]{2,1,0:T(8,128)(2,1)} collective-permute-done((bf16[2,176,2048]{2,1,0:T(8,128)(2,1)}, bf16[2,176,2048]{2,1,0:T(8,128)(2,1)}, u32[]{:S(2)}, u32[]{:S(2)}) %collective-permute-start.20) | collective-permute-done | bytes 1441824 | tf_op jit(solution)/shard_map/ppermute | solution.py:140
  414.6 37.6 %collective-permute-done.19 = bf16[1024,704]{0,1:T(8,128)(2,1)} collective-permute-done((bf16[1024,704]{0,1:T(8,128)(2,1)}, bf16[1024,704]{0,1:T(8,128)(2,1)}, u32[]{:S(2)}, u32[]{:S(2)}) %collective-permute-start.19) | collective-permute-done | bytes 1441824 | tf_op jit(solution)/shard_map/ppermute | solution.py:140
  452.2 3.5 add_convert_fusion.2
  467.7 15.6 %collective-permute-done.22 = bf16[192,2048]{1,0:T(8,128)(2,1)S(1)} collective-permute-done((bf16[192,2048]{1,0:T(8,128)(2,1)S(1)}, bf16[192,2048]{1,0:T(8,128)(2,1)S(1)}, u32[]{:S(2)}, u32[]{:S(2)}) %collective-permute-start.22) | collective-permute-done | bytes 786464 | tf_op jit(solution)/shard_map/ppermute | solution.py:140
  489.9 3.0 copy.212
  495.6 3.6 collective-permute-done.26
  499.2 3.2 add_convert_fusion.1
  502.4 3.5 pad_maximum_fusion.1
  507.0 4.6 convolution_convert_fusion.8
  514.3 3.9 subtract_multiply_fusion
  521.8 3.2 convolution_convert_fusion.5
  525.0 3.2 convolution_convert_fusion.6
  528.2 3.2 convolution_convert_fusion.7
  531.4 6.9 collective-permute-done.27
  548.8 8.2 %fusion.141 = bf16[768,2048]{1,0:T(8,128)(2,1)S(1)} fusion(bf16[2048,3072]{0,1:T(8,128)(2,1)} %all-gather.4.cloned.1.call-done, s32[]{:T(128)S(6)} %select_n.686, bf16[768,512]{1,0:T(8,128)(2,1)S(1)} %copy-done.89, bf16[768,512]{1,0:T(8,128)(2,1)S(1)} %copy-done.66, bf16[768,512]{1,0:T(8,128)(2,1)S(1)} %copy-done.68), kind=kOutput, calls=%fused_computation.167 | convolution fusion | flops 4840488960 | bytes 11796484 | tf_op jit(solution)/shard_map/dot_general | solution.py:33
  557.1 3.5 add_convert_fusion.6
  569.3 7.6 %collective-permute-done.33 = bf16[512,704]{0,1:T(8,128)(2,1)} collective-permute-done((bf16[512,704]{0,1:T(8,128)(2,1)}, bf16[512,704]{0,1:T(8,128)(2,1)}, u32[]{:S(2)}, u32[]{:S(2)}) %collective-permute-start.33) | collective-permute-done | bytes 720928 | tf_op jit(solution)/shard_map/ppermute | solution.py:140
  578.2 9.7 %collective-permute-done.31 = bf16[2,64,2048]{2,1,0:T(8,128)(2,1)S(1)} collective-permute-done((bf16[2,64,2048]{2,1,0:T(8,128)(2,1)S(1)}, bf16[2,64,2048]{2,1,0:T(8,128)(2,1)S(1)}, u32[]{:S(2)}, u32[]{:S(2)}) %collective-permute-start.31) | collective-permute-done | bytes 524320 | tf_op jit(solution)/shard_map/ppermute | solution.py:140
  591.3 3.7 convert_add_fusion
  611.2 2.9 collective-permute-done.37
  616.4 3.6 collective-permute-done.36
  626.0 15.4 %collective-permute-done.46 = bf16[2,2,128,704]{2,3,1,0:T(8,128)(2,1)} collective-permute-done((bf16[2,2,128,704]{2,3,1,0:T(8,128)(2,1)}, bf16[2,2,128,704]{2,3,1,0:T(8,128)(2,1)}, u32[]{:S(2)}, u32[]{:S(2)}) %collective-permute-start.46) | collective-permute-done | bytes 720928 | tf_op jit(solution)/shard_map/ppermute | solution.py:140
  646.2 6.7 collective-permute-done.41
  654.7 4.5 collective-permute-done.40
  664.1 10.3 %collective-permute-done.44 = bf16[256,512]{1,0:T(8,128)(2,1)S(1)} collective-permute-done((bf16[256,512]{1,0:T(8,128)(2,1)S(1)}, bf16[256,512]{1,0:T(8,128)(2,1)S(1)}, u32[]{:S(2)}, u32[]{:S(2)}) %collective-permute-start.44) | collective-permute-done | bytes 262176 | tf_op jit(solution)/shard_map/ppermute | solution.py:140
  674.5 5.8 collective-permute-done.43
  683.5 11.7 %collective-permute-done.48 = bf16[256,512]{1,0:T(8,128)(2,1)S(1)} collective-permute-done((bf16[256,512]{1,0:T(8,128)(2,1)S(1)}, bf16[256,512]{1,0:T(8,128)(2,1)S(1)}, u32[]{:S(2)}, u32[]{:S(2)}) %collective-permute-start.48) | collective-permute-done | bytes 262176 | tf_op jit(solution)/shard_map/ppermute | solution.py:140
  710.9 3.5 copy.216
  723.4 5.4 fusion.11
  (507 shorter events, 202.9 us)
Async XLA Ops:
  7.2 149.6 %all-gather.4.cloned.1.call-start = ((), (), s32[]{:S(2)}) async-start(), calls=%async_computation.2 | async-start | bytes 13369344 | tf_op jit(solution)/shard_map/all_gather | solution.py:280
  15.4 296.5 %all-gather.8.cloned.1.call-start = ((), (), s32[]{:S(2)}) async-start(), calls=%async_computation.4 | async-start | bytes 7077888 | tf_op jit(solution)/shard_map/all_gather | solution.py:224
  16.3 36.4 %collective-permute-start.2 = (bf16[64,2048]{1,0:T(8,128)(2,1)}, bf16[64,2048]{1,0:T(8,128)(2,1)}, u32[]{:S(2)}, u32[]{:S(2)}) collective-permute-start(bf16[64,2048]{1,0:T(8,128)(2,1)} %dynamic-slice_bitcast_fusion.19), channel_id=1, source_target_pairs={{0,8},{1,9},{2,10},{3,11},{4,12},{5,13},{6,14},{7,15},{8,0},{9,1},... | collective-permute-start | bytes 786440 | tf_op jit(solution)/shard_map/ppermute | solution.py:140
  29.8 54.8 %collective-permute-start.5 = (bf16[512,704]{0,1:T(8,128)(2,1)}, bf16[512,704]{0,1:T(8,128)(2,1)}, u32[]{:S(2)}, u32[]{:S(2)}) collective-permute-start(bf16[512,704]{0,1:T(8,128)(2,1)} %pad_maximum_fusion.19), channel_id=1, source_target_pairs={{0,1},{1,0},{2,3},{3,2},{4,5},{5,4},{6,7},{7,6},{8,9},{9,8},{10,11... | collective-permute-start | bytes 2162696 | tf_op jit(solution)/shard_map/ppermute | solution.py:140
  29.8 69.2 %collective-permute-start = (bf16[192,2048]{1,0:T(8,128)(2,1)S(1)}, bf16[192,2048]{1,0:T(8,128)(2,1)S(1)}, u32[]{:S(2)}, u32[]{:S(2)}) collective-permute-start(bf16[192,2048]{1,0:T(8,128)(2,1)S(1)} %bitcast.393), channel_id=1, source_target_pairs={{0,16},{1,17},{2,18},{3,19},{4,20},{5,21},{6,22},{7,23},{8,24},{9,... | collective-permute-start | bytes 2359304 | tf_op jit(solution)/shard_map/ppermute | solution.py:140
  31.3 18.6 %collective-permute-start.3 = (s32[1,192]{1,0:T(1,128)}, s32[1,192]{1,0:T(1,128)}, u32[]{:S(2)}, u32[]{:S(2)}) collective-permute-start(s32[1,192]{1,0:T(1,128)} %param.14), channel_id=1, source_target_pairs={{0,16},{1,17},{2,18},{3,19},{4,20},{5,21},{6,22},{7,23},{8,24},{9,... | collective-permute-start | bytes 2312 | tf_op jit(solution)/shard_map/ppermute | solution.py:140
  50.5 1.2 collective-permute-start.4
  53.7 43.0 %collective-permute-start.7 = (bf16[2,64,2048]{2,1,0:T(8,128)(2,1)S(1)}, bf16[2,64,2048]{2,1,0:T(8,128)(2,1)}, u32[]{:S(2)}, u32[]{:S(2)}) collective-permute-start(bf16[2,64,2048]{2,1,0:T(8,128)(2,1)S(1)} %pad_maximum_fusion.24), channel_id=1, source_target_pairs={{0,4},{1,5},{2,6},{3,7},{4,0},{5,1},{6,2},{7,3},{8,12},{9,13},{10,... | collective-permute-start | bytes 1572872 | tf_op jit(solution)/shard_map/ppermute | solution.py:140
  94.1 30.3 %collective-permute-start.6 = (bf16[512,704]{0,1:T(8,128)(2,1)}, bf16[512,704]{0,1:T(8,128)(2,1)}, u32[]{:S(2)}, u32[]{:S(2)}) collective-permute-start(bf16[512,704]{0,1:T(8,128)(2,1)} %bitcast.436), channel_id=1, source_target_pairs={{0,2},{1,3},{2,0},{3,1},{4,6},{5,7},{6,4},{7,5},{8,10},{9,11},{10,... | collective-permute-start | bytes 2162696 | tf_op jit(solution)/shard_map/ppermute | solution.py:140
  99.0 47.9 %collective-permute-start.8 = (bf16[2,2,64,2048]{3,2,1,0:T(8,128)(2,1)}, bf16[2,2,64,2048]{3,2,1,0:T(8,128)(2,1)}, u32[]{:S(2)}, u32[]{:S(2)}) collective-permute-start(bf16[2,2,64,2048]{3,2,1,0:T(8,128)(2,1)} %pad_maximum_fusion.17), channel_id=1, source_target_pairs={{0,2},{1,3},{2,0},{3,1},{4,6},{5,7},{6,4},{7,5},{8,10},{9,11},{10,... | collective-permute-start | bytes 3145736 | tf_op jit(solution)/shard_map/ppermute | solution.py:140
  100.2 49.5 %collective-permute-start.1 = (bf16[384,2048]{1,0:T(8,128)(2,1)}, bf16[384,2048]{1,0:T(8,128)(2,1)}, u32[]{:S(2)}, u32[]{:S(2)}) collective-permute-start(bf16[384,2048]{1,0:T(8,128)(2,1)} %pad_maximum_fusion.6), channel_id=1, source_target_pairs={{0,1},{1,0},{2,3},{3,2},{4,5},{5,4},{6,7},{7,6},{8,9},{9,8},{10,11... | collective-permute-start | bytes 4718600 | tf_op jit(solution)/shard_map/ppermute | solution.py:140
  100.3 51.4 %copy-start.74 = (f32[1,2048]{1,0:T(1,128)}, f32[1,2048]{1,0:T(1,128)S(1)}, u32[]{:S(2)}) copy-start(f32[1,2048]{1,0:T(1,128)S(1)} %get-tuple-element.346) | copy-start | bytes 24580
  156.8 155.1 %all-gather.6.cloned.1.call-start = ((), (), s32[]{:S(2)}) async-start(), calls=%async_computation.3 | async-start | bytes 7077888 | tf_op jit(solution)/shard_map/all_gather | solution.py:224
  164.9 34.7 %collective-permute-start.9 = (bf16[512,704]{0,1:T(8,128)(2,1)}, bf16[512,704]{0,1:T(8,128)(2,1)}, u32[]{:S(2)}, u32[]{:S(2)}) collective-permute-start(bf16[512,704]{0,1:T(8,128)(2,1)} %bitcast.169), channel_id=1, source_target_pairs={{0,8},{1,9},{2,10},{3,11},{4,12},{5,13},{6,14},{7,15},{8,0},{9,1},... | collective-permute-start | bytes 2162696 | tf_op jit(solution)/shard_map/ppermute | solution.py:140
  202.4 3.8 collective-permute-start.10
  202.4 49.6 %collective-permute-start.14 = (bf16[1024,704]{0,1:T(8,128)(2,1)S(1)}, bf16[1024,704]{0,1:T(8,128)(2,1)}, u32[]{:S(2)}, u32[]{:S(2)}) collective-permute-start(bf16[1024,704]{0,1:T(8,128)(2,1)S(1)} %pad_maximum_fusion.11), channel_id=1, source_target_pairs={{0,4},{1,5},{2,6},{3,7},{4,0},{5,1},{6,2},{7,3},{8,12},{9,13},{10,... | collective-permute-start | bytes 4325384 | tf_op jit(solution)/shard_map/ppermute | solution.py:140
  202.9 47.0 %collective-permute-start.15 = (bf16[512,704]{0,1:T(8,128)(2,1)}, bf16[512,704]{0,1:T(8,128)(2,1)S(1)}, u32[]{:S(2)}, u32[]{:S(2)}) collective-permute-start(bf16[512,704]{0,1:T(8,128)(2,1)} %bitcast.415), channel_id=1, source_target_pairs={{0,8},{1,9},{2,10},{3,11},{4,12},{5,13},{6,14},{7,15},{8,0},{9,1},... | collective-permute-start | bytes 2162696 | tf_op jit(solution)/shard_map/ppermute | solution.py:140
  206.2 4.2 collective-permute-start.12
  208.9 46.3 %collective-permute-start.11 = (bf16[192,2048]{1,0:T(8,128)(2,1)S(1)}, bf16[192,2048]{1,0:T(8,128)(2,1)S(1)}, u32[]{:S(2)}, u32[]{:S(2)}) collective-permute-start(bf16[192,2048]{1,0:T(8,128)(2,1)S(1)} %slice.200), channel_id=1, source_target_pairs={{0,16},{1,17},{2,18},{3,19},{4,20},{5,21},{6,22},{7,23},{8,24},{9,... | collective-permute-start | bytes 2359304 | tf_op jit(solution)/shard_map/ppermute | solution.py:140
  210.5 18.5 %collective-permute-start.13 = (f32[1,192]{1,0:T(1,128)S(1)}, f32[1,192]{1,0:T(1,128)S(1)}, u32[]{:S(2)}, u32[]{:S(2)}) collective-permute-start(f32[1,192]{1,0:T(1,128)S(1)} %slice.146), channel_id=1, source_target_pairs={{0,16},{1,17},{2,18},{3,19},{4,20},{5,21},{6,22},{7,23},{8,24},{9,... | collective-permute-start | bytes 2312 | tf_op jit(solution)/shard_map/ppermute | solution.py:140
  260.1 197.9 %reduce-scatter.3.cloned.1.call-start = ((), (), s32[]{:S(2)}) async-start(), calls=%async_computation.5 | async-start | bytes 7077888 | tf_op jit(solution)/shard_map/reduce_scatter | solution.py:227
  260.2 49.9 %copy-start.29 = (bf16[1024,704]{0,1:T(8,128)(2,1)S(1)}, bf16[1024,704]{0,1:T(8,128)(2,1)}, u32[]{:S(2)}) copy-start(bf16[1024,704]{0,1:T(8,128)(2,1)} %pad_maximum_fusion.12) | copy-start | bytes 4325380
  260.2 34.5 %collective-permute-start.17 = (bf16[176,2048]{1,0:T(8,128)(2,1)}, bf16[176,2048]{1,0:T(8,128)(2,1)S(1)}, u32[]{:S(2)}, u32[]{:S(2)}) collective-permute-start(bf16[176,2048]{1,0:T(8,128)(2,1)} %dynamic-slice_bitcast_fusion.10), channel_id=1, source_target_pairs={{0,8},{1,9},{2,10},{3,11},{4,12},{5,13},{6,14},{7,15},{8,0},{9,1},... | collective-permute-start | bytes 2162696 | tf_op jit(solution)/shard_map/ppermute | solution.py:140
  262.8 47.3 %collective-permute-start.16 = (bf16[1024,704]{0,1:T(8,128)(2,1)}, bf16[1024,704]{0,1:T(8,128)(2,1)S(1)}, u32[]{:S(2)}, u32[]{:S(2)}) collective-permute-start(bf16[1024,704]{0,1:T(8,128)(2,1)} %pad_maximum_fusion.12), channel_id=1, source_target_pairs={{0,4},{1,5},{2,6},{3,7},{4,0},{5,1},{6,2},{7,3},{8,12},{9,13},{10,... | collective-permute-start | bytes 4325384 | tf_op jit(solution)/shard_map/ppermute | solution.py:140
  311.9 33.8 %collective-permute-start.18 = (bf16[2,176,2048]{2,1,0:T(8,128)(2,1)}, bf16[2,176,2048]{2,1,0:T(8,128)(2,1)S(1)}, u32[]{:S(2)}, u32[]{:S(2)}) collective-permute-start(bf16[2,176,2048]{2,1,0:T(8,128)(2,1)} %pad_maximum_fusion.13), channel_id=1, source_target_pairs={{0,4},{1,5},{2,6},{3,7},{4,0},{5,1},{6,2},{7,3},{8,12},{9,13},{10,... | collective-permute-start | bytes 4325384 | tf_op jit(solution)/shard_map/ppermute | solution.py:140
  370.0 169.7 %reduce-scatter.5.cloned.1.call-start = ((), (), s32[]{:S(2)}) async-start(), calls=%async_computation.6 | async-start | bytes 7077888 | tf_op jit(solution)/shard_map/reduce_scatter | solution.py:227
  372.9 34.8 %collective-permute-start.20 = (bf16[2,176,2048]{2,1,0:T(8,128)(2,1)}, bf16[2,176,2048]{2,1,0:T(8,128)(2,1)}, u32[]{:S(2)}, u32[]{:S(2)}) collective-permute-start(bf16[2,176,2048]{2,1,0:T(8,128)(2,1)} %dynamic-slice_bitcast_fusion), channel_id=1, source_target_pairs={{0,4},{1,5},{2,6},{3,7},{4,0},{5,1},{6,2},{7,3},{8,12},{9,13},{10,... | collective-permute-start | bytes 4325384 | tf_op jit(solution)/shard_map/ppermute | solution.py:140
  391.0 61.2 %collective-permute-start.19 = (bf16[1024,704]{0,1:T(8,128)(2,1)}, bf16[1024,704]{0,1:T(8,128)(2,1)}, u32[]{:S(2)}, u32[]{:S(2)}) collective-permute-start(bf16[1024,704]{0,1:T(8,128)(2,1)} %slice.149), channel_id=1, source_target_pairs={{0,4},{1,5},{2,6},{3,7},{4,0},{5,1},{6,2},{7,3},{8,12},{9,13},{10,... | collective-permute-start | bytes 4325384 | tf_op jit(solution)/shard_map/ppermute | solution.py:140
  412.1 43.7 %collective-permute-start.21 = (bf16[176,2048]{1,0:T(8,128)(2,1)}, bf16[176,2048]{1,0:T(8,128)(2,1)}, u32[]{:S(2)}, u32[]{:S(2)}) collective-permute-start(bf16[176,2048]{1,0:T(8,128)(2,1)} %dynamic-slice_bitcast_fusion.9), channel_id=1, source_target_pairs={{0,8},{1,9},{2,10},{3,11},{4,12},{5,13},{6,14},{7,15},{8,0},{9,1},... | collective-permute-start | bytes 2162696 | tf_op jit(solution)/shard_map/ppermute | solution.py:140
  465.4 18.0 %collective-permute-start.22 = (bf16[192,2048]{1,0:T(8,128)(2,1)S(1)}, bf16[192,2048]{1,0:T(8,128)(2,1)S(1)}, u32[]{:S(2)}, u32[]{:S(2)}) collective-permute-start(bf16[192,2048]{1,0:T(8,128)(2,1)S(1)} %get-tuple-element.267), channel_id=1, source_target_pairs={{0,16},{1,17},{2,18},{3,19},{4,20},{5,21},{6,22},{7,23},{8,24},{9,... | collective-permute-start | bytes 2359304 | tf_op jit(solution)/shard_map/ppermute | solution.py:140
  467.7 31.5 %collective-permute-start.26 = (bf16[1024,704]{0,1:T(8,128)(2,1)}, bf16[1024,704]{0,1:T(8,128)(2,1)}, u32[]{:S(2)}, u32[]{:S(2)}) collective-permute-start(bf16[1024,704]{0,1:T(8,128)(2,1)} %slice.122), channel_id=1, source_target_pairs={{0,4},{1,5},{2,6},{3,7},{4,0},{5,1},{6,2},{7,3},{8,12},{9,13},{10,... | collective-permute-start | bytes 4325384 | tf_op jit(solution)/shard_map/ppermute | solution.py:140
  484.7 17.6 %collective-permute-start.23 = (bf16[384,2048]{1,0:T(8,128)(2,1)}, bf16[384,2048]{1,0:T(8,128)(2,1)}, u32[]{:S(2)}, u32[]{:S(2)}) collective-permute-start(bf16[384,2048]{1,0:T(8,128)(2,1)} %pad_maximum_fusion.8), channel_id=1, source_target_pairs={{0,1},{1,0},{2,3},{3,2},{4,5},{5,4},{6,7},{7,6},{8,9},{9,8},{10,11... | collective-permute-start | bytes 4718600 | tf_op jit(solution)/shard_map/ppermute | solution.py:140
  484.8 9.5 %collective-permute-start.24 = (f32[1,2,192]{2,1,0:T(2,128)S(1)}, f32[1,2,192]{2,1,0:T(2,128)S(1)}, u32[]{:S(2)}, u32[]{:S(2)}) collective-permute-start(f32[1,2,192]{2,1,0:T(2,128)S(1)} %maximum_bitcast_fusion), channel_id=1, source_target_pairs={{0,16},{1,17},{2,18},{3,19},{4,20},{5,21},{6,22},{7,23},{8,24},{9,... | collective-permute-start | bytes 4616 | tf_op jit(solution)/shard_map/ppermute | solution.py:140
  494.3 1.2 collective-permute-start.25
  506.8 31.4 %collective-permute-start.27 = (bf16[512,704]{0,1:T(8,128)(2,1)}, bf16[512,704]{0,1:T(8,128)(2,1)}, u32[]{:S(2)}, u32[]{:S(2)}) collective-permute-start(bf16[512,704]{0,1:T(8,128)(2,1)} %slice.127), channel_id=1, source_target_pairs={{0,8},{1,9},{2,10},{3,11},{4,12},{5,13},{6,14},{7,15},{8,0},{9,1},... | collective-permute-start | bytes 2162696 | tf_op jit(solution)/shard_map/ppermute | solution.py:140
  513.1 44.0 %collective-permute-start.29 = (bf16[2,2,64,2048]{3,2,1,0:T(8,128)(2,1)}, bf16[2,2,64,2048]{3,2,1,0:T(8,128)(2,1)}, u32[]{:S(2)}, u32[]{:S(2)}) collective-permute-start(bf16[2,2,64,2048]{3,2,1,0:T(8,128)(2,1)} %get-tuple-element.290), channel_id=1, source_target_pairs={{0,2},{1,3},{2,0},{3,1},{4,6},{5,7},{6,4},{7,5},{8,10},{9,11},{10,... | collective-permute-start | bytes 3145736 | tf_op jit(solution)/shard_map/ppermute | solution.py:140
  543.9 16.7 %collective-permute-start.28 = (bf16[256,704]{0,1:T(8,128)(2,1)S(1)}, bf16[256,704]{0,1:T(8,128)(2,1)S(1)}, u32[]{:S(2)}, u32[]{:S(2)}) collective-permute-start(bf16[256,704]{0,1:T(8,128)(2,1)S(1)} %bitcast.439), channel_id=1, source_target_pairs={{0,2},{1,3},{2,0},{3,1},{4,6},{5,7},{6,4},{7,5},{8,10},{9,11},{10,... | collective-permute-start | bytes 1081352 | tf_op jit(solution)/shard_map/ppermute | solution.py:140
  545.6 31.2 %collective-permute-start.33 = (bf16[512,704]{0,1:T(8,128)(2,1)}, bf16[512,704]{0,1:T(8,128)(2,1)}, u32[]{:S(2)}, u32[]{:S(2)}) collective-permute-start(bf16[512,704]{0,1:T(8,128)(2,1)} %get-tuple-element.304), channel_id=1, source_target_pairs={{0,8},{1,9},{2,10},{3,11},{4,12},{5,13},{6,14},{7,15},{8,0},{9,1},... | collective-permute-start | bytes 2162696 | tf_op jit(solution)/shard_map/ppermute | solution.py:140
  547.2 41.6 %collective-permute-start.30 = (bf16[2,2,256,512]{3,2,1,0:T(8,128)(2,1)}, bf16[2,2,256,512]{3,2,1,0:T(8,128)(2,1)}, u32[]{:S(2)}, u32[]{:S(2)}) collective-permute-start(bf16[2,2,256,512]{3,2,1,0:T(8,128)(2,1)} %get-tuple-element.289), channel_id=1, source_target_pairs={{0,2},{1,3},{2,0},{3,1},{4,6},{5,7},{6,4},{7,5},{8,10},{9,11},{10,... | collective-permute-start | bytes 3145736 | tf_op jit(solution)/shard_map/ppermute | solution.py:140
  562.0 29.3 %collective-permute-start.34 = (bf16[384,2048]{1,0:T(8,128)(2,1)}, bf16[384,2048]{1,0:T(8,128)(2,1)}, u32[]{:S(2)}, u32[]{:S(2)}) collective-permute-start(bf16[384,2048]{1,0:T(8,128)(2,1)} %slice.131), channel_id=1, source_target_pairs={{0,1},{1,0},{2,3},{3,2},{4,5},{5,4},{6,7},{7,6},{8,9},{9,8},{10,11... | collective-permute-start | bytes 4718600 | tf_op jit(solution)/shard_map/ppermute | solution.py:140
  563.7 4.1 collective-permute-start.32
  565.4 22.5 %collective-permute-start.31 = (bf16[2,64,2048]{2,1,0:T(8,128)(2,1)S(1)}, bf16[2,64,2048]{2,1,0:T(8,128)(2,1)S(1)}, u32[]{:S(2)}, u32[]{:S(2)}) collective-permute-start(bf16[2,64,2048]{2,1,0:T(8,128)(2,1)S(1)} %dynamic-slice_bitcast_fusion.14), channel_id=1, source_target_pairs={{0,4},{1,5},{2,6},{3,7},{4,0},{5,1},{6,2},{7,3},{8,12},{9,13},{10,... | collective-permute-start | bytes 1572872 | tf_op jit(solution)/shard_map/ppermute | solution.py:140
  567.9 39.0 %collective-permute-start.35 = (bf16[2,2,256,512]{3,2,1,0:T(8,128)(2,1)}, bf16[2,2,256,512]{3,2,1,0:T(8,128)(2,1)}, u32[]{:S(2)}, u32[]{:S(2)}) collective-permute-start(bf16[2,2,256,512]{3,2,1,0:T(8,128)(2,1)} %get-tuple-element.286), channel_id=1, source_target_pairs={{0,2},{1,3},{2,0},{3,1},{4,6},{5,7},{6,4},{7,5},{8,10},{9,11},{10,... | collective-permute-start | bytes 3145736 | tf_op jit(solution)/shard_map/ppermute | solution.py:140
  596.8 18.6 %collective-permute-start.38 = (bf16[256,704]{0,1:T(8,128)(2,1)S(1)}, bf16[256,704]{0,1:T(8,128)(2,1)S(1)}, u32[]{:S(2)}, u32[]{:S(2)}) collective-permute-start(bf16[256,704]{0,1:T(8,128)(2,1)S(1)} %bitcast.437), channel_id=1, source_target_pairs={{0,2},{1,3},{2,0},{3,1},{4,6},{5,7},{6,4},{7,5},{8,10},{9,11},{10,... | collective-permute-start | bytes 1081352 | tf_op jit(solution)/shard_map/ppermute | solution.py:140
  599.4 14.7 %collective-permute-start.37 = (bf16[64,2048]{1,0:T(8,128)(2,1)S(1)}, bf16[64,2048]{1,0:T(8,128)(2,1)S(1)}, u32[]{:S(2)}, u32[]{:S(2)}) collective-permute-start(bf16[64,2048]{1,0:T(8,128)(2,1)S(1)} %dynamic-slice_bitcast_fusion.18), channel_id=1, source_target_pairs={{0,8},{1,9},{2,10},{3,11},{4,12},{5,13},{6,14},{7,15},{8,0},{9,1},... | collective-permute-start | bytes 786440 | tf_op jit(solution)/shard_map/ppermute | solution.py:140
  600.2 19.7 %collective-permute-start.36 = (bf16[2,256,512]{2,1,0:T(8,128)(2,1)S(1)}, bf16[2,256,512]{2,1,0:T(8,128)(2,1)S(1)}, u32[]{:S(2)}, u32[]{:S(2)}) collective-permute-start(bf16[2,256,512]{2,1,0:T(8,128)(2,1)S(1)} %dynamic-slice_bitcast_fusion.13), channel_id=1, source_target_pairs={{0,4},{1,5},{2,6},{3,7},{4,0},{5,1},{6,2},{7,3},{8,12},{9,13},{10,... | collective-permute-start | bytes 1572872 | tf_op jit(solution)/shard_map/ppermute | solution.py:140
  605.2 37.8 %collective-permute-start.47 = (bf16[192,2048]{1,0:T(8,128)(2,1)}, bf16[192,2048]{1,0:T(8,128)(2,1)}, u32[]{:S(2)}, u32[]{:S(2)}) collective-permute-start(bf16[192,2048]{1,0:T(8,128)(2,1)} %slice.199), channel_id=1, source_target_pairs={{0,16},{1,17},{2,18},{3,19},{4,20},{5,21},{6,22},{7,23},{8,24},{9,... | collective-permute-start | bytes 2359304 | tf_op jit(solution)/shard_map/ppermute | solution.py:140
  606.9 34.5 %collective-permute-start.46 = (bf16[2,2,128,704]{2,3,1,0:T(8,128)(2,1)}, bf16[2,2,128,704]{2,3,1,0:T(8,128)(2,1)}, u32[]{:S(2)}, u32[]{:S(2)}) collective-permute-start(bf16[2,2,128,704]{2,3,1,0:T(8,128)(2,1)} %pad_maximum_fusion.21), channel_id=1, source_target_pairs={{0,16},{1,17},{2,18},{3,19},{4,20},{5,21},{6,22},{7,23},{8,24},{9,... | collective-permute-start | bytes 2162696 | tf_op jit(solution)/shard_map/ppermute | solution.py:140
  614.1 39.0 %collective-permute-start.39 = (bf16[2,2,256,512]{3,2,1,0:T(8,128)(2,1)}, bf16[2,2,256,512]{3,2,1,0:T(8,128)(2,1)}, u32[]{:S(2)}, u32[]{:S(2)}) collective-permute-start(bf16[2,2,256,512]{3,2,1,0:T(8,128)(2,1)} %get-tuple-element.285), channel_id=1, source_target_pairs={{0,2},{1,3},{2,0},{3,1},{4,6},{5,7},{6,4},{7,5},{8,10},{9,11},{10,... | collective-permute-start | bytes 3145736 | tf_op jit(solution)/shard_map/ppermute | solution.py:140
  620.9 42.1 %collective-permute-start.53 = (bf16[176,2048]{1,0:T(8,128)(2,1)S(1)}, bf16[176,2048]{1,0:T(8,128)(2,1)}, u32[]{:S(2)}, u32[]{:S(2)}) collective-permute-start(bf16[176,2048]{1,0:T(8,128)(2,1)S(1)} %copy-done.52), channel_id=1, source_target_pairs={{0,16},{1,17},{2,18},{3,19},{4,20},{5,21},{6,22},{7,23},{8,24},{9,... | collective-permute-start | bytes 2162696 | tf_op jit(solution)/shard_map/ppermute | solution.py:140
  624.8 28.2 %collective-permute-start.42 = (bf16[2,128,704]{1,2,0:T(8,128)(2,1)S(1)}, bf16[2,128,704]{1,2,0:T(8,128)(2,1)S(1)}, u32[]{:S(2)}, u32[]{:S(2)}) collective-permute-start(bf16[2,128,704]{1,2,0:T(8,128)(2,1)S(1)} %bitcast.438), channel_id=1, source_target_pairs={{0,1},{1,0},{2,3},{3,2},{4,5},{5,4},{6,7},{7,6},{8,9},{9,8},{10,11... | collective-permute-start | bytes 1081352 | tf_op jit(solution)/shard_map/ppermute | solution.py:140
  641.4 11.5 %collective-permute-start.41 = (bf16[256,512]{1,0:T(8,128)(2,1)S(1)}, bf16[256,512]{1,0:T(8,128)(2,1)S(1)}, u32[]{:S(2)}, u32[]{:S(2)}) collective-permute-start(bf16[256,512]{1,0:T(8,128)(2,1)S(1)} %dynamic-slice_bitcast_fusion.17), channel_id=1, source_target_pairs={{0,8},{1,9},{2,10},{3,11},{4,12},{5,13},{6,14},{7,15},{8,0},{9,1},... | collective-permute-start | bytes 786440 | tf_op jit(solution)/shard_map/ppermute | solution.py:140
  643.0 16.3 %collective-permute-start.40 = (bf16[2,256,512]{2,1,0:T(8,128)(2,1)S(1)}, bf16[2,256,512]{2,1,0:T(8,128)(2,1)S(1)}, u32[]{:S(2)}, u32[]{:S(2)}) collective-permute-start(bf16[2,256,512]{2,1,0:T(8,128)(2,1)S(1)} %dynamic-slice_bitcast_fusion.12), channel_id=1, source_target_pairs={{0,4},{1,5},{2,6},{3,7},{4,0},{5,1},{6,2},{7,3},{8,12},{9,13},{10,... | collective-permute-start | bytes 1572872 | tf_op jit(solution)/shard_map/ppermute | solution.py:140
  659.5 3.4 collective-permute-start.45
  659.6 14.9 %collective-permute-start.44 = (bf16[256,512]{1,0:T(8,128)(2,1)S(1)}, bf16[256,512]{1,0:T(8,128)(2,1)S(1)}, u32[]{:S(2)}, u32[]{:S(2)}) collective-permute-start(bf16[256,512]{1,0:T(8,128)(2,1)S(1)} %dynamic-slice_bitcast_fusion.16), channel_id=1, source_target_pairs={{0,8},{1,9},{2,10},{3,11},{4,12},{5,13},{6,14},{7,15},{8,0},{9,1},... | collective-permute-start | bytes 786440 | tf_op jit(solution)/shard_map/ppermute | solution.py:140
  659.9 20.5 %collective-permute-start.43 = (bf16[2,256,512]{2,1,0:T(8,128)(2,1)S(1)}, bf16[2,256,512]{2,1,0:T(8,128)(2,1)S(1)}, u32[]{:S(2)}, u32[]{:S(2)}) collective-permute-start(bf16[2,256,512]{2,1,0:T(8,128)(2,1)S(1)} %dynamic-slice_bitcast_fusion.11), channel_id=1, source_target_pairs={{0,4},{1,5},{2,6},{3,7},{4,0},{5,1},{6,2},{7,3},{8,12},{9,13},{10,... | collective-permute-start | bytes 1572872 | tf_op jit(solution)/shard_map/ppermute | solution.py:140
  662.4 20.8 %collective-permute-start.51 = (bf16[2,2,128,704]{2,3,1,0:T(8,128)(2,1)S(1)}, bf16[2,2,128,704]{2,3,1,0:T(8,128)(2,1)S(1)}, u32[]{:S(2)}, u32[]{:S(2)}) collective-permute-start(bf16[2,2,128,704]{2,3,1,0:T(8,128)(2,1)S(1)} %pad_maximum_fusion.23), channel_id=1, source_target_pairs={{0,16},{1,17},{2,18},{3,19},{4,20},{5,21},{6,22},{7,23},{8,24},{9,... | collective-permute-start | bytes 2162696 | tf_op jit(solution)/shard_map/ppermute | solution.py:140
  680.5 2.6 collective-permute-start.49
  680.7 17.7 %collective-permute-start.52 = (bf16[64,2048]{1,0:T(8,128)(2,1)}, bf16[64,2048]{1,0:T(8,128)(2,1)S(1)}, u32[]{:S(2)}, u32[]{:S(2)}) collective-permute-start(bf16[64,2048]{1,0:T(8,128)(2,1)} %fusion.205), channel_id=1, source_target_pairs={{0,16},{1,17},{2,18},{3,19},{4,20},{5,21},{6,22},{7,23},{8,24},{9,... | collective-permute-start | bytes 786440 | tf_op jit(solution)/shard_map/ppermute | solution.py:140
  681.2 14.1 %collective-permute-start.48 = (bf16[256,512]{1,0:T(8,128)(2,1)S(1)}, bf16[256,512]{1,0:T(8,128)(2,1)S(1)}, u32[]{:S(2)}, u32[]{:S(2)}) collective-permute-start(bf16[256,512]{1,0:T(8,128)(2,1)S(1)} %dynamic-slice_bitcast_fusion.15), channel_id=1, source_target_pairs={{0,8},{1,9},{2,10},{3,11},{4,12},{5,13},{6,14},{7,15},{8,0},{9,1},... | collective-permute-start | bytes 786440 | tf_op jit(solution)/shard_map/ppermute | solution.py:140
  681.5 15.6 %collective-permute-start.56 = (bf16[2,1,128,512]{3,2,0,1:T(8,128)(2,1)S(1)}, bf16[2,1,128,512]{3,2,0,1:T(8,128)(2,1)S(1)}, u32[]{:S(2)}, u32[]{:S(2)}) collective-permute-start(bf16[2,1,128,512]{3,2,0,1:T(8,128)(2,1)S(1)} %pad_maximum_fusion.29), channel_id=1, source_target_pairs={{0,16},{1,17},{2,18},{3,19},{4,20},{5,21},{6,22},{7,23},{8,24},{9,... | collective-permute-start | bytes 786440 | tf_op jit(solution)/shard_map/ppermute | solution.py:140
  695.4 4.1 collective-permute-start.50
  695.5 22.0 %collective-permute-start.54 = (bf16[2,1,128,512]{3,2,0,1:T(8,128)(2,1)S(1)}, bf16[2,1,128,512]{3,2,0,1:T(8,128)(2,1)}, u32[]{:S(2)}, u32[]{:S(2)}) collective-permute-start(bf16[2,1,128,512]{3,2,0,1:T(8,128)(2,1)S(1)} %bitcast.417), channel_id=1, source_target_pairs={{0,16},{1,17},{2,18},{3,19},{4,20},{5,21},{6,22},{7,23},{8,24},{9,... | collective-permute-start | bytes 786440 | tf_op jit(solution)/shard_map/ppermute | solution.py:140
  701.4 17.6 %collective-permute-start.55 = (bf16[2,1,128,512]{3,2,0,1:T(8,128)(2,1)}, bf16[2,1,128,512]{3,2,0,1:T(8,128)(2,1)}, u32[]{:S(2)}, u32[]{:S(2)}) collective-permute-start(bf16[2,1,128,512]{3,2,0,1:T(8,128)(2,1)} %bitcast.122), channel_id=1, source_target_pairs={{0,16},{1,17},{2,18},{3,19},{4,20},{5,21},{6,22},{7,23},{8,24},{9,... | collective-permute-start | bytes 786440 | tf_op jit(solution)/shard_map/ppermute | solution.py:140
  (99 other events, 703.5 us)
Sparse Core Ops, SparseCore 0:
  15.5 125.6 all-gather.3
  156.9 45.5 all-gather.7
  260.3 45.4 all-gather.5
  370.1 61.5 reduce-scatter.2
  458.1 63.2 reduce-scatter.4

commit v4 on v3

--- a/solution.py
+++ b/solution.py
@@ -310,13 +310,13 @@
     lines = lambda value: value.reshape(2 * CORES, rows, part)
     chip = at.merge(lines(kept), lines(at.swap(given, at.core)), at.core, 1).reshape(2, CORES * chip_rows, part)
     own_pair = at.trade(chip, at.low, 0)
-    mix_all, normed, same, own_pair, out_rows, grad_out_sent, own_down = fence(
-        mix_all, normed, same, own_pair, out_rows, grad_out, at.own_rep(ffn_down_weight)
-    )
-
-    all_grad_out = at.gather_group(grad_out_sent)
     pair_grid = own_pair.reshape(2, 2, chip_rows, part)
     gate_half, up_half = pair_grid[:, 0].reshape(-1, part), pair_grid[:, 1].reshape(-1, part)
+    mix_all, normed, same, gate_half, up_half, out_rows, grad_out_sent, own_down = fence(
+        mix_all, normed, same, gate_half, up_half, out_rows, grad_out, at.own_rep(ffn_down_weight)
+    )
+
+    all_grad_out = at.gather_group(grad_out_sent)
     for which in at.his:
         gate_half = at.extend(gate_half, which)
     mix_weight = lax.dynamic_slice_in_dim(mix_all, at.c * (3 * channels), 3 * channels, 1)
@@ -387,8 +387,9 @@
     inner_own = jnp.mean(grad_branch_own.astype(F32) * branch, axis=1)
     row_facts = at.gather_members(jnp.stack([state_scale.reshape(length), inner_own])[None], at.mixers)
     grad_branch = at.gather_members(grad_branch_own, at.mixers)
-    grad_branch, row_facts, up_line, gate_line = fence(grad_branch, row_facts, up_line, gate_line)
-
+    grad_branch, row_facts, up_line, gate_line, down_own = fence(grad_branch, row_facts, up_line, gate_line, down_own)
+
+    down_own = at.join_reps(down_own)
     gate_hi = fold_rest(at.end(*fold_begin(gate_line, at.his[-1])))
     all_scale = row_facts[:, 0].reshape(count * length, 1)
     all_inner = row_facts[:, 1].reshape(count * length, 1)
@@ -406,36 +407,37 @@
     grad_input_pre = (carried * (1.0 - forget) * input_slope).astype(BF16)
     grad_forget_pre = (grad_forget * forget * (1.0 - forget)).astype(BF16)
     cut_a, cut_b, cut_c = (plane(matmul(normed, g, (0, 0), BF16)) for g in (grad_gate_pre, grad_input_pre, grad_forget_pre))
-    out_keep, cut_a, cut_b, cut_c, up_line, gate_hi, ffn_out, down_own, grad_input_pre, grad_forget_pre = fence(
-        out_keep, cut_a, cut_b, cut_c, up_line, gate_hi, ffn_out, down_own, grad_input_pre, grad_forget_pre
+    triple = jnp.concatenate([grad_input_pre, grad_forget_pre, grad_gate_pre], axis=1)
+    normed_cut = matmul(triple, mix_weight, (1, 1), BF16)
+    out_keep, cut_a, cut_b, cut_c, up_line, gate_hi, ffn_out, down_own, normed_cut = fence(
+        out_keep, cut_a, cut_b, cut_c, up_line, gate_hi, ffn_out, down_own, normed_cut
     )
 
     sum_low = lambda cut: at.reduce(cut, at.low, 2)
     sum_lo = lambda line: at.reduce(line, at.lo, 1)
-    triple = jnp.concatenate([grad_input_pre, grad_forget_pre, grad_gate_pre], axis=1)
-    normed_cut = matmul(triple, mix_weight, (1, 1), BF16)
     gate_sets, out_low = mates(gate_hi), at.end(out_keep, out_other)
     keep_a, other_a = at.begin(cut_a, at.low, 2)
+    gate_sets, out_low, keep_a, cut_b, cut_c, up_line, normed_cut, down_own = fence(
+        gate_sets, out_low, keep_a, cut_b, cut_c, up_line, normed_cut, down_own
+    )
     up_keep, up_other = fold_begin(up_line, at.his[-1])
-    gate_sets, out_low, keep_a, cut_b, cut_c, up_keep, normed_cut, down_own = fence(
-        gate_sets, out_low, keep_a, cut_b, cut_c, up_keep, normed_cut, down_own
-    )
     keep_b, other_b = at.begin(cut_b, at.low, 2)
     normed_half = at.sum_members(normed_cut, [at.core])
-    low_a, out_lo, gate_cores, up_hi = at.end(keep_a, other_a), sum_lo(out_low), cores(gate_sets), fold_rest(at.end(up_keep, up_other))
-    low_a, out_lo, gate_cores, up_hi, keep_b, cut_c, normed_half, down_own = fence(
-        low_a, out_lo, gate_cores, up_hi, keep_b, cut_c, normed_half, down_own
-    )
+    low_a, out_lo, gate_cores = at.end(keep_a, other_a), sum_lo(out_low), cores(gate_sets)
+    low_a, out_lo, gate_cores, up_keep, keep_b, cut_c, normed_half, down_own = fence(
+        low_a, out_lo, gate_cores, up_keep, keep_b, cut_c, normed_half, down_own
+    )
+    up_hi = fold_rest(at.end(up_keep, up_other))
     grad_normed = at.sum_members(normed_half, at.rep_bits, BF16)
-    up_sets, gate_own = mates(up_hi), at.join_reps(gate_cores)
+    up_sets = mates(up_hi)
     keep_c, other_c = at.begin(cut_c, at.low, 2)
     low_b, lo_a, out_own = at.end(keep_b, other_b), sum_lo(low_a), at.reduce_his(out_lo)
-    low_b, lo_a, out_own, keep_c, up_sets, down_own = fence(low_b, lo_a, out_own, keep_c, up_sets, down_own)
-    down_own = at.join_reps(down_own)
+    low_b, lo_a, out_own, keep_c, up_sets, gate_cores = fence(low_b, lo_a, out_own, keep_c, up_sets, gate_cores)
+    gate_own = at.join_reps(gate_cores)
     low_c, lo_b, hi_a, up_cores = at.end(keep_c, other_c), sum_lo(low_b), at.reduce_his(lo_a), cores(up_sets)
-    low_c, lo_b, hi_a, up_cores = fence(low_c, lo_b, hi_a, up_cores)
+    low_c, lo_b, hi_a, up_cores, grad_normed = fence(low_c, lo_b, hi_a, up_cores, grad_normed)
     up_own, lo_c, hi_b, own_a = at.join_reps(up_cores), sum_lo(low_c), at.reduce_his(lo_b), cores(hi_a)
-    lo_c, hi_b, own_a, out_own, gate_own, grad_normed = fence(lo_c, hi_b, own_a, out_own, gate_own, grad_normed)
+    lo_c, hi_b, own_a, out_own, gate_own = fence(lo_c, hi_b, own_a, out_own, gate_own)
     hi_c, own_b, own_a, out_own = at.reduce_his(lo_c), cores(hi_b), at.join_reps(own_a), at.join_reps(out_own)
     hi_c, own_b = fence(hi_c, own_b)
     own_c, own_b = cores(hi_c), at.join_reps(own_b)

time: 743 us -> 723 us (0.973)
  waiting for transfers between devices: 310 us -> 284 us
    ppermute x57, waiting for transfers between devices: 309 us -> 284 us  [swap(): lax.ppermute(value, AXES, [(n, n ^ flip) for n in range(self.reps * self....]
    another operation x43 -> x41, other arithmetic: 23.6 us -> 20.1 us  [merge(): jnp.stack([jnp.where(first, own, other), jnp.where(first, other, own)], a...]
    unnamed x214 -> x233, local copies, waits for them, and re-layouts: 23.2 us -> 25.8 us
  transfers between devices with their start and end apart: 62 -> 62, of which waited for: 27 -> 28; matrix products, arithmetic and copies ran while one was open for 36% -> 37% of each run, Pallas kernels for 1% -> 1%
where the time goes in v4:
time: 723 us; the launch traced here: 718 us
  waiting for transfers between devices  284 us (39%)
  matrix products  128 us (18%)
  other arithmetic  109 us (15%)
  local copies, waits for them, and re-layouts  84.3 us (12%)
  starting transfers between devices  59.9 us (8%)
  blocking collectives  29.3 us (4%)
  between operations  16.2 us (2%)
  Pallas kernels  7.26 us (1%)
    ppermute x57, waiting for transfers between devices, swap(): lax.ppermute(value, AXES, [(n, n ^ flip) for n in range(self.reps * self....  284 us
    dot_general x23, matrix products, matmul(): lax.dot_general(left, right, ((dims[:1], dims[1:]), ((), ())), preferred_...  128 us
    ppermute x57, starting transfers between devices, swap(): lax.ppermute(value, AXES, [(n, n ^ flip) for n in range(self.reps * self....  59.4 us
    all_gather x1, blocking collectives, shards(): gains = lax.all_gather(own_gains, 'shard', axis=1, tiled=True).astype(F32)  29.3 us
    unnamed x233, local copies, waits for them, and re-layouts  25.8 us
    another operation x41, other arithmetic, merge(): jnp.stack([jnp.where(first, own, other), jnp.where(first, other, own)], a...  20.1 us
  transfers between devices with their start and end apart: 62, of which 28 were waited for; matrix products, arithmetic and copies ran while one was open for 37% of the time, Pallas kernels for 1%

profile of v4, /device:TPU:0, one launch (start us, length us, event | category | flops | bytes accessed | tf_op | source)
XLA Modules:
  0.0 718.3 jit_solution(11131405092945482010)
XLA Ops:
  7.3 3.4 fusion.174
  12.2 3.2 copy.179
  16.4 4.0 collective-permute-start.2
  22.1 3.4 fusion.182
  25.6 3.4 fusion.188
  33.5 5.0 fusion.179
  38.6 3.4 fusion.185
  42.1 7.8 %collective-permute-done.3 = s32[1,192]{1,0:T(1,128)} collective-permute-done((s32[1,192]{1,0:T(1,128)}, s32[1,192]{1,0:T(1,128)}, u32[]{:S(2)}, u32[]{:S(2)}) %collective-permute-start.3) | collective-permute-done | bytes 800 | tf_op jit(solution)/shard_map/ppermute | solution.py:140
  55.4 29.3 %all_gather.13 = bf16[3,2048]{1,0:T(4,128)(2,1)S(1)} all-gather(bf16[3,128]{1,0:T(4,128)(2,1)S(1)} %pad_maximum_fusion.33), channel_id=1, replica_groups=mesh['rep'=2,'shard'=16] {'shard'}, dimensions={1}, use_global_device_ids=true | all-gather | bytes 13056 | tf_op jit(solution)/shard_map/all_gather | solution.py:305
  95.4 2.6 collective-permute-start.6
  102.7 22.0 %collective-permute-done.6 = bf16[512,704]{0,1:T(8,128)(2,1)} collective-permute-done((bf16[512,704]{0,1:T(8,128)(2,1)}, bf16[512,704]{0,1:T(8,128)(2,1)}, u32[]{:S(2)}, u32[]{:S(2)}) %collective-permute-start.6) | collective-permute-done | bytes 720928 | tf_op jit(solution)/shard_map/ppermute | solution.py:140
  127.0 2.8 stack.221
  129.8 2.8 stack.222
  142.1 4.9 collective-permute-done.8
  151.8 5.2 fusion.118
  159.7 8.4 %fusion.121 = f32[768,1536]{1,0:T(8,128)S(1)} fusion(bf16[768,2048]{1,0:T(8,128)(2,1)} %fusion.118, bf16[2048,3072]{0,1:T(8,128)(2,1)} %all-gather.4.cloned.1.call-done, s32[]{:T(128)S(6)} %select_n.686), kind=kOutput, calls=%fused_computation.142 | convolution fusion | flops 4831838208 | bytes 14155780 | tf_op jit(solution)/shard_map/dot_general | solution.py:33
  171.8 3.9 convolution_convert_fusion.1
  175.7 16.3 %collective-permute-done.9 = bf16[512,704]{0,1:T(8,128)(2,1)} collective-permute-done((bf16[512,704]{0,1:T(8,128)(2,1)}, bf16[512,704]{0,1:T(8,128)(2,1)}, u32[]{:S(2)}, u32[]{:S(2)}) %collective-permute-start.9) | collective-permute-done | bytes 720928 | tf_op jit(solution)/shard_map/ppermute | solution.py:140
  195.2 3.4 collective-permute-start.15
  198.6 2.6 convert_add_fusion.1
  204.0 17.3 %collective-permute-done.13 = f32[1,192]{1,0:T(1,128)S(1)} collective-permute-done((f32[1,192]{1,0:T(1,128)S(1)}, f32[1,192]{1,0:T(1,128)S(1)}, u32[]{:S(2)}, u32[]{:S(2)}) %collective-permute-start.13) | collective-permute-done | bytes 800 | tf_op jit(solution)/shard_map/ppermute | solution.py:140
  221.3 21.0 %collective-permute-done.15 = bf16[512,704]{0,1:T(8,128)(2,1)S(1)} collective-permute-done((bf16[512,704]{0,1:T(8,128)(2,1)}, bf16[512,704]{0,1:T(8,128)(2,1)S(1)}, u32[]{:S(2)}, u32[]{:S(2)}) %collective-permute-start.15) | collective-permute-done | bytes 720928 | tf_op jit(solution)/shard_map/ppermute | solution.py:140
  244.3 3.3 pad_maximum_fusion.2
  253.0 2.6 collective-permute-start.17
  256.9 30.6 %collective-permute-done.17 = bf16[176,2048]{1,0:T(8,128)(2,1)S(1)} collective-permute-done((bf16[176,2048]{1,0:T(8,128)(2,1)}, bf16[176,2048]{1,0:T(8,128)(2,1)S(1)}, u32[]{:S(2)}, u32[]{:S(2)}) %collective-permute-start.17) | collective-permute-done | bytes 720928 | tf_op jit(solution)/shard_map/ppermute | solution.py:140
  290.0 12.9 %collective-permute-done.16 = bf16[1024,704]{0,1:T(8,128)(2,1)S(1)} collective-permute-done((bf16[1024,704]{0,1:T(8,128)(2,1)}, bf16[1024,704]{0,1:T(8,128)(2,1)S(1)}, u32[]{:S(2)}, u32[]{:S(2)}) %collective-permute-start.16) | collective-permute-done | bytes 1441824 | tf_op jit(solution)/shard_map/ppermute | solution.py:140
  306.5 8.6 %fusion.284 = f32[1536,704]{0,1:T(8,128)S(1)} fusion(bf16[1536,2048]{1,0:T(8,128)(2,1)} %all-gather.6.cloned.1.call-done, bf16[2048,704]{0,1:T(8,128)(2,1)} %pad_maximum_fusion.2), kind=kOutput, calls=%fused_computation.541 | convolution fusion | flops 4429185024 | bytes 13500416 | tf_op jit(solution)/shard_map/dot_general | solution.py:33
  315.1 6.6 multiply_convert_fusion.2
  321.8 6.0 convolution_convert_fusion.4
  327.8 10.7 %collective-permute-done.18 = bf16[2,176,2048]{2,1,0:T(8,128)(2,1)S(1)} collective-permute-done((bf16[2,176,2048]{2,1,0:T(8,128)(2,1)}, bf16[2,176,2048]{2,1,0:T(8,128)(2,1)S(1)}, u32[]{:S(2)}, u32[]{:S(2)}) %collective-permute-start.18) | collective-permute-done | bytes 1441824 | tf_op jit(solution)/shard_map/ppermute | solution.py:140
  339.0 10.0 %multiply_convert_fusion.1 = (bf16[1536,704]{0,1:T(8,128)(2,1)}, bf16[1536,704]{0,1:T(8,128)(2,1)S(1)}) fusion(f32[1536,704]{0,1:T(8,128)S(1)} %fusion.284, f32[1536,704]{0,1:T(8,128)} %get-tuple-element.350, bf16[1536,2048]{1,0:T(8,128)(2,1)S(1)} %bitcast.451, bf16[704,2048]{1,0:T(8,128)(2,1)S(1)} %bitcast.405), kind=kOutput, calls=%fused_computation.145 | convolution fusion | flops 4443242496 | bytes 22151168 | tf_op jit(solution)/shard_map/dot_general | solution.py:33
  349.0 5.1 fusion.285
  354.2 8.6 %add_convert_fusion = bf16[1536,2048]{1,0:T(8,128)(2,1)} fusion(f32[1536,2048]{1,0:T(8,128)S(1)} %fusion.285, bf16[1536,704]{0,1:T(8,128)(2,1)} %get-tuple-element.131, bf16[2048,704]{0,1:T(8,128)(2,1)S(1)} %copy-done.47), kind=kOutput, calls=%fused_computation.56 | convolution fusion | flops 4435476480 | bytes 23920640 | tf_op jit(solution)/shard_map/dot_general | solution.py:33
  362.9 2.8 dynamic-slice_bitcast_fusion
  366.3 10.2 %convolution_convert_fusion.2 = bf16[2048,704]{0,1:T(8,128)(2,1)} fusion(bf16[1536,704]{0,1:T(8,128)(2,1)S(1)} %copy-done.97, bf16[1536,2048]{1,0:T(8,128)(2,1)} %all-gather.6.cloned.1.call-done), kind=kOutput, calls=%fused_computation.168 | convolution fusion | flops 4430626816 | bytes 11337728 | tf_op jit(solution)/shard_map/dot_general | solution.py:33
  376.5 4.8 convolution_convert_fusion.3
  385.4 7.0 convolution_convert_fusion
  392.4 8.1 %collective-permute-done.20 = bf16[2,176,2048]{2,1,0:T(8,128)(2,1)} collective-permute-done((bf16[2,176,2048]{2,1,0:T(8,128)(2,1)}, bf16[2,176,2048]{2,1,0:T(8,128)(2,1)}, u32[]{:S(2)}, u32[]{:S(2)}) %collective-permute-start.20) | collective-permute-done | bytes 1441824 | tf_op jit(solution)/shard_map/ppermute | solution.py:140
  408.0 37.1 %collective-permute-done.19 = bf16[1024,704]{0,1:T(8,128)(2,1)} collective-permute-done((bf16[1024,704]{0,1:T(8,128)(2,1)}, bf16[1024,704]{0,1:T(8,128)(2,1)}, u32[]{:S(2)}, u32[]{:S(2)}) %collective-permute-start.19) | collective-permute-done | bytes 1441824 | tf_op jit(solution)/shard_map/ppermute | solution.py:140
  445.1 3.5 add_convert_fusion.2
  459.9 14.8 %collective-permute-done.22 = bf16[192,2048]{1,0:T(8,128)(2,1)S(1)} collective-permute-done((bf16[192,2048]{1,0:T(8,128)(2,1)S(1)}, bf16[192,2048]{1,0:T(8,128)(2,1)S(1)}, u32[]{:S(2)}, u32[]{:S(2)}) %collective-permute-start.22) | collective-permute-done | bytes 786464 | tf_op jit(solution)/shard_map/ppermute | solution.py:140
  485.6 2.7 copy.212
  491.5 3.2 add_convert_fusion.1
  494.7 3.4 pad_maximum_fusion.1
  500.8 4.6 convolution_convert_fusion.8
  508.1 3.9 subtract_multiply_fusion
  515.5 3.2 convolution_convert_fusion.5
  518.7 3.2 convolution_convert_fusion.6
  521.9 3.2 convolution_convert_fusion.7
  525.1 6.7 fusion.141
  541.8 2.6 add_convert_fusion.6
  544.4 5.0 collective-permute-done.29
  554.6 2.9 collective-permute-start.38
  560.9 19.7 %collective-permute-done.32 = bf16[2,64,2048]{2,1,0:T(8,128)(2,1)S(1)} collective-permute-done((bf16[2,64,2048]{2,1,0:T(8,128)(2,1)S(1)}, bf16[2,64,2048]{2,1,0:T(8,128)(2,1)S(1)}, u32[]{:S(2)}, u32[]{:S(2)}) %collective-permute-start.32) | collective-permute-done | bytes 524320 | tf_op jit(solution)/shard_map/ppermute | solution.py:140
  584.0 3.7 convert_add_fusion
  592.4 4.4 collective-permute-start.36
  606.9 4.9 collective-permute-done.36
  621.9 9.6 %collective-permute-done.42 = bf16[256,512]{1,0:T(8,128)(2,1)S(1)} collective-permute-done((bf16[256,512]{1,0:T(8,128)(2,1)S(1)}, bf16[256,512]{1,0:T(8,128)(2,1)S(1)}, u32[]{:S(2)}, u32[]{:S(2)}) %collective-permute-start.42) | collective-permute-done | bytes 262176 | tf_op jit(solution)/shard_map/ppermute | solution.py:140
  633.4 4.9 collective-permute-done.41
  643.6 9.4 %collective-permute-done.46 = bf16[256,512]{1,0:T(8,128)(2,1)S(1)} collective-permute-done((bf16[256,512]{1,0:T(8,128)(2,1)S(1)}, bf16[256,512]{1,0:T(8,128)(2,1)S(1)}, u32[]{:S(2)}, u32[]{:S(2)}) %collective-permute-start.46) | collective-permute-done | bytes 262176 | tf_op jit(solution)/shard_map/ppermute | solution.py:140
  653.0 5.8 collective-permute-done.45
  662.0 12.7 %collective-permute-done.49 = bf16[256,512]{1,0:T(8,128)(2,1)S(1)} collective-permute-done((bf16[256,512]{1,0:T(8,128)(2,1)S(1)}, bf16[256,512]{1,0:T(8,128)(2,1)S(1)}, u32[]{:S(2)}, u32[]{:S(2)}) %collective-permute-start.49) | collective-permute-done | bytes 262176 | tf_op jit(solution)/shard_map/ppermute | solution.py:140
  691.2 3.5 copy.216
  703.8 5.4 fusion.11
  (528 shorter events, 204.2 us)
Async XLA Ops:
  7.2 149.8 %all-gather.4.cloned.1.call-start = ((), (), s32[]{:S(2)}) async-start(), calls=%async_computation.2 | async-start | bytes 13369344 | tf_op jit(solution)/shard_map/all_gather | solution.py:280
  15.4 289.3 %all-gather.8.cloned.1.call-start = ((), (), s32[]{:S(2)}) async-start(), calls=%async_computation.4 | async-start | bytes 7077888 | tf_op jit(solution)/shard_map/all_gather | solution.py:224
  16.4 36.3 %collective-permute-start.2 = (bf16[64,2048]{1,0:T(8,128)(2,1)}, bf16[64,2048]{1,0:T(8,128)(2,1)}, u32[]{:S(2)}, u32[]{:S(2)}) collective-permute-start(bf16[64,2048]{1,0:T(8,128)(2,1)} %dynamic-slice_bitcast_fusion.19), channel_id=1, source_target_pairs={{0,8},{1,9},{2,10},{3,11},{4,12},{5,13},{6,14},{7,15},{8,0},{9,1},... | collective-permute-start | bytes 786440 | tf_op jit(solution)/shard_map/ppermute | solution.py:140
  29.9 54.9 %collective-permute-start.5 = (bf16[512,704]{0,1:T(8,128)(2,1)}, bf16[512,704]{0,1:T(8,128)(2,1)}, u32[]{:S(2)}, u32[]{:S(2)}) collective-permute-start(bf16[512,704]{0,1:T(8,128)(2,1)} %pad_maximum_fusion.18), channel_id=1, source_target_pairs={{0,1},{1,0},{2,3},{3,2},{4,5},{5,4},{6,7},{7,6},{8,9},{9,8},{10,11... | collective-permute-start | bytes 2162696 | tf_op jit(solution)/shard_map/ppermute | solution.py:140
  29.9 71.5 %collective-permute-start = (bf16[192,2048]{1,0:T(8,128)(2,1)S(1)}, bf16[192,2048]{1,0:T(8,128)(2,1)S(1)}, u32[]{:S(2)}, u32[]{:S(2)}) collective-permute-start(bf16[192,2048]{1,0:T(8,128)(2,1)S(1)} %bitcast.387), channel_id=1, source_target_pairs={{0,16},{1,17},{2,18},{3,19},{4,20},{5,21},{6,22},{7,23},{8,24},{9,... | collective-permute-start | bytes 2359304 | tf_op jit(solution)/shard_map/ppermute | solution.py:140
  31.4 18.5 %collective-permute-start.3 = (s32[1,192]{1,0:T(1,128)}, s32[1,192]{1,0:T(1,128)}, u32[]{:S(2)}, u32[]{:S(2)}) collective-permute-start(s32[1,192]{1,0:T(1,128)} %param.14), channel_id=1, source_target_pairs={{0,16},{1,17},{2,18},{3,19},{4,20},{5,21},{6,22},{7,23},{8,24},{9,... | collective-permute-start | bytes 2312 | tf_op jit(solution)/shard_map/ppermute | solution.py:140
  50.6 1.2 collective-permute-start.4
  53.8 45.4 %collective-permute-start.7 = (bf16[2,64,2048]{2,1,0:T(8,128)(2,1)S(1)}, bf16[2,64,2048]{2,1,0:T(8,128)(2,1)}, u32[]{:S(2)}, u32[]{:S(2)}) collective-permute-start(bf16[2,64,2048]{2,1,0:T(8,128)(2,1)S(1)} %pad_maximum_fusion.23), channel_id=1, source_target_pairs={{0,4},{1,5},{2,6},{3,7},{4,0},{5,1},{6,2},{7,3},{8,12},{9,13},{10,... | collective-permute-start | bytes 1572872 | tf_op jit(solution)/shard_map/ppermute | solution.py:140
  84.8 67.0 %copy-start.69 = (f32[1,2048]{1,0:T(1,128)}, f32[1,2048]{1,0:T(1,128)S(1)}, u32[]{:S(2)}) copy-start(f32[1,2048]{1,0:T(1,128)S(1)} %get-tuple-element.348) | copy-start | bytes 24580
  95.4 29.2 %collective-permute-start.6 = (bf16[512,704]{0,1:T(8,128)(2,1)}, bf16[512,704]{0,1:T(8,128)(2,1)}, u32[]{:S(2)}, u32[]{:S(2)}) collective-permute-start(bf16[512,704]{0,1:T(8,128)(2,1)} %bitcast.430), channel_id=1, source_target_pairs={{0,2},{1,3},{2,0},{3,1},{4,6},{5,7},{6,4},{7,5},{8,10},{9,11},{10,... | collective-permute-start | bytes 2162696 | tf_op jit(solution)/shard_map/ppermute | solution.py:140
  101.4 45.6 %collective-permute-start.8 = (bf16[2,2,64,2048]{3,2,1,0:T(8,128)(2,1)}, bf16[2,2,64,2048]{3,2,1,0:T(8,128)(2,1)}, u32[]{:S(2)}, u32[]{:S(2)}) collective-permute-start(bf16[2,2,64,2048]{3,2,1,0:T(8,128)(2,1)} %pad_maximum_fusion.16), channel_id=1, source_target_pairs={{0,2},{1,3},{2,0},{3,1},{4,6},{5,7},{6,4},{7,5},{8,10},{9,11},{10,... | collective-permute-start | bytes 3145736 | tf_op jit(solution)/shard_map/ppermute | solution.py:140
  102.6 47.2 %collective-permute-start.1 = (bf16[384,2048]{1,0:T(8,128)(2,1)}, bf16[384,2048]{1,0:T(8,128)(2,1)}, u32[]{:S(2)}, u32[]{:S(2)}) collective-permute-start(bf16[384,2048]{1,0:T(8,128)(2,1)} %pad_maximum_fusion.6), channel_id=1, source_target_pairs={{0,1},{1,0},{2,3},{3,2},{4,5},{5,4},{6,7},{7,6},{8,9},{9,8},{10,11... | collective-permute-start | bytes 4718600 | tf_op jit(solution)/shard_map/ppermute | solution.py:140
  157.0 147.7 %all-gather.6.cloned.1.call-start = ((), (), s32[]{:S(2)}) async-start(), calls=%async_computation.3 | async-start | bytes 7077888 | tf_op jit(solution)/shard_map/all_gather | solution.py:224
  157.3 34.7 %collective-permute-start.9 = (bf16[512,704]{0,1:T(8,128)(2,1)}, bf16[512,704]{0,1:T(8,128)(2,1)}, u32[]{:S(2)}, u32[]{:S(2)}) collective-permute-start(bf16[512,704]{0,1:T(8,128)(2,1)} %bitcast.168), channel_id=1, source_target_pairs={{0,8},{1,9},{2,10},{3,11},{4,12},{5,13},{6,14},{7,15},{8,0},{9,1},... | collective-permute-start | bytes 2162696 | tf_op jit(solution)/shard_map/ppermute | solution.py:140
  194.7 3.8 collective-permute-start.10
  194.8 49.6 %collective-permute-start.14 = (bf16[1024,704]{0,1:T(8,128)(2,1)S(1)}, bf16[1024,704]{0,1:T(8,128)(2,1)}, u32[]{:S(2)}, u32[]{:S(2)}) collective-permute-start(bf16[1024,704]{0,1:T(8,128)(2,1)S(1)} %pad_maximum_fusion.10), channel_id=1, source_target_pairs={{0,4},{1,5},{2,6},{3,7},{4,0},{5,1},{6,2},{7,3},{8,12},{9,13},{10,... | collective-permute-start | bytes 4325384 | tf_op jit(solution)/shard_map/ppermute | solution.py:140
  195.2 47.1 %collective-permute-start.15 = (bf16[512,704]{0,1:T(8,128)(2,1)}, bf16[512,704]{0,1:T(8,128)(2,1)S(1)}, u32[]{:S(2)}, u32[]{:S(2)}) collective-permute-start(bf16[512,704]{0,1:T(8,128)(2,1)} %bitcast.409), channel_id=1, source_target_pairs={{0,8},{1,9},{2,10},{3,11},{4,12},{5,13},{6,14},{7,15},{8,0},{9,1},... | collective-permute-start | bytes 2162696 | tf_op jit(solution)/shard_map/ppermute | solution.py:140
  198.6 4.2 collective-permute-start.12
  201.3 46.3 %collective-permute-start.11 = (bf16[192,2048]{1,0:T(8,128)(2,1)S(1)}, bf16[192,2048]{1,0:T(8,128)(2,1)S(1)}, u32[]{:S(2)}, u32[]{:S(2)}) collective-permute-start(bf16[192,2048]{1,0:T(8,128)(2,1)S(1)} %slice.200), channel_id=1, source_target_pairs={{0,16},{1,17},{2,18},{3,19},{4,20},{5,21},{6,22},{7,23},{8,24},{9,... | collective-permute-start | bytes 2359304 | tf_op jit(solution)/shard_map/ppermute | solution.py:140
  202.8 18.5 %collective-permute-start.13 = (f32[1,192]{1,0:T(1,128)S(1)}, f32[1,192]{1,0:T(1,128)S(1)}, u32[]{:S(2)}, u32[]{:S(2)}) collective-permute-start(f32[1,192]{1,0:T(1,128)S(1)} %slice.146), channel_id=1, source_target_pairs={{0,16},{1,17},{2,18},{3,19},{4,20},{5,21},{6,22},{7,23},{8,24},{9,... | collective-permute-start | bytes 2312 | tf_op jit(solution)/shard_map/ppermute | solution.py:140
  253.0 197.8 %reduce-scatter.3.cloned.1.call-start = ((), (), s32[]{:S(2)}) async-start(), calls=%async_computation.5 | async-start | bytes 7077888 | tf_op jit(solution)/shard_map/reduce_scatter | solution.py:227
  253.0 49.9 %copy-start.29 = (bf16[1024,704]{0,1:T(8,128)(2,1)S(1)}, bf16[1024,704]{0,1:T(8,128)(2,1)}, u32[]{:S(2)}) copy-start(bf16[1024,704]{0,1:T(8,128)(2,1)} %pad_maximum_fusion.11) | copy-start | bytes 4325380
  253.0 34.5 %collective-permute-start.17 = (bf16[176,2048]{1,0:T(8,128)(2,1)}, bf16[176,2048]{1,0:T(8,128)(2,1)S(1)}, u32[]{:S(2)}, u32[]{:S(2)}) collective-permute-start(bf16[176,2048]{1,0:T(8,128)(2,1)} %dynamic-slice_bitcast_fusion.10), channel_id=1, source_target_pairs={{0,8},{1,9},{2,10},{3,11},{4,12},{5,13},{6,14},{7,15},{8,0},{9,1},... | collective-permute-start | bytes 2162696 | tf_op jit(solution)/shard_map/ppermute | solution.py:140
  255.6 47.2 %collective-permute-start.16 = (bf16[1024,704]{0,1:T(8,128)(2,1)}, bf16[1024,704]{0,1:T(8,128)(2,1)S(1)}, u32[]{:S(2)}, u32[]{:S(2)}) collective-permute-start(bf16[1024,704]{0,1:T(8,128)(2,1)} %pad_maximum_fusion.11), channel_id=1, source_target_pairs={{0,4},{1,5},{2,6},{3,7},{4,0},{5,1},{6,2},{7,3},{8,12},{9,13},{10,... | collective-permute-start | bytes 4325384 | tf_op jit(solution)/shard_map/ppermute | solution.py:140
  304.7 33.8 %collective-permute-start.18 = (bf16[2,176,2048]{2,1,0:T(8,128)(2,1)}, bf16[2,176,2048]{2,1,0:T(8,128)(2,1)S(1)}, u32[]{:S(2)}, u32[]{:S(2)}) collective-permute-start(bf16[2,176,2048]{2,1,0:T(8,128)(2,1)} %pad_maximum_fusion.12), channel_id=1, source_target_pairs={{0,4},{1,5},{2,6},{3,7},{4,0},{5,1},{6,2},{7,3},{8,12},{9,13},{10,... | collective-permute-start | bytes 4325384 | tf_op jit(solution)/shard_map/ppermute | solution.py:140
  362.8 171.0 %reduce-scatter.5.cloned.1.call-start = ((), (), s32[]{:S(2)}) async-start(), calls=%async_computation.6 | async-start | bytes 7077888 | tf_op jit(solution)/shard_map/reduce_scatter | solution.py:227
  365.7 34.8 %collective-permute-start.20 = (bf16[2,176,2048]{2,1,0:T(8,128)(2,1)}, bf16[2,176,2048]{2,1,0:T(8,128)(2,1)}, u32[]{:S(2)}, u32[]{:S(2)}) collective-permute-start(bf16[2,176,2048]{2,1,0:T(8,128)(2,1)} %dynamic-slice_bitcast_fusion), channel_id=1, source_target_pairs={{0,4},{1,5},{2,6},{3,7},{4,0},{5,1},{6,2},{7,3},{8,12},{9,13},{10,... | collective-permute-start | bytes 4325384 | tf_op jit(solution)/shard_map/ppermute | solution.py:140
  384.2 60.9 %collective-permute-start.19 = (bf16[1024,704]{0,1:T(8,128)(2,1)}, bf16[1024,704]{0,1:T(8,128)(2,1)}, u32[]{:S(2)}, u32[]{:S(2)}) collective-permute-start(bf16[1024,704]{0,1:T(8,128)(2,1)} %slice.149), channel_id=1, source_target_pairs={{0,4},{1,5},{2,6},{3,7},{4,0},{5,1},{6,2},{7,3},{8,12},{9,13},{10,... | collective-permute-start | bytes 4325384 | tf_op jit(solution)/shard_map/ppermute | solution.py:140
  404.9 43.7 %collective-permute-start.21 = (bf16[176,2048]{1,0:T(8,128)(2,1)}, bf16[176,2048]{1,0:T(8,128)(2,1)}, u32[]{:S(2)}, u32[]{:S(2)}) collective-permute-start(bf16[176,2048]{1,0:T(8,128)(2,1)} %dynamic-slice_bitcast_fusion.9), channel_id=1, source_target_pairs={{0,8},{1,9},{2,10},{3,11},{4,12},{5,13},{6,14},{7,15},{8,0},{9,1},... | collective-permute-start | bytes 2162696 | tf_op jit(solution)/shard_map/ppermute | solution.py:140
  457.0 17.7 %collective-permute-start.22 = (bf16[192,2048]{1,0:T(8,128)(2,1)S(1)}, bf16[192,2048]{1,0:T(8,128)(2,1)S(1)}, u32[]{:S(2)}, u32[]{:S(2)}) collective-permute-start(bf16[192,2048]{1,0:T(8,128)(2,1)S(1)} %get-tuple-element.269), channel_id=1, source_target_pairs={{0,16},{1,17},{2,18},{3,19},{4,20},{5,21},{6,22},{7,23},{8,24},{9,... | collective-permute-start | bytes 2359304 | tf_op jit(solution)/shard_map/ppermute | solution.py:140
  459.9 31.6 %collective-permute-start.26 = (bf16[1024,704]{0,1:T(8,128)(2,1)}, bf16[1024,704]{0,1:T(8,128)(2,1)}, u32[]{:S(2)}, u32[]{:S(2)}) collective-permute-start(bf16[1024,704]{0,1:T(8,128)(2,1)} %slice.122), channel_id=1, source_target_pairs={{0,4},{1,5},{2,6},{3,7},{4,0},{5,1},{6,2},{7,3},{8,12},{9,13},{10,... | collective-permute-start | bytes 4325384 | tf_op jit(solution)/shard_map/ppermute | solution.py:140
  476.0 18.7 %collective-permute-start.23 = (bf16[384,2048]{1,0:T(8,128)(2,1)}, bf16[384,2048]{1,0:T(8,128)(2,1)}, u32[]{:S(2)}, u32[]{:S(2)}) collective-permute-start(bf16[384,2048]{1,0:T(8,128)(2,1)} %pad_maximum_fusion.8), channel_id=1, source_target_pairs={{0,1},{1,0},{2,3},{3,2},{4,5},{5,4},{6,7},{7,6},{8,9},{9,8},{10,11... | collective-permute-start | bytes 4718600 | tf_op jit(solution)/shard_map/ppermute | solution.py:140
  478.5 4.0 collective-permute-start.24
  482.4 7.2 %collective-permute-start.25 = (f32[2,2,192]{2,1,0:T(2,128)S(1)}, f32[2,2,192]{2,1,0:T(2,128)S(1)}, u32[]{:S(2)}, u32[]{:S(2)}) collective-permute-start(f32[2,2,192]{2,1,0:T(2,128)S(1)} %pad_maximum_fusion.32), channel_id=1, source_target_pairs={{0,1},{1,0},{2,3},{3,2},{4,5},{5,4},{6,7},{7,6},{8,9},{9,8},{10,11... | collective-permute-start | bytes 9224 | tf_op jit(solution)/shard_map/ppermute | solution.py:140
  498.3 33.5 %collective-permute-start.28 = (bf16[176,2048]{1,0:T(8,128)(2,1)}, bf16[176,2048]{1,0:T(8,128)(2,1)S(1)}, u32[]{:S(2)}, u32[]{:S(2)}) collective-permute-start(bf16[176,2048]{1,0:T(8,128)(2,1)} %fusion.173), channel_id=1, source_target_pairs={{0,16},{1,17},{2,18},{3,19},{4,20},{5,21},{6,22},{7,23},{8,24},{9,... | collective-permute-start | bytes 2162696 | tf_op jit(solution)/shard_map/ppermute | solution.py:140
  500.7 32.9 %collective-permute-start.27 = (bf16[512,704]{0,1:T(8,128)(2,1)S(1)}, bf16[512,704]{0,1:T(8,128)(2,1)S(1)}, u32[]{:S(2)}, u32[]{:S(2)}) collective-permute-start(bf16[512,704]{0,1:T(8,128)(2,1)S(1)} %slice.127), channel_id=1, source_target_pairs={{0,8},{1,9},{2,10},{3,11},{4,12},{5,13},{6,14},{7,15},{8,0},{9,1},... | collective-permute-start | bytes 2162696 | tf_op jit(solution)/shard_map/ppermute | solution.py:140
  506.9 34.9 %collective-permute-start.30 = (bf16[2,2,64,2048]{3,2,1,0:T(8,128)(2,1)}, bf16[2,2,64,2048]{3,2,1,0:T(8,128)(2,1)}, u32[]{:S(2)}, u32[]{:S(2)}) collective-permute-start(bf16[2,2,64,2048]{3,2,1,0:T(8,128)(2,1)} %get-tuple-element.292), channel_id=1, source_target_pairs={{0,2},{1,3},{2,0},{3,1},{4,6},{5,7},{6,4},{7,5},{8,10},{9,11},{10,... | collective-permute-start | bytes 3145736 | tf_op jit(solution)/shard_map/ppermute | solution.py:140
  538.1 11.3 %collective-permute-start.29 = (bf16[256,704]{0,1:T(8,128)(2,1)S(1)}, bf16[256,704]{0,1:T(8,128)(2,1)S(1)}, u32[]{:S(2)}, u32[]{:S(2)}) collective-permute-start(bf16[256,704]{0,1:T(8,128)(2,1)S(1)} %bitcast.434), channel_id=1, source_target_pairs={{0,2},{1,3},{2,0},{3,1},{4,6},{5,7},{6,4},{7,5},{8,10},{9,11},{10,... | collective-permute-start | bytes 1081352 | tf_op jit(solution)/shard_map/ppermute | solution.py:140
  540.5 41.0 %collective-permute-start.31 = (bf16[2,2,256,512]{3,2,1,0:T(8,128)(2,1)}, bf16[2,2,256,512]{3,2,1,0:T(8,128)(2,1)}, u32[]{:S(2)}, u32[]{:S(2)}) collective-permute-start(bf16[2,2,256,512]{3,2,1,0:T(8,128)(2,1)} %get-tuple-element.291), channel_id=1, source_target_pairs={{0,2},{1,3},{2,0},{3,1},{4,6},{5,7},{6,4},{7,5},{8,10},{9,11},{10,... | collective-permute-start | bytes 3145736 | tf_op jit(solution)/shard_map/ppermute | solution.py:140
  550.9 33.1 %collective-permute-start.34 = (bf16[384,2048]{1,0:T(8,128)(2,1)}, bf16[384,2048]{1,0:T(8,128)(2,1)}, u32[]{:S(2)}, u32[]{:S(2)}) collective-permute-start(bf16[384,2048]{1,0:T(8,128)(2,1)} %slice.130), channel_id=1, source_target_pairs={{0,1},{1,0},{2,3},{3,2},{4,5},{5,4},{6,7},{7,6},{8,9},{9,8},{10,11... | collective-permute-start | bytes 4718600 | tf_op jit(solution)/shard_map/ppermute | solution.py:140
  552.6 6.4 collective-permute-start.33
  554.3 26.3 %collective-permute-start.32 = (bf16[2,64,2048]{2,1,0:T(8,128)(2,1)S(1)}, bf16[2,64,2048]{2,1,0:T(8,128)(2,1)S(1)}, u32[]{:S(2)}, u32[]{:S(2)}) collective-permute-start(bf16[2,64,2048]{2,1,0:T(8,128)(2,1)S(1)} %dynamic-slice_bitcast_fusion.14), channel_id=1, source_target_pairs={{0,4},{1,5},{2,6},{3,7},{4,0},{5,1},{6,2},{7,3},{8,12},{9,13},{10,... | collective-permute-start | bytes 1572872 | tf_op jit(solution)/shard_map/ppermute | solution.py:140
  554.6 34.8 %collective-permute-start.38 = (bf16[512,704]{0,1:T(8,128)(2,1)S(1)}, bf16[512,704]{0,1:T(8,128)(2,1)S(1)}, u32[]{:S(2)}, u32[]{:S(2)}) collective-permute-start(bf16[512,704]{0,1:T(8,128)(2,1)S(1)} %get-tuple-element.304), channel_id=1, source_target_pairs={{0,8},{1,9},{2,10},{3,11},{4,12},{5,13},{6,14},{7,15},{8,0},{9,1},... | collective-permute-start | bytes 2162696 | tf_op jit(solution)/shard_map/ppermute | solution.py:140
  559.0 42.8 %collective-permute-start.35 = (bf16[2,2,256,512]{3,2,1,0:T(8,128)(2,1)}, bf16[2,2,256,512]{3,2,1,0:T(8,128)(2,1)}, u32[]{:S(2)}, u32[]{:S(2)}) collective-permute-start(bf16[2,2,256,512]{3,2,1,0:T(8,128)(2,1)} %get-tuple-element.288), channel_id=1, source_target_pairs={{0,2},{1,3},{2,0},{3,1},{4,6},{5,7},{6,4},{7,5},{8,10},{9,11},{10,... | collective-permute-start | bytes 3145736 | tf_op jit(solution)/shard_map/ppermute | solution.py:140
  591.4 15.4 %collective-permute-start.39 = (bf16[256,704]{0,1:T(8,128)(2,1)S(1)}, bf16[256,704]{0,1:T(8,128)(2,1)S(1)}, u32[]{:S(2)}, u32[]{:S(2)}) collective-permute-start(bf16[256,704]{0,1:T(8,128)(2,1)S(1)} %bitcast.431), channel_id=1, source_target_pairs={{0,2},{1,3},{2,0},{3,1},{4,6},{5,7},{6,4},{7,5},{8,10},{9,11},{10,... | collective-permute-start | bytes 1081352 | tf_op jit(solution)/shard_map/ppermute | solution.py:140
  592.3 13.7 %collective-permute-start.37 = (bf16[64,2048]{1,0:T(8,128)(2,1)S(1)}, bf16[64,2048]{1,0:T(8,128)(2,1)S(1)}, u32[]{:S(2)}, u32[]{:S(2)}) collective-permute-start(bf16[64,2048]{1,0:T(8,128)(2,1)S(1)} %dynamic-slice_bitcast_fusion.18), channel_id=1, source_target_pairs={{0,8},{1,9},{2,10},{3,11},{4,12},{5,13},{6,14},{7,15},{8,0},{9,1},... | collective-permute-start | bytes 786440 | tf_op jit(solution)/shard_map/ppermute | solution.py:140
  592.4 19.4 %collective-permute-start.36 = (bf16[2,256,512]{2,1,0:T(8,128)(2,1)S(1)}, bf16[2,256,512]{2,1,0:T(8,128)(2,1)S(1)}, u32[]{:S(2)}, u32[]{:S(2)}) collective-permute-start(bf16[2,256,512]{2,1,0:T(8,128)(2,1)S(1)} %dynamic-slice_bitcast_fusion.13), channel_id=1, source_target_pairs={{0,4},{1,5},{2,6},{3,7},{4,0},{5,1},{6,2},{7,3},{8,12},{9,13},{10,... | collective-permute-start | bytes 1572872 | tf_op jit(solution)/shard_map/ppermute | solution.py:140
  599.2 20.8 %collective-permute-start.44 = (bf16[192,2048]{1,0:T(8,128)(2,1)}, bf16[192,2048]{1,0:T(8,128)(2,1)}, u32[]{:S(2)}, u32[]{:S(2)}) collective-permute-start(bf16[192,2048]{1,0:T(8,128)(2,1)} %slice.199), channel_id=1, source_target_pairs={{0,16},{1,17},{2,18},{3,19},{4,20},{5,21},{6,22},{7,23},{8,24},{9,... | collective-permute-start | bytes 2359304 | tf_op jit(solution)/shard_map/ppermute | solution.py:140
  601.8 29.9 %collective-permute-start.40 = (bf16[2,2,256,512]{3,2,1,0:T(8,128)(2,1)}, bf16[2,2,256,512]{3,2,1,0:T(8,128)(2,1)}, u32[]{:S(2)}, u32[]{:S(2)}) collective-permute-start(bf16[2,2,256,512]{3,2,1,0:T(8,128)(2,1)} %get-tuple-element.287), channel_id=1, source_target_pairs={{0,2},{1,3},{2,0},{3,1},{4,6},{5,7},{6,4},{7,5},{8,10},{9,11},{10,... | collective-permute-start | bytes 3145736 | tf_op jit(solution)/shard_map/ppermute | solution.py:140
  612.7 29.2 %collective-permute-start.48 = (bf16[2,2,128,704]{2,3,1,0:T(8,128)(2,1)}, bf16[2,2,128,704]{2,3,1,0:T(8,128)(2,1)}, u32[]{:S(2)}, u32[]{:S(2)}) collective-permute-start(bf16[2,2,128,704]{2,3,1,0:T(8,128)(2,1)} %pad_maximum_fusion.20), channel_id=1, source_target_pairs={{0,16},{1,17},{2,18},{3,19},{4,20},{5,21},{6,22},{7,23},{8,24},{9,... | collective-permute-start | bytes 2162696 | tf_op jit(solution)/shard_map/ppermute | solution.py:140
  616.3 15.2 %collective-permute-start.43 = (bf16[2,128,704]{1,2,0:T(8,128)(2,1)S(1)}, bf16[2,128,704]{1,2,0:T(8,128)(2,1)S(1)}, u32[]{:S(2)}, u32[]{:S(2)}) collective-permute-start(bf16[2,128,704]{1,2,0:T(8,128)(2,1)S(1)} %bitcast.432), channel_id=1, source_target_pairs={{0,1},{1,0},{2,3},{3,2},{4,5},{5,4},{6,7},{7,6},{8,9},{9,8},{10,11... | collective-permute-start | bytes 1081352 | tf_op jit(solution)/shard_map/ppermute | solution.py:140
  616.4 15.0 %collective-permute-start.42 = (bf16[256,512]{1,0:T(8,128)(2,1)S(1)}, bf16[256,512]{1,0:T(8,128)(2,1)S(1)}, u32[]{:S(2)}, u32[]{:S(2)}) collective-permute-start(bf16[256,512]{1,0:T(8,128)(2,1)S(1)} %dynamic-slice_bitcast_fusion.17), channel_id=1, source_target_pairs={{0,8},{1,9},{2,10},{3,11},{4,12},{5,13},{6,14},{7,15},{8,0},{9,1},... | collective-permute-start | bytes 786440 | tf_op jit(solution)/shard_map/ppermute | solution.py:140
  620.0 18.3 %collective-permute-start.41 = (bf16[2,256,512]{2,1,0:T(8,128)(2,1)S(1)}, bf16[2,256,512]{2,1,0:T(8,128)(2,1)S(1)}, u32[]{:S(2)}, u32[]{:S(2)}) collective-permute-start(bf16[2,256,512]{2,1,0:T(8,128)(2,1)S(1)} %dynamic-slice_bitcast_fusion.12), channel_id=1, source_target_pairs={{0,4},{1,5},{2,6},{3,7},{4,0},{5,1},{6,2},{7,3},{8,12},{9,13},{10,... | collective-permute-start | bytes 1572872 | tf_op jit(solution)/shard_map/ppermute | solution.py:140
  638.5 3.4 collective-permute-start.47
  638.6 14.4 %collective-permute-start.46 = (bf16[256,512]{1,0:T(8,128)(2,1)S(1)}, bf16[256,512]{1,0:T(8,128)(2,1)S(1)}, u32[]{:S(2)}, u32[]{:S(2)}) collective-permute-start(bf16[256,512]{1,0:T(8,128)(2,1)S(1)} %dynamic-slice_bitcast_fusion.16), channel_id=1, source_target_pairs={{0,8},{1,9},{2,10},{3,11},{4,12},{5,13},{6,14},{7,15},{8,0},{9,1},... | collective-permute-start | bytes 786440 | tf_op jit(solution)/shard_map/ppermute | solution.py:140
  638.7 20.1 %collective-permute-start.45 = (bf16[2,256,512]{2,1,0:T(8,128)(2,1)S(1)}, bf16[2,256,512]{2,1,0:T(8,128)(2,1)S(1)}, u32[]{:S(2)}, u32[]{:S(2)}) collective-permute-start(bf16[2,256,512]{2,1,0:T(8,128)(2,1)S(1)} %dynamic-slice_bitcast_fusion.11), channel_id=1, source_target_pairs={{0,4},{1,5},{2,6},{3,7},{4,0},{5,1},{6,2},{7,3},{8,12},{9,13},{10,... | collective-permute-start | bytes 1572872 | tf_op jit(solution)/shard_map/ppermute | solution.py:140
  640.9 20.7 %collective-permute-start.52 = (bf16[2,2,128,704]{2,3,1,0:T(8,128)(2,1)S(1)}, bf16[2,2,128,704]{2,3,1,0:T(8,128)(2,1)S(1)}, u32[]{:S(2)}, u32[]{:S(2)}) collective-permute-start(bf16[2,2,128,704]{2,3,1,0:T(8,128)(2,1)S(1)} %pad_maximum_fusion.22), channel_id=1, source_target_pairs={{0,16},{1,17},{2,18},{3,19},{4,20},{5,21},{6,22},{7,23},{8,24},{9,... | collective-permute-start | bytes 2162696 | tf_op jit(solution)/shard_map/ppermute | solution.py:140
  659.0 2.6 collective-permute-start.50
  659.1 18.2 %collective-permute-start.53 = (bf16[64,2048]{1,0:T(8,128)(2,1)}, bf16[64,2048]{1,0:T(8,128)(2,1)S(1)}, u32[]{:S(2)}, u32[]{:S(2)}) collective-permute-start(bf16[64,2048]{1,0:T(8,128)(2,1)} %fusion.203), channel_id=1, source_target_pairs={{0,16},{1,17},{2,18},{3,19},{4,20},{5,21},{6,22},{7,23},{8,24},{9,... | collective-permute-start | bytes 786440 | tf_op jit(solution)/shard_map/ppermute | solution.py:140
  660.2 14.5 %collective-permute-start.49 = (bf16[256,512]{1,0:T(8,128)(2,1)S(1)}, bf16[256,512]{1,0:T(8,128)(2,1)S(1)}, u32[]{:S(2)}, u32[]{:S(2)}) collective-permute-start(bf16[256,512]{1,0:T(8,128)(2,1)S(1)} %dynamic-slice_bitcast_fusion.15), channel_id=1, source_target_pairs={{0,8},{1,9},{2,10},{3,11},{4,12},{5,13},{6,14},{7,15},{8,0},{9,1},... | collective-permute-start | bytes 786440 | tf_op jit(solution)/shard_map/ppermute | solution.py:140
  660.5 15.5 %collective-permute-start.56 = (bf16[2,1,128,512]{3,2,0,1:T(8,128)(2,1)S(1)}, bf16[2,1,128,512]{3,2,0,1:T(8,128)(2,1)S(1)}, u32[]{:S(2)}, u32[]{:S(2)}) collective-permute-start(bf16[2,1,128,512]{3,2,0,1:T(8,128)(2,1)S(1)} %pad_maximum_fusion.28), channel_id=1, source_target_pairs={{0,16},{1,17},{2,18},{3,19},{4,20},{5,21},{6,22},{7,23},{8,24},{9,... | collective-permute-start | bytes 786440 | tf_op jit(solution)/shard_map/ppermute | solution.py:140
  674.8 3.6 collective-permute-start.51
  674.9 22.8 %collective-permute-start.54 = (bf16[2,1,128,512]{3,2,0,1:T(8,128)(2,1)S(1)}, bf16[2,1,128,512]{3,2,0,1:T(8,128)(2,1)}, u32[]{:S(2)}, u32[]{:S(2)}) collective-permute-start(bf16[2,1,128,512]{3,2,0,1:T(8,128)(2,1)S(1)} %bitcast.411), channel_id=1, source_target_pairs={{0,16},{1,17},{2,18},{3,19},{4,20},{5,21},{6,22},{7,23},{8,24},{9,... | collective-permute-start | bytes 786440 | tf_op jit(solution)/shard_map/ppermute | solution.py:140
  680.3 18.9 %collective-permute-start.55 = (bf16[2,1,128,512]{3,2,0,1:T(8,128)(2,1)}, bf16[2,1,128,512]{3,2,0,1:T(8,128)(2,1)}, u32[]{:S(2)}, u32[]{:S(2)}) collective-permute-start(bf16[2,1,128,512]{3,2,0,1:T(8,128)(2,1)} %bitcast.120), channel_id=1, source_target_pairs={{0,16},{1,17},{2,18},{3,19},{4,20},{5,21},{6,22},{7,23},{8,24},{9,... | collective-permute-start | bytes 786440 | tf_op jit(solution)/shard_map/ppermute | solution.py:140
  (108 other events, 727.8 us)
Sparse Core Ops, SparseCore 0:
  15.5 124.6 all-gather.3
  157.1 45.5 all-gather.7
  253.1 45.4 all-gather.5
  363.0 61.5 reduce-scatter.2
  450.9 68.5 reduce-scatter.4

commit v5 on v4

--- a/solution.py
+++ b/solution.py
@@ -301,12 +301,15 @@
     same = same.reshape(count * length, 1)
     out_lines = at.join_his(at.own_rep(out_weight))
     out_lines, own_gains = fence(out_lines, jnp.stack([norm_gain, mixer_gain, ffn_gain]))
-    out_rows = at.join(at.join(out_lines, at.lo, 1), at.low, 2).reshape(channels, width)
+    out_lines = at.join(out_lines, at.lo, 1)
+    out_other = at.swap(out_lines, at.low)
     gains = lax.all_gather(own_gains, "shard", axis=1, tiled=True).astype(F32)
     gain_one, gain_two, gain_three = gains[0], gains[1], gains[2]
     gain_grid = gain_two.reshape(at.chips, CORES, reps, small)
     gain_mix = lax.dynamic_index_in_dim(lax.dynamic_index_in_dim(gain_grid, at.c, 1, keepdims=False), at.r, 1, keepdims=False).reshape(-1)
     normed = (normalize(all_tokens.astype(F32))[0] * gain_one).astype(BF16)
+    out_lines, normed = fence(out_lines, normed)
+    out_rows = at.merge(out_lines, out_other, at.low, 2).reshape(channels, width)
     lines = lambda value: value.reshape(2 * CORES, rows, part)
     chip = at.merge(lines(kept), lines(at.swap(given, at.core)), at.core, 1).reshape(2, CORES * chip_rows, part)
     own_pair = at.trade(chip, at.low, 0)
@@ -413,6 +416,13 @@
         out_keep, cut_a, cut_b, cut_c, up_line, gate_hi, ffn_out, down_own, normed_cut
     )
 
+    def whole_units(own):
+        grid = own.reshape(reps, CORES, 2, rows, at.length, slim)
+        return grid.transpose(3, 4, 2, 1, 0, 5).reshape(rows, units).astype(F32)
+
+    def whole_rows(own):
+        return own.reshape(-1, width).astype(F32)
+
     sum_low = lambda cut: at.reduce(cut, at.low, 2)
     sum_lo = lambda line: at.reduce(line, at.lo, 1)
     gate_sets, out_low = mates(gate_hi), at.end(out_keep, out_other)
@@ -437,11 +447,11 @@
     low_c, lo_b, hi_a, up_cores = at.end(keep_c, other_c), sum_lo(low_b), at.reduce_his(lo_a), cores(up_sets)
     low_c, lo_b, hi_a, up_cores, grad_normed = fence(low_c, lo_b, hi_a, up_cores, grad_normed)
     up_own, lo_c, hi_b, own_a = at.join_reps(up_cores), sum_lo(low_c), at.reduce_his(lo_b), cores(hi_a)
-    lo_c, hi_b, own_a, out_own, gate_own = fence(lo_c, hi_b, own_a, out_own, gate_own)
+    lo_c, hi_b, own_a, out_own, gate_own, down_total = fence(lo_c, hi_b, own_a, out_own, gate_own, whole_rows(down_own))
     hi_c, own_b, own_a, out_own = at.reduce_his(lo_c), cores(hi_b), at.join_reps(own_a), at.join_reps(out_own)
     hi_c, own_b = fence(hi_c, own_b)
     own_c, own_b = cores(hi_c), at.join_reps(own_b)
-    own_c, gate_own, up_own, out_own, down_own, grad_normed, ffn_out = fence(own_c, gate_own, up_own, out_own, down_own, grad_normed, ffn_out)
+    own_c, gate_own, up_own, out_own, grad_normed, ffn_out = fence(own_c, gate_own, up_own, out_own, grad_normed, ffn_out)
     mix_owns = [own_b, at.join_reps(own_c), own_a]
     block_output = (resid + ffn_out).astype(BF16)
     scaled_in, scale_in = normalize(inputs)
@@ -455,14 +465,6 @@
         lines = jnp.stack(owns).reshape(len(owns), reps * CORES, rows, channels).transpose(0, 2, 1, 3).reshape(-1, width)
         return jnp.split(matmul(lines, chooser(width, width, channel_place), (1, 0)), len(owns))
 
-    def whole_units(own):
-        grid = own.reshape(reps, CORES, 2, rows, at.length, slim)
-        return grid.transpose(3, 4, 2, 1, 0, 5).reshape(rows, units).astype(F32)
-
-    def whole_rows(own):
-        return own.reshape(-1, width).astype(F32)
-
-    down_total = whole_rows(down_own)
     gate_total, up_total = whole_units(gate_own), whole_units(up_own)
     out_total = whole_rows(out_own)
     mix_totals = whole_channels(mix_owns)

time: 723 us -> 714 us (0.988)
  blocking collectives: 29.3 us -> 21.9 us
    all_gather x1, blocking collectives: 29.3 us -> 21.9 us  [shards(): gains = lax.all_gather(own_gains, 'shard', axis=1, tiled=True).astype(F32)]
    unnamed x233 -> x241, local copies, waits for them, and re-layouts: 25.8 us -> 26.4 us
  transfers between devices with their start and end apart: 62 -> 62, of which waited for: 28 -> 29; matrix products, arithmetic and copies ran while one was open for 37% -> 38% of each run, Pallas kernels for 1% -> 1%
where the time goes in v5:
time: 714 us; the launch traced here: 708 us
  waiting for transfers between devices  289 us (40%)
  matrix products  128 us (18%)
  other arithmetic  107 us (15%)
  local copies, waits for them, and re-layouts  85.3 us (12%)
  starting transfers between devices  54.2 us (8%)
  blocking collectives  21.9 us (3%)
  between operations  16.2 us (2%)
  Pallas kernels  7.26 us (1%)
    ppermute x57, waiting for transfers between devices, swap(): lax.ppermute(value, AXES, [(n, n ^ flip) for n in range(self.reps * self....  282 us
    dot_general x23, matrix products, matmul(): lax.dot_general(left, right, ((dims[:1], dims[1:]), ((), ())), preferred_...  128 us
    ppermute x57, starting transfers between devices, swap(): lax.ppermute(value, AXES, [(n, n ^ flip) for n in range(self.reps * self....  53.7 us
    unnamed x241, local copies, waits for them, and re-layouts  26.4 us
    all_gather x1, blocking collectives, shards(): gains = lax.all_gather(own_gains, 'shard', axis=1, tiled=True).astype(F32)  21.9 us
    another operation x41, other arithmetic, merge(): jnp.stack([jnp.where(first, own, other), jnp.where(first, other, own)], a...  18.1 us
  transfers between devices with their start and end apart: 62, of which 29 were waited for; matrix products, arithmetic and copies ran while one was open for 38% of the time, Pallas kernels for 1%

profile of v5, /device:TPU:0, one launch (start us, length us, event | category | flops | bytes accessed | tf_op | source)
XLA Modules:
  0.0 708.3 jit_solution(11236099394104880924)
XLA Ops:
  7.3 4.3 fusion.174
  11.6 2.7 reshape.238
  17.2 4.0 collective-permute-start
  24.6 3.4 fusion.182
  28.0 3.4 fusion.188
  34.5 5.0 fusion.179
  39.6 3.4 fusion.185
  47.0 21.9 %all_gather.13 = bf16[3,2048]{1,0:T(4,128)(2,1)S(1)} all-gather(bf16[3,128]{1,0:T(4,128)(2,1)S(1)} %pad_maximum_fusion.33), channel_id=1, replica_groups=mesh['rep'=2,'shard'=16] {'shard'}, dimensions={1}, use_global_device_ids=true | all-gather | bytes 13056 | tf_op jit(solution)/shard_map/all_gather | solution.py:306
  82.4 19.4 %collective-permute-done.1 = bf16[2,64,2048]{2,1,0:T(8,128)(2,1)S(1)} collective-permute-done((bf16[2,64,2048]{2,1,0:T(8,128)(2,1)S(1)}, bf16[2,64,2048]{2,1,0:T(8,128)(2,1)S(1)}, u32[]{:S(2)}, u32[]{:S(2)}) %collective-permute-start.1) | collective-permute-done | bytes 524320 | tf_op jit(solution)/shard_map/ppermute | solution.py:140
  102.1 12.4 %collective-permute-done.7 = bf16[512,704]{0,1:T(8,128)(2,1)} collective-permute-done((bf16[512,704]{0,1:T(8,128)(2,1)}, bf16[512,704]{0,1:T(8,128)(2,1)}, u32[]{:S(2)}, u32[]{:S(2)}) %collective-permute-start.7) | collective-permute-done | bytes 720928 | tf_op jit(solution)/shard_map/ppermute | solution.py:140
  116.9 3.3 stack.224
  120.2 2.8 stack.225
  134.5 5.2 fusion.118
  144.1 7.0 all-gather.4.cloned.1.call-done
  151.4 2.6 collective-permute-start.9
  154.0 7.4 %fusion.121 = f32[768,1536]{1,0:T(8,128)S(1)} fusion(bf16[768,2048]{1,0:T(8,128)(2,1)S(1)} %copy-done.44, bf16[2048,3072]{0,1:T(8,128)(2,1)} %all-gather.4.cloned.1.call-done, s32[]{:T(128)S(6)} %select_n.686), kind=kOutput, calls=%fused_computation.142 | convolution fusion | flops 4831838208 | bytes 14155780 | tf_op jit(solution)/shard_map/dot_general | solution.py:33
  165.1 4.0 convolution_convert_fusion.1
  169.1 16.1 %collective-permute-done.9 = bf16[512,704]{0,1:T(8,128)(2,1)} collective-permute-done((bf16[512,704]{0,1:T(8,128)(2,1)}, bf16[512,704]{0,1:T(8,128)(2,1)}, u32[]{:S(2)}, u32[]{:S(2)}) %collective-permute-start.9) | collective-permute-done | bytes 720928 | tf_op jit(solution)/shard_map/ppermute | solution.py:140
  187.8 3.2 collective-permute-start.15
  191.5 2.6 convert_add_fusion.1
  196.9 17.0 %collective-permute-done.13 = f32[1,192]{1,0:T(1,128)S(1)} collective-permute-done((f32[1,192]{1,0:T(1,128)S(1)}, f32[1,192]{1,0:T(1,128)S(1)}, u32[]{:S(2)}, u32[]{:S(2)}) %collective-permute-start.13) | collective-permute-done | bytes 800 | tf_op jit(solution)/shard_map/ppermute | solution.py:140
  213.9 21.2 %collective-permute-done.15 = bf16[512,704]{0,1:T(8,128)(2,1)S(1)} collective-permute-done((bf16[512,704]{0,1:T(8,128)(2,1)}, bf16[512,704]{0,1:T(8,128)(2,1)S(1)}, u32[]{:S(2)}, u32[]{:S(2)}) %collective-permute-start.15) | collective-permute-done | bytes 720928 | tf_op jit(solution)/shard_map/ppermute | solution.py:140
  237.3 3.3 pad_maximum_fusion.2
  249.3 31.2 %collective-permute-done.17 = bf16[176,2048]{1,0:T(8,128)(2,1)S(1)} collective-permute-done((bf16[176,2048]{1,0:T(8,128)(2,1)}, bf16[176,2048]{1,0:T(8,128)(2,1)S(1)}, u32[]{:S(2)}, u32[]{:S(2)}) %collective-permute-start.17) | collective-permute-done | bytes 720928 | tf_op jit(solution)/shard_map/ppermute | solution.py:140
  282.9 12.9 %collective-permute-done.16 = bf16[1024,704]{0,1:T(8,128)(2,1)S(1)} collective-permute-done((bf16[1024,704]{0,1:T(8,128)(2,1)}, bf16[1024,704]{0,1:T(8,128)(2,1)S(1)}, u32[]{:S(2)}, u32[]{:S(2)}) %collective-permute-start.16) | collective-permute-done | bytes 1441824 | tf_op jit(solution)/shard_map/ppermute | solution.py:140
  299.5 8.6 %fusion.284 = f32[1536,704]{0,1:T(8,128)S(1)} fusion(bf16[1536,2048]{1,0:T(8,128)(2,1)} %all-gather.6.cloned.1.call-done, bf16[2048,704]{0,1:T(8,128)(2,1)} %pad_maximum_fusion.2), kind=kOutput, calls=%fused_computation.541 | convolution fusion | flops 4429185024 | bytes 13500416 | tf_op jit(solution)/shard_map/dot_general | solution.py:33
  308.2 6.6 multiply_convert_fusion.2
  314.8 6.0 convolution_convert_fusion.4
  320.7 10.5 %collective-permute-done.18 = bf16[2,176,2048]{2,1,0:T(8,128)(2,1)S(1)} collective-permute-done((bf16[2,176,2048]{2,1,0:T(8,128)(2,1)}, bf16[2,176,2048]{2,1,0:T(8,128)(2,1)S(1)}, u32[]{:S(2)}, u32[]{:S(2)}) %collective-permute-start.18) | collective-permute-done | bytes 1441824 | tf_op jit(solution)/shard_map/ppermute | solution.py:140
  331.7 10.0 %multiply_convert_fusion.1 = (bf16[1536,704]{0,1:T(8,128)(2,1)}, bf16[1536,704]{0,1:T(8,128)(2,1)S(1)}) fusion(f32[1536,704]{0,1:T(8,128)S(1)} %fusion.284, f32[1536,704]{0,1:T(8,128)} %get-tuple-element.354, bf16[1536,2048]{1,0:T(8,128)(2,1)S(1)} %bitcast.453, bf16[704,2048]{1,0:T(8,128)(2,1)S(1)} %bitcast.405), kind=kOutput, calls=%fused_computation.145 | convolution fusion | flops 4443242496 | bytes 22151168 | tf_op jit(solution)/shard_map/dot_general | solution.py:33
  341.7 5.1 fusion.285
  346.9 8.7 %add_convert_fusion = bf16[1536,2048]{1,0:T(8,128)(2,1)} fusion(f32[1536,2048]{1,0:T(8,128)S(1)} %fusion.285, bf16[1536,704]{0,1:T(8,128)(2,1)} %get-tuple-element.135, bf16[2048,704]{0,1:T(8,128)(2,1)S(1)} %copy-done.48), kind=kOutput, calls=%fused_computation.56 | convolution fusion | flops 4435476480 | bytes 23920640 | tf_op jit(solution)/shard_map/dot_general | solution.py:33
  355.6 2.8 dynamic-slice_bitcast_fusion
  359.4 10.1 %convolution_convert_fusion.2 = bf16[2048,704]{0,1:T(8,128)(2,1)} fusion(bf16[1536,704]{0,1:T(8,128)(2,1)S(1)} %copy-done.101, bf16[1536,2048]{1,0:T(8,128)(2,1)} %all-gather.6.cloned.1.call-done), kind=kOutput, calls=%fused_computation.168 | convolution fusion | flops 4430626816 | bytes 11337728 | tf_op jit(solution)/shard_map/dot_general | solution.py:33
  369.6 4.8 convolution_convert_fusion.3
  378.3 7.0 convolution_convert_fusion
  385.3 7.9 %collective-permute-done.20 = bf16[2,176,2048]{2,1,0:T(8,128)(2,1)} collective-permute-done((bf16[2,176,2048]{2,1,0:T(8,128)(2,1)}, bf16[2,176,2048]{2,1,0:T(8,128)(2,1)}, u32[]{:S(2)}, u32[]{:S(2)}) %collective-permute-start.20) | collective-permute-done | bytes 1441824 | tf_op jit(solution)/shard_map/ppermute | solution.py:140
  400.4 37.1 %collective-permute-done.19 = bf16[1024,704]{0,1:T(8,128)(2,1)} collective-permute-done((bf16[1024,704]{0,1:T(8,128)(2,1)}, bf16[1024,704]{0,1:T(8,128)(2,1)}, u32[]{:S(2)}, u32[]{:S(2)}) %collective-permute-start.19) | collective-permute-done | bytes 1441824 | tf_op jit(solution)/shard_map/ppermute | solution.py:140
  437.5 3.5 add_convert_fusion.2
  452.4 14.7 %collective-permute-done.22 = bf16[192,2048]{1,0:T(8,128)(2,1)S(1)} collective-permute-done((bf16[192,2048]{1,0:T(8,128)(2,1)S(1)}, bf16[192,2048]{1,0:T(8,128)(2,1)S(1)}, u32[]{:S(2)}, u32[]{:S(2)}) %collective-permute-start.22) | collective-permute-done | bytes 786464 | tf_op jit(solution)/shard_map/ppermute | solution.py:140
  471.0 2.5 collective-permute-start.24
  478.3 2.7 copy.212
  483.6 3.2 add_convert_fusion.1
  486.8 3.4 pad_maximum_fusion.1
  493.5 4.6 convolution_convert_fusion.8
  500.7 3.9 subtract_multiply_fusion
  508.2 3.2 convolution_convert_fusion.5
  511.4 3.2 convolution_convert_fusion.6
  514.6 3.2 convolution_convert_fusion.7
  517.8 6.7 fusion.141
  534.4 2.6 add_convert_fusion.6
  537.0 5.1 collective-permute-done.29
  547.1 2.9 collective-permute-start.38
  553.6 19.7 %collective-permute-done.32 = bf16[2,64,2048]{2,1,0:T(8,128)(2,1)S(1)} collective-permute-done((bf16[2,64,2048]{2,1,0:T(8,128)(2,1)S(1)}, bf16[2,64,2048]{2,1,0:T(8,128)(2,1)S(1)}, u32[]{:S(2)}, u32[]{:S(2)}) %collective-permute-start.32) | collective-permute-done | bytes 524320 | tf_op jit(solution)/shard_map/ppermute | solution.py:140
  576.6 3.7 convert_add_fusion
  585.1 4.4 collective-permute-start.36
  600.6 4.5 collective-permute-done.36
  614.2 9.4 %collective-permute-done.42 = bf16[256,512]{1,0:T(8,128)(2,1)S(1)} collective-permute-done((bf16[256,512]{1,0:T(8,128)(2,1)S(1)}, bf16[256,512]{1,0:T(8,128)(2,1)S(1)}, u32[]{:S(2)}, u32[]{:S(2)}) %collective-permute-start.42) | collective-permute-done | bytes 262176 | tf_op jit(solution)/shard_map/ppermute | solution.py:140
  625.6 4.9 collective-permute-done.41
  636.4 8.7 %collective-permute-done.46 = bf16[256,512]{1,0:T(8,128)(2,1)S(1)} collective-permute-done((bf16[256,512]{1,0:T(8,128)(2,1)S(1)}, bf16[256,512]{1,0:T(8,128)(2,1)S(1)}, u32[]{:S(2)}, u32[]{:S(2)}) %collective-permute-start.46) | collective-permute-done | bytes 262176 | tf_op jit(solution)/shard_map/ppermute | solution.py:140
  645.2 5.7 collective-permute-done.45
  654.2 13.3 %collective-permute-done.49 = bf16[256,512]{1,0:T(8,128)(2,1)S(1)} collective-permute-done((bf16[256,512]{1,0:T(8,128)(2,1)S(1)}, bf16[256,512]{1,0:T(8,128)(2,1)S(1)}, u32[]{:S(2)}, u32[]{:S(2)}) %collective-permute-start.49) | collective-permute-done | bytes 262176 | tf_op jit(solution)/shard_map/ppermute | solution.py:140
  681.3 3.5 copy.216
  693.8 5.4 fusion.11
  (536 shorter events, 198.9 us)
Async XLA Ops:
  7.2 143.8 %all-gather.4.cloned.1.call-start = ((), (), s32[]{:S(2)}) async-start(), calls=%async_computation.2 | async-start | bytes 13369344 | tf_op jit(solution)/shard_map/all_gather | solution.py:280
  16.1 281.6 %all-gather.8.cloned.1.call-start = ((), (), s32[]{:S(2)}) async-start(), calls=%async_computation.4 | async-start | bytes 7077888 | tf_op jit(solution)/shard_map/all_gather | solution.py:224
  17.2 28.7 %collective-permute-start = (bf16[64,2048]{1,0:T(8,128)(2,1)}, bf16[64,2048]{1,0:T(8,128)(2,1)}, u32[]{:S(2)}, u32[]{:S(2)}) collective-permute-start(bf16[64,2048]{1,0:T(8,128)(2,1)} %dynamic-slice_bitcast_fusion.19), channel_id=1, source_target_pairs={{0,8},{1,9},{2,10},{3,11},{4,12},{5,13},{6,14},{7,15},{8,0},{9,1},... | collective-permute-start | bytes 786440 | tf_op jit(solution)/shard_map/ppermute | solution.py:140
  21.2 59.6 %collective-permute-start.2 = (bf16[192,2048]{1,0:T(8,128)(2,1)S(1)}, bf16[192,2048]{1,0:T(8,128)(2,1)S(1)}, u32[]{:S(2)}, u32[]{:S(2)}) collective-permute-start(bf16[192,2048]{1,0:T(8,128)(2,1)S(1)} %bitcast.387), channel_id=1, source_target_pairs={{0,16},{1,17},{2,18},{3,19},{4,20},{5,21},{6,22},{7,23},{8,24},{9,... | collective-permute-start | bytes 2359304 | tf_op jit(solution)/shard_map/ppermute | solution.py:140
  32.4 36.6 %collective-permute-start.6 = (bf16[512,704]{0,1:T(8,128)(2,1)}, bf16[512,704]{0,1:T(8,128)(2,1)}, u32[]{:S(2)}, u32[]{:S(2)}) collective-permute-start(bf16[512,704]{0,1:T(8,128)(2,1)} %pad_maximum_fusion.18), channel_id=1, source_target_pairs={{0,1},{1,0},{2,3},{3,2},{4,5},{5,4},{6,7},{7,6},{8,9},{9,8},{10,11... | collective-permute-start | bytes 2162696 | tf_op jit(solution)/shard_map/ppermute | solution.py:140
  32.4 10.7 %collective-permute-start.4 = (s32[1,192]{1,0:T(1,128)}, s32[1,192]{1,0:T(1,128)}, u32[]{:S(2)}, u32[]{:S(2)}) collective-permute-start(s32[1,192]{1,0:T(1,128)} %param.14), channel_id=1, source_target_pairs={{0,16},{1,17},{2,18},{3,19},{4,20},{5,21},{6,22},{7,23},{8,24},{9,... | collective-permute-start | bytes 2312 | tf_op jit(solution)/shard_map/ppermute | solution.py:140
  43.8 1.2 collective-permute-start.5
  68.9 65.6 %copy-start.73 = (f32[1,2048]{1,0:T(1,128)}, f32[1,2048]{1,0:T(1,128)S(1)}, u32[]{:S(2)}) copy-start(f32[1,2048]{1,0:T(1,128)S(1)} %get-tuple-element.352) | copy-start | bytes 24580
  68.9 32.9 %collective-permute-start.1 = (bf16[2,64,2048]{2,1,0:T(8,128)(2,1)S(1)}, bf16[2,64,2048]{2,1,0:T(8,128)(2,1)S(1)}, u32[]{:S(2)}, u32[]{:S(2)}) collective-permute-start(bf16[2,64,2048]{2,1,0:T(8,128)(2,1)S(1)} %pad_maximum_fusion.23), channel_id=1, source_target_pairs={{0,4},{1,5},{2,6},{3,7},{4,0},{5,1},{6,2},{7,3},{8,12},{9,13},{10,... | collective-permute-start | bytes 1572872 | tf_op jit(solution)/shard_map/ppermute | solution.py:140
  79.7 34.7 %collective-permute-start.7 = (bf16[512,704]{0,1:T(8,128)(2,1)}, bf16[512,704]{0,1:T(8,128)(2,1)}, u32[]{:S(2)}, u32[]{:S(2)}) collective-permute-start(bf16[512,704]{0,1:T(8,128)(2,1)} %bitcast.432), channel_id=1, source_target_pairs={{0,2},{1,3},{2,0},{3,1},{4,6},{5,7},{6,4},{7,5},{8,10},{9,11},{10,... | collective-permute-start | bytes 2162696 | tf_op jit(solution)/shard_map/ppermute | solution.py:140
  82.1 50.5 %collective-permute-start.3 = (bf16[384,2048]{1,0:T(8,128)(2,1)}, bf16[384,2048]{1,0:T(8,128)(2,1)}, u32[]{:S(2)}, u32[]{:S(2)}) collective-permute-start(bf16[384,2048]{1,0:T(8,128)(2,1)} %pad_maximum_fusion.6), channel_id=1, source_target_pairs={{0,1},{1,0},{2,3},{3,2},{4,5},{5,4},{6,7},{7,6},{8,9},{9,8},{10,11... | collective-permute-start | bytes 4718600 | tf_op jit(solution)/shard_map/ppermute | solution.py:140
  102.0 39.2 %collective-permute-start.8 = (bf16[2,2,64,2048]{3,2,1,0:T(8,128)(2,1)S(1)}, bf16[2,2,64,2048]{3,2,1,0:T(8,128)(2,1)}, u32[]{:S(2)}, u32[]{:S(2)}) collective-permute-start(bf16[2,2,64,2048]{3,2,1,0:T(8,128)(2,1)S(1)} %pad_maximum_fusion.16), channel_id=1, source_target_pairs={{0,2},{1,3},{2,0},{3,1},{4,6},{5,7},{6,4},{7,5},{8,10},{9,11},{10,... | collective-permute-start | bytes 3145736 | tf_op jit(solution)/shard_map/ppermute | solution.py:140
  151.1 146.6 %all-gather.6.cloned.1.call-start = ((), (), s32[]{:S(2)}) async-start(), calls=%async_computation.3 | async-start | bytes 7077888 | tf_op jit(solution)/shard_map/all_gather | solution.py:224
  151.4 33.9 %collective-permute-start.9 = (bf16[512,704]{0,1:T(8,128)(2,1)}, bf16[512,704]{0,1:T(8,128)(2,1)}, u32[]{:S(2)}, u32[]{:S(2)}) collective-permute-start(bf16[512,704]{0,1:T(8,128)(2,1)} %bitcast.411), channel_id=1, source_target_pairs={{0,8},{1,9},{2,10},{3,11},{4,12},{5,13},{6,14},{7,15},{8,0},{9,1},... | collective-permute-start | bytes 2162696 | tf_op jit(solution)/shard_map/ppermute | solution.py:140
  187.7 3.8 collective-permute-start.10
  187.8 49.5 %collective-permute-start.14 = (bf16[1024,704]{0,1:T(8,128)(2,1)S(1)}, bf16[1024,704]{0,1:T(8,128)(2,1)}, u32[]{:S(2)}, u32[]{:S(2)}) collective-permute-start(bf16[1024,704]{0,1:T(8,128)(2,1)S(1)} %pad_maximum_fusion.10), channel_id=1, source_target_pairs={{0,4},{1,5},{2,6},{3,7},{4,0},{5,1},{6,2},{7,3},{8,12},{9,13},{10,... | collective-permute-start | bytes 4325384 | tf_op jit(solution)/shard_map/ppermute | solution.py:140
  187.8 47.3 %collective-permute-start.15 = (bf16[512,704]{0,1:T(8,128)(2,1)}, bf16[512,704]{0,1:T(8,128)(2,1)S(1)}, u32[]{:S(2)}, u32[]{:S(2)}) collective-permute-start(bf16[512,704]{0,1:T(8,128)(2,1)} %bitcast.409), channel_id=1, source_target_pairs={{0,8},{1,9},{2,10},{3,11},{4,12},{5,13},{6,14},{7,15},{8,0},{9,1},... | collective-permute-start | bytes 2162696 | tf_op jit(solution)/shard_map/ppermute | solution.py:140
  191.0 4.8 collective-permute-start.12
  194.2 46.4 %collective-permute-start.11 = (bf16[192,2048]{1,0:T(8,128)(2,1)S(1)}, bf16[192,2048]{1,0:T(8,128)(2,1)S(1)}, u32[]{:S(2)}, u32[]{:S(2)}) collective-permute-start(bf16[192,2048]{1,0:T(8,128)(2,1)S(1)} %slice.200), channel_id=1, source_target_pairs={{0,16},{1,17},{2,18},{3,19},{4,20},{5,21},{6,22},{7,23},{8,24},{9,... | collective-permute-start | bytes 2359304 | tf_op jit(solution)/shard_map/ppermute | solution.py:140
  195.8 18.2 %collective-permute-start.13 = (f32[1,192]{1,0:T(1,128)S(1)}, f32[1,192]{1,0:T(1,128)S(1)}, u32[]{:S(2)}, u32[]{:S(2)}) collective-permute-start(f32[1,192]{1,0:T(1,128)S(1)} %slice.146), channel_id=1, source_target_pairs={{0,16},{1,17},{2,18},{3,19},{4,20},{5,21},{6,22},{7,23},{8,24},{9,... | collective-permute-start | bytes 2312 | tf_op jit(solution)/shard_map/ppermute | solution.py:140
  246.0 197.2 %reduce-scatter.3.cloned.1.call-start = ((), (), s32[]{:S(2)}) async-start(), calls=%async_computation.5 | async-start | bytes 7077888 | tf_op jit(solution)/shard_map/reduce_scatter | solution.py:227
  246.0 49.8 %copy-start.29 = (bf16[1024,704]{0,1:T(8,128)(2,1)S(1)}, bf16[1024,704]{0,1:T(8,128)(2,1)}, u32[]{:S(2)}) copy-start(bf16[1024,704]{0,1:T(8,128)(2,1)} %pad_maximum_fusion.11) | copy-start | bytes 4325380
  246.0 34.4 %collective-permute-start.17 = (bf16[176,2048]{1,0:T(8,128)(2,1)}, bf16[176,2048]{1,0:T(8,128)(2,1)S(1)}, u32[]{:S(2)}, u32[]{:S(2)}) collective-permute-start(bf16[176,2048]{1,0:T(8,128)(2,1)} %dynamic-slice_bitcast_fusion.10), channel_id=1, source_target_pairs={{0,8},{1,9},{2,10},{3,11},{4,12},{5,13},{6,14},{7,15},{8,0},{9,1},... | collective-permute-start | bytes 2162696 | tf_op jit(solution)/shard_map/ppermute | solution.py:140
  248.5 47.3 %collective-permute-start.16 = (bf16[1024,704]{0,1:T(8,128)(2,1)}, bf16[1024,704]{0,1:T(8,128)(2,1)S(1)}, u32[]{:S(2)}, u32[]{:S(2)}) collective-permute-start(bf16[1024,704]{0,1:T(8,128)(2,1)} %pad_maximum_fusion.11), channel_id=1, source_target_pairs={{0,4},{1,5},{2,6},{3,7},{4,0},{5,1},{6,2},{7,3},{8,12},{9,13},{10,... | collective-permute-start | bytes 4325384 | tf_op jit(solution)/shard_map/ppermute | solution.py:140
  297.7 33.5 %collective-permute-start.18 = (bf16[2,176,2048]{2,1,0:T(8,128)(2,1)}, bf16[2,176,2048]{2,1,0:T(8,128)(2,1)S(1)}, u32[]{:S(2)}, u32[]{:S(2)}) collective-permute-start(bf16[2,176,2048]{2,1,0:T(8,128)(2,1)} %pad_maximum_fusion.12), channel_id=1, source_target_pairs={{0,4},{1,5},{2,6},{3,7},{4,0},{5,1},{6,2},{7,3},{8,12},{9,13},{10,... | collective-permute-start | bytes 4325384 | tf_op jit(solution)/shard_map/ppermute | solution.py:140
  355.5 171.0 %reduce-scatter.5.cloned.1.call-start = ((), (), s32[]{:S(2)}) async-start(), calls=%async_computation.6 | async-start | bytes 7077888 | tf_op jit(solution)/shard_map/reduce_scatter | solution.py:227
  358.4 34.8 %collective-permute-start.20 = (bf16[2,176,2048]{2,1,0:T(8,128)(2,1)}, bf16[2,176,2048]{2,1,0:T(8,128)(2,1)}, u32[]{:S(2)}, u32[]{:S(2)}) collective-permute-start(bf16[2,176,2048]{2,1,0:T(8,128)(2,1)} %dynamic-slice_bitcast_fusion), channel_id=1, source_target_pairs={{0,4},{1,5},{2,6},{3,7},{4,0},{5,1},{6,2},{7,3},{8,12},{9,13},{10,... | collective-permute-start | bytes 4325384 | tf_op jit(solution)/shard_map/ppermute | solution.py:140
  377.3 60.2 %collective-permute-start.19 = (bf16[1024,704]{0,1:T(8,128)(2,1)}, bf16[1024,704]{0,1:T(8,128)(2,1)}, u32[]{:S(2)}, u32[]{:S(2)}) collective-permute-start(bf16[1024,704]{0,1:T(8,128)(2,1)} %slice.149), channel_id=1, source_target_pairs={{0,4},{1,5},{2,6},{3,7},{4,0},{5,1},{6,2},{7,3},{8,12},{9,13},{10,... | collective-permute-start | bytes 4325384 | tf_op jit(solution)/shard_map/ppermute | solution.py:140
  397.6 43.4 %collective-permute-start.21 = (bf16[176,2048]{1,0:T(8,128)(2,1)}, bf16[176,2048]{1,0:T(8,128)(2,1)}, u32[]{:S(2)}, u32[]{:S(2)}) collective-permute-start(bf16[176,2048]{1,0:T(8,128)(2,1)} %dynamic-slice_bitcast_fusion.9), channel_id=1, source_target_pairs={{0,8},{1,9},{2,10},{3,11},{4,12},{5,13},{6,14},{7,15},{8,0},{9,1},... | collective-permute-start | bytes 2162696 | tf_op jit(solution)/shard_map/ppermute | solution.py:140
  449.9 17.2 %collective-permute-start.22 = (bf16[192,2048]{1,0:T(8,128)(2,1)S(1)}, bf16[192,2048]{1,0:T(8,128)(2,1)S(1)}, u32[]{:S(2)}, u32[]{:S(2)}) collective-permute-start(bf16[192,2048]{1,0:T(8,128)(2,1)S(1)} %get-tuple-element.273), channel_id=1, source_target_pairs={{0,16},{1,17},{2,18},{3,19},{4,20},{5,21},{6,22},{7,23},{8,24},{9,... | collective-permute-start | bytes 2359304 | tf_op jit(solution)/shard_map/ppermute | solution.py:140
  452.4 31.2 %collective-permute-start.26 = (bf16[1024,704]{0,1:T(8,128)(2,1)}, bf16[1024,704]{0,1:T(8,128)(2,1)}, u32[]{:S(2)}, u32[]{:S(2)}) collective-permute-start(bf16[1024,704]{0,1:T(8,128)(2,1)} %slice.122), channel_id=1, source_target_pairs={{0,4},{1,5},{2,6},{3,7},{4,0},{5,1},{6,2},{7,3},{8,12},{9,13},{10,... | collective-permute-start | bytes 4325384 | tf_op jit(solution)/shard_map/ppermute | solution.py:140
  468.5 18.3 %collective-permute-start.23 = (bf16[384,2048]{1,0:T(8,128)(2,1)}, bf16[384,2048]{1,0:T(8,128)(2,1)}, u32[]{:S(2)}, u32[]{:S(2)}) collective-permute-start(bf16[384,2048]{1,0:T(8,128)(2,1)} %pad_maximum_fusion.8), channel_id=1, source_target_pairs={{0,1},{1,0},{2,3},{3,2},{4,5},{5,4},{6,7},{7,6},{8,9},{9,8},{10,11... | collective-permute-start | bytes 4718600 | tf_op jit(solution)/shard_map/ppermute | solution.py:140
  471.0 4.1 collective-permute-start.24
  475.1 7.2 %collective-permute-start.25 = (f32[2,2,192]{2,1,0:T(2,128)S(1)}, f32[2,2,192]{2,1,0:T(2,128)S(1)}, u32[]{:S(2)}, u32[]{:S(2)}) collective-permute-start(f32[2,2,192]{2,1,0:T(2,128)S(1)} %pad_maximum_fusion.32), channel_id=1, source_target_pairs={{0,1},{1,0},{2,3},{3,2},{4,5},{5,4},{6,7},{7,6},{8,9},{9,8},{10,11... | collective-permute-start | bytes 9224 | tf_op jit(solution)/shard_map/ppermute | solution.py:140
  490.4 34.1 %collective-permute-start.28 = (bf16[176,2048]{1,0:T(8,128)(2,1)}, bf16[176,2048]{1,0:T(8,128)(2,1)S(1)}, u32[]{:S(2)}, u32[]{:S(2)}) collective-permute-start(bf16[176,2048]{1,0:T(8,128)(2,1)} %fusion.173), channel_id=1, source_target_pairs={{0,16},{1,17},{2,18},{3,19},{4,20},{5,21},{6,22},{7,23},{8,24},{9,... | collective-permute-start | bytes 2162696 | tf_op jit(solution)/shard_map/ppermute | solution.py:140
  493.4 32.6 %collective-permute-start.27 = (bf16[512,704]{0,1:T(8,128)(2,1)S(1)}, bf16[512,704]{0,1:T(8,128)(2,1)S(1)}, u32[]{:S(2)}, u32[]{:S(2)}) collective-permute-start(bf16[512,704]{0,1:T(8,128)(2,1)S(1)} %slice.127), channel_id=1, source_target_pairs={{0,8},{1,9},{2,10},{3,11},{4,12},{5,13},{6,14},{7,15},{8,0},{9,1},... | collective-permute-start | bytes 2162696 | tf_op jit(solution)/shard_map/ppermute | solution.py:140
  499.5 34.9 %collective-permute-start.30 = (bf16[2,2,64,2048]{3,2,1,0:T(8,128)(2,1)}, bf16[2,2,64,2048]{3,2,1,0:T(8,128)(2,1)}, u32[]{:S(2)}, u32[]{:S(2)}) collective-permute-start(bf16[2,2,64,2048]{3,2,1,0:T(8,128)(2,1)} %get-tuple-element.296), channel_id=1, source_target_pairs={{0,2},{1,3},{2,0},{3,1},{4,6},{5,7},{6,4},{7,5},{8,10},{9,11},{10,... | collective-permute-start | bytes 3145736 | tf_op jit(solution)/shard_map/ppermute | solution.py:140
  530.8 11.3 %collective-permute-start.29 = (bf16[256,704]{0,1:T(8,128)(2,1)S(1)}, bf16[256,704]{0,1:T(8,128)(2,1)S(1)}, u32[]{:S(2)}, u32[]{:S(2)}) collective-permute-start(bf16[256,704]{0,1:T(8,128)(2,1)S(1)} %bitcast.436), channel_id=1, source_target_pairs={{0,2},{1,3},{2,0},{3,1},{4,6},{5,7},{6,4},{7,5},{8,10},{9,11},{10,... | collective-permute-start | bytes 1081352 | tf_op jit(solution)/shard_map/ppermute | solution.py:140
  533.2 40.9 %collective-permute-start.31 = (bf16[2,2,256,512]{3,2,1,0:T(8,128)(2,1)}, bf16[2,2,256,512]{3,2,1,0:T(8,128)(2,1)}, u32[]{:S(2)}, u32[]{:S(2)}) collective-permute-start(bf16[2,2,256,512]{3,2,1,0:T(8,128)(2,1)} %get-tuple-element.295), channel_id=1, source_target_pairs={{0,2},{1,3},{2,0},{3,1},{4,6},{5,7},{6,4},{7,5},{8,10},{9,11},{10,... | collective-permute-start | bytes 3145736 | tf_op jit(solution)/shard_map/ppermute | solution.py:140
  543.5 33.1 %collective-permute-start.34 = (bf16[384,2048]{1,0:T(8,128)(2,1)}, bf16[384,2048]{1,0:T(8,128)(2,1)}, u32[]{:S(2)}, u32[]{:S(2)}) collective-permute-start(bf16[384,2048]{1,0:T(8,128)(2,1)} %slice.130), channel_id=1, source_target_pairs={{0,1},{1,0},{2,3},{3,2},{4,5},{5,4},{6,7},{7,6},{8,9},{9,8},{10,11... | collective-permute-start | bytes 4718600 | tf_op jit(solution)/shard_map/ppermute | solution.py:140
  545.3 6.4 collective-permute-start.33
  546.9 26.3 %collective-permute-start.32 = (bf16[2,64,2048]{2,1,0:T(8,128)(2,1)S(1)}, bf16[2,64,2048]{2,1,0:T(8,128)(2,1)S(1)}, u32[]{:S(2)}, u32[]{:S(2)}) collective-permute-start(bf16[2,64,2048]{2,1,0:T(8,128)(2,1)S(1)} %dynamic-slice_bitcast_fusion.14), channel_id=1, source_target_pairs={{0,4},{1,5},{2,6},{3,7},{4,0},{5,1},{6,2},{7,3},{8,12},{9,13},{10,... | collective-permute-start | bytes 1572872 | tf_op jit(solution)/shard_map/ppermute | solution.py:140
  547.1 34.9 %collective-permute-start.38 = (bf16[512,704]{0,1:T(8,128)(2,1)S(1)}, bf16[512,704]{0,1:T(8,128)(2,1)S(1)}, u32[]{:S(2)}, u32[]{:S(2)}) collective-permute-start(bf16[512,704]{0,1:T(8,128)(2,1)S(1)} %get-tuple-element.308), channel_id=1, source_target_pairs={{0,8},{1,9},{2,10},{3,11},{4,12},{5,13},{6,14},{7,15},{8,0},{9,1},... | collective-permute-start | bytes 2162696 | tf_op jit(solution)/shard_map/ppermute | solution.py:140
  551.6 44.4 %collective-permute-start.35 = (bf16[2,2,256,512]{3,2,1,0:T(8,128)(2,1)}, bf16[2,2,256,512]{3,2,1,0:T(8,128)(2,1)}, u32[]{:S(2)}, u32[]{:S(2)}) collective-permute-start(bf16[2,2,256,512]{3,2,1,0:T(8,128)(2,1)} %get-tuple-element.292), channel_id=1, source_target_pairs={{0,2},{1,3},{2,0},{3,1},{4,6},{5,7},{6,4},{7,5},{8,10},{9,11},{10,... | collective-permute-start | bytes 3145736 | tf_op jit(solution)/shard_map/ppermute | solution.py:140
  584.0 16.4 %collective-permute-start.39 = (bf16[256,704]{0,1:T(8,128)(2,1)S(1)}, bf16[256,704]{0,1:T(8,128)(2,1)S(1)}, u32[]{:S(2)}, u32[]{:S(2)}) collective-permute-start(bf16[256,704]{0,1:T(8,128)(2,1)S(1)} %bitcast.433), channel_id=1, source_target_pairs={{0,2},{1,3},{2,0},{3,1},{4,6},{5,7},{6,4},{7,5},{8,10},{9,11},{10,... | collective-permute-start | bytes 1081352 | tf_op jit(solution)/shard_map/ppermute | solution.py:140
  585.0 14.6 %collective-permute-start.37 = (bf16[64,2048]{1,0:T(8,128)(2,1)S(1)}, bf16[64,2048]{1,0:T(8,128)(2,1)S(1)}, u32[]{:S(2)}, u32[]{:S(2)}) collective-permute-start(bf16[64,2048]{1,0:T(8,128)(2,1)S(1)} %dynamic-slice_bitcast_fusion.18), channel_id=1, source_target_pairs={{0,8},{1,9},{2,10},{3,11},{4,12},{5,13},{6,14},{7,15},{8,0},{9,1},... | collective-permute-start | bytes 786440 | tf_op jit(solution)/shard_map/ppermute | solution.py:140
  585.1 19.9 %collective-permute-start.36 = (bf16[2,256,512]{2,1,0:T(8,128)(2,1)S(1)}, bf16[2,256,512]{2,1,0:T(8,128)(2,1)S(1)}, u32[]{:S(2)}, u32[]{:S(2)}) collective-permute-start(bf16[2,256,512]{2,1,0:T(8,128)(2,1)S(1)} %dynamic-slice_bitcast_fusion.13), channel_id=1, source_target_pairs={{0,4},{1,5},{2,6},{3,7},{4,0},{5,1},{6,2},{7,3},{8,12},{9,13},{10,... | collective-permute-start | bytes 1572872 | tf_op jit(solution)/shard_map/ppermute | solution.py:140
  591.9 20.8 %collective-permute-start.44 = (bf16[192,2048]{1,0:T(8,128)(2,1)}, bf16[192,2048]{1,0:T(8,128)(2,1)}, u32[]{:S(2)}, u32[]{:S(2)}) collective-permute-start(bf16[192,2048]{1,0:T(8,128)(2,1)} %slice.199), channel_id=1, source_target_pairs={{0,16},{1,17},{2,18},{3,19},{4,20},{5,21},{6,22},{7,23},{8,24},{9,... | collective-permute-start | bytes 2359304 | tf_op jit(solution)/shard_map/ppermute | solution.py:140
  596.0 27.9 %collective-permute-start.40 = (bf16[2,2,256,512]{3,2,1,0:T(8,128)(2,1)}, bf16[2,2,256,512]{3,2,1,0:T(8,128)(2,1)}, u32[]{:S(2)}, u32[]{:S(2)}) collective-permute-start(bf16[2,2,256,512]{3,2,1,0:T(8,128)(2,1)} %get-tuple-element.291), channel_id=1, source_target_pairs={{0,2},{1,3},{2,0},{3,1},{4,6},{5,7},{6,4},{7,5},{8,10},{9,11},{10,... | collective-permute-start | bytes 3145736 | tf_op jit(solution)/shard_map/ppermute | solution.py:140
  606.0 28.9 %collective-permute-start.48 = (bf16[2,2,128,704]{2,3,1,0:T(8,128)(2,1)}, bf16[2,2,128,704]{2,3,1,0:T(8,128)(2,1)}, u32[]{:S(2)}, u32[]{:S(2)}) collective-permute-start(bf16[2,2,128,704]{2,3,1,0:T(8,128)(2,1)} %pad_maximum_fusion.20), channel_id=1, source_target_pairs={{0,16},{1,17},{2,18},{3,19},{4,20},{5,21},{6,22},{7,23},{8,24},{9,... | collective-permute-start | bytes 2162696 | tf_op jit(solution)/shard_map/ppermute | solution.py:140
  608.2 15.5 %collective-permute-start.43 = (bf16[2,128,704]{1,2,0:T(8,128)(2,1)S(1)}, bf16[2,128,704]{1,2,0:T(8,128)(2,1)S(1)}, u32[]{:S(2)}, u32[]{:S(2)}) collective-permute-start(bf16[2,128,704]{1,2,0:T(8,128)(2,1)S(1)} %bitcast.434), channel_id=1, source_target_pairs={{0,1},{1,0},{2,3},{3,2},{4,5},{5,4},{6,7},{7,6},{8,9},{9,8},{10,11... | collective-permute-start | bytes 1081352 | tf_op jit(solution)/shard_map/ppermute | solution.py:140
  608.4 15.3 %collective-permute-start.42 = (bf16[256,512]{1,0:T(8,128)(2,1)S(1)}, bf16[256,512]{1,0:T(8,128)(2,1)S(1)}, u32[]{:S(2)}, u32[]{:S(2)}) collective-permute-start(bf16[256,512]{1,0:T(8,128)(2,1)S(1)} %dynamic-slice_bitcast_fusion.17), channel_id=1, source_target_pairs={{0,8},{1,9},{2,10},{3,11},{4,12},{5,13},{6,14},{7,15},{8,0},{9,1},... | collective-permute-start | bytes 786440 | tf_op jit(solution)/shard_map/ppermute | solution.py:140
  612.7 17.8 %collective-permute-start.41 = (bf16[2,256,512]{2,1,0:T(8,128)(2,1)S(1)}, bf16[2,256,512]{2,1,0:T(8,128)(2,1)S(1)}, u32[]{:S(2)}, u32[]{:S(2)}) collective-permute-start(bf16[2,256,512]{2,1,0:T(8,128)(2,1)S(1)} %dynamic-slice_bitcast_fusion.12), channel_id=1, source_target_pairs={{0,4},{1,5},{2,6},{3,7},{4,0},{5,1},{6,2},{7,3},{8,12},{9,13},{10,... | collective-permute-start | bytes 1572872 | tf_op jit(solution)/shard_map/ppermute | solution.py:140
  630.7 4.1 collective-permute-start.47
  630.8 14.4 %collective-permute-start.46 = (bf16[256,512]{1,0:T(8,128)(2,1)S(1)}, bf16[256,512]{1,0:T(8,128)(2,1)S(1)}, u32[]{:S(2)}, u32[]{:S(2)}) collective-permute-start(bf16[256,512]{1,0:T(8,128)(2,1)S(1)} %dynamic-slice_bitcast_fusion.16), channel_id=1, source_target_pairs={{0,8},{1,9},{2,10},{3,11},{4,12},{5,13},{6,14},{7,15},{8,0},{9,1},... | collective-permute-start | bytes 786440 | tf_op jit(solution)/shard_map/ppermute | solution.py:140
  630.9 20.1 %collective-permute-start.45 = (bf16[2,256,512]{2,1,0:T(8,128)(2,1)S(1)}, bf16[2,256,512]{2,1,0:T(8,128)(2,1)S(1)}, u32[]{:S(2)}, u32[]{:S(2)}) collective-permute-start(bf16[2,256,512]{2,1,0:T(8,128)(2,1)S(1)} %dynamic-slice_bitcast_fusion.11), channel_id=1, source_target_pairs={{0,4},{1,5},{2,6},{3,7},{4,0},{5,1},{6,2},{7,3},{8,12},{9,13},{10,... | collective-permute-start | bytes 1572872 | tf_op jit(solution)/shard_map/ppermute | solution.py:140
  633.1 20.8 %collective-permute-start.52 = (bf16[2,2,128,704]{2,3,1,0:T(8,128)(2,1)S(1)}, bf16[2,2,128,704]{2,3,1,0:T(8,128)(2,1)S(1)}, u32[]{:S(2)}, u32[]{:S(2)}) collective-permute-start(bf16[2,2,128,704]{2,3,1,0:T(8,128)(2,1)S(1)} %pad_maximum_fusion.22), channel_id=1, source_target_pairs={{0,16},{1,17},{2,18},{3,19},{4,20},{5,21},{6,22},{7,23},{8,24},{9,... | collective-permute-start | bytes 2162696 | tf_op jit(solution)/shard_map/ppermute | solution.py:140
  651.1 2.6 collective-permute-start.50
  651.2 18.3 %collective-permute-start.53 = (bf16[64,2048]{1,0:T(8,128)(2,1)}, bf16[64,2048]{1,0:T(8,128)(2,1)S(1)}, u32[]{:S(2)}, u32[]{:S(2)}) collective-permute-start(bf16[64,2048]{1,0:T(8,128)(2,1)} %fusion.203), channel_id=1, source_target_pairs={{0,16},{1,17},{2,18},{3,19},{4,20},{5,21},{6,22},{7,23},{8,24},{9,... | collective-permute-start | bytes 786440 | tf_op jit(solution)/shard_map/ppermute | solution.py:140
  653.0 14.4 %collective-permute-start.49 = (bf16[256,512]{1,0:T(8,128)(2,1)S(1)}, bf16[256,512]{1,0:T(8,128)(2,1)S(1)}, u32[]{:S(2)}, u32[]{:S(2)}) collective-permute-start(bf16[256,512]{1,0:T(8,128)(2,1)S(1)} %dynamic-slice_bitcast_fusion.15), channel_id=1, source_target_pairs={{0,8},{1,9},{2,10},{3,11},{4,12},{5,13},{6,14},{7,15},{8,0},{9,1},... | collective-permute-start | bytes 786440 | tf_op jit(solution)/shard_map/ppermute | solution.py:140
  653.3 14.9 %collective-permute-start.56 = (bf16[2,1,128,512]{3,2,0,1:T(8,128)(2,1)S(1)}, bf16[2,1,128,512]{3,2,0,1:T(8,128)(2,1)S(1)}, u32[]{:S(2)}, u32[]{:S(2)}) collective-permute-start(bf16[2,1,128,512]{3,2,0,1:T(8,128)(2,1)S(1)} %pad_maximum_fusion.28), channel_id=1, source_target_pairs={{0,16},{1,17},{2,18},{3,19},{4,20},{5,21},{6,22},{7,23},{8,24},{9,... | collective-permute-start | bytes 786440 | tf_op jit(solution)/shard_map/ppermute | solution.py:140
  667.6 3.0 collective-permute-start.51
  667.7 20.0 %collective-permute-start.54 = (bf16[2,1,128,512]{3,2,0,1:T(8,128)(2,1)S(1)}, bf16[2,1,128,512]{3,2,0,1:T(8,128)(2,1)}, u32[]{:S(2)}, u32[]{:S(2)}) collective-permute-start(bf16[2,1,128,512]{3,2,0,1:T(8,128)(2,1)S(1)} %bitcast.413), channel_id=1, source_target_pairs={{0,16},{1,17},{2,18},{3,19},{4,20},{5,21},{6,22},{7,23},{8,24},{9,... | collective-permute-start | bytes 786440 | tf_op jit(solution)/shard_map/ppermute | solution.py:140
  672.5 16.7 %collective-permute-start.55 = (bf16[2,1,128,512]{3,2,0,1:T(8,128)(2,1)}, bf16[2,1,128,512]{3,2,0,1:T(8,128)(2,1)}, u32[]{:S(2)}, u32[]{:S(2)}) collective-permute-start(bf16[2,1,128,512]{3,2,0,1:T(8,128)(2,1)} %bitcast.121), channel_id=1, source_target_pairs={{0,16},{1,17},{2,18},{3,19},{4,20},{5,21},{6,22},{7,23},{8,24},{9,... | collective-permute-start | bytes 786440 | tf_op jit(solution)/shard_map/ppermute | solution.py:140
  (112 other events, 768.5 us)
Sparse Core Ops, SparseCore 0:
  16.2 134.7 all-gather.3
  152.9 44.8 all-gather.7
  246.1 44.8 all-gather.5
  355.6 60.6 reduce-scatter.2
  443.3 68.0 reduce-scatter.4

commit v6 on v5

--- a/solution.py
+++ b/solution.py
@@ -369,7 +369,7 @@
     ffn_part = matmul(hidden, down_rows, (1, 0), BF16)
     down_line, ffn_part, up_cut = fence(down_line, ffn_part, up_cut)
     down_own = at.reduce_his(down_line)
-    grad_ffn_in, gate_line, down_own, ffn_part, up_cut = fence(grad_ffn_in, gate_line, down_own, ffn_part, up_cut)
+    grad_ffn_in, gate_line, ffn_part, up_cut = fence(grad_ffn_in, gate_line, ffn_part, up_cut)
 
     def fold_begin(lines, which):
         half = lines.shape[0] // 2

time: 714 us -> 720 us (level)
    unnamed x241 -> x227, local copies, waits for them, and re-layouts: 26.4 us -> 26.5 us
  transfers between devices with their start and end apart: 62 -> 62, of which waited for: 29 -> 28; matrix products, arithmetic and copies ran while one was open for 38% -> 38% of each run, Pallas kernels for 1% -> 1%
where the time goes in v6:
time: 720 us; the launch traced here: 714 us
  waiting for transfers between devices  289 us (40%)
  matrix products  128 us (18%)
  other arithmetic  111 us (15%)
  local copies, waits for them, and re-layouts  88 us (12%)
  starting transfers between devices  52.9 us (7%)
  blocking collectives  21.9 us (3%)
  between operations  16.1 us (2%)
  Pallas kernels  7.26 us (1%)
    ppermute x57, waiting for transfers between devices, swap(): lax.ppermute(value, AXES, [(n, n ^ flip) for n in range(self.reps * self....  281 us
    dot_general x23, matrix products, matmul(): lax.dot_general(left, right, ((dims[:1], dims[1:]), ((), ())), preferred_...  128 us
    ppermute x57, starting transfers between devices, swap(): lax.ppermute(value, AXES, [(n, n ^ flip) for n in range(self.reps * self....  52.4 us
    unnamed x227, local copies, waits for them, and re-layouts  26.5 us
    all_gather x1, blocking collectives, shards(): gains = lax.all_gather(own_gains, 'shard', axis=1, tiled=True).astype(F32)  21.9 us
    another operation x41, other arithmetic, merge(): jnp.stack([jnp.where(first, own, other), jnp.where(first, other, own)], a...  18.1 us
  transfers between devices with their start and end apart: 62, of which 28 were waited for; matrix products, arithmetic and copies ran while one was open for 38% of the time, Pallas kernels for 1%

profile of v6, /device:TPU:0, one launch (start us, length us, event | category | flops | bytes accessed | tf_op | source)
XLA Modules:
  0.0 714.0 jit_solution(17882019177719809376)
XLA Ops:
  7.3 4.3 fusion.174
  17.2 4.0 collective-permute-start
  24.6 3.4 fusion.182
  28.0 3.4 fusion.188
  34.5 5.0 fusion.179
  39.6 3.4 fusion.185
  47.0 21.9 %all_gather.13 = bf16[3,2048]{1,0:T(4,128)(2,1)S(1)} all-gather(bf16[3,128]{1,0:T(4,128)(2,1)S(1)} %pad_maximum_fusion.33), channel_id=1, replica_groups=mesh['rep'=2,'shard'=16] {'shard'}, dimensions={1}, use_global_device_ids=true | all-gather | bytes 13056 | tf_op jit(solution)/shard_map/all_gather | solution.py:306
  82.4 19.4 %collective-permute-done.1 = bf16[2,64,2048]{2,1,0:T(8,128)(2,1)S(1)} collective-permute-done((bf16[2,64,2048]{2,1,0:T(8,128)(2,1)S(1)}, bf16[2,64,2048]{2,1,0:T(8,128)(2,1)S(1)}, u32[]{:S(2)}, u32[]{:S(2)}) %collective-permute-start.1) | collective-permute-done | bytes 524320 | tf_op jit(solution)/shard_map/ppermute | solution.py:140
  102.1 12.4 %collective-permute-done.7 = bf16[512,704]{0,1:T(8,128)(2,1)} collective-permute-done((bf16[512,704]{0,1:T(8,128)(2,1)}, bf16[512,704]{0,1:T(8,128)(2,1)}, u32[]{:S(2)}, u32[]{:S(2)}) %collective-permute-start.7) | collective-permute-done | bytes 720928 | tf_op jit(solution)/shard_map/ppermute | solution.py:140
  116.9 3.3 stack.224
  120.2 2.8 stack.225
  134.5 5.2 fusion.118
  144.1 7.0 all-gather.4.cloned.1.call-done
  154.0 7.4 %fusion.121 = f32[768,1536]{1,0:T(8,128)S(1)} fusion(bf16[768,2048]{1,0:T(8,128)(2,1)S(1)} %copy-done.37, bf16[2048,3072]{0,1:T(8,128)(2,1)} %all-gather.4.cloned.1.call-done, s32[]{:T(128)S(6)} %select_n.686), kind=kOutput, calls=%fused_computation.142 | convolution fusion | flops 4831838208 | bytes 14155780 | tf_op jit(solution)/shard_map/dot_general | solution.py:33
  165.2 4.0 convolution_convert_fusion.1
  169.1 16.1 %collective-permute-done.9 = bf16[512,704]{0,1:T(8,128)(2,1)} collective-permute-done((bf16[512,704]{0,1:T(8,128)(2,1)}, bf16[512,704]{0,1:T(8,128)(2,1)}, u32[]{:S(2)}, u32[]{:S(2)}) %collective-permute-start.9) | collective-permute-done | bytes 720928 | tf_op jit(solution)/shard_map/ppermute | solution.py:140
  187.8 3.2 collective-permute-start.15
  196.9 17.0 %collective-permute-done.13 = f32[1,192]{1,0:T(1,128)S(1)} collective-permute-done((f32[1,192]{1,0:T(1,128)S(1)}, f32[1,192]{1,0:T(1,128)S(1)}, u32[]{:S(2)}, u32[]{:S(2)}) %collective-permute-start.13) | collective-permute-done | bytes 800 | tf_op jit(solution)/shard_map/ppermute | solution.py:140
  213.9 21.2 %collective-permute-done.15 = bf16[512,704]{0,1:T(8,128)(2,1)S(1)} collective-permute-done((bf16[512,704]{0,1:T(8,128)(2,1)}, bf16[512,704]{0,1:T(8,128)(2,1)S(1)}, u32[]{:S(2)}, u32[]{:S(2)}) %collective-permute-start.15) | collective-permute-done | bytes 720928 | tf_op jit(solution)/shard_map/ppermute | solution.py:140
  237.3 3.3 pad_maximum_fusion.2
  249.4 31.2 %collective-permute-done.17 = bf16[176,2048]{1,0:T(8,128)(2,1)S(1)} collective-permute-done((bf16[176,2048]{1,0:T(8,128)(2,1)}, bf16[176,2048]{1,0:T(8,128)(2,1)S(1)}, u32[]{:S(2)}, u32[]{:S(2)}) %collective-permute-start.17) | collective-permute-done | bytes 720928 | tf_op jit(solution)/shard_map/ppermute | solution.py:140
  283.0 12.9 %collective-permute-done.16 = bf16[1024,704]{0,1:T(8,128)(2,1)S(1)} collective-permute-done((bf16[1024,704]{0,1:T(8,128)(2,1)}, bf16[1024,704]{0,1:T(8,128)(2,1)S(1)}, u32[]{:S(2)}, u32[]{:S(2)}) %collective-permute-start.16) | collective-permute-done | bytes 1441824 | tf_op jit(solution)/shard_map/ppermute | solution.py:140
  299.5 8.6 %fusion.284 = f32[1536,704]{0,1:T(8,128)S(1)} fusion(bf16[1536,2048]{1,0:T(8,128)(2,1)} %all-gather.6.cloned.1.call-done, bf16[2048,704]{0,1:T(8,128)(2,1)} %pad_maximum_fusion.2), kind=kOutput, calls=%fused_computation.541 | convolution fusion | flops 4429185024 | bytes 13500416 | tf_op jit(solution)/shard_map/dot_general | solution.py:33
  308.2 6.6 multiply_convert_fusion.2
  314.9 6.0 convolution_convert_fusion.4
  320.9 10.4 %collective-permute-done.18 = bf16[2,176,2048]{2,1,0:T(8,128)(2,1)S(1)} collective-permute-done((bf16[2,176,2048]{2,1,0:T(8,128)(2,1)}, bf16[2,176,2048]{2,1,0:T(8,128)(2,1)S(1)}, u32[]{:S(2)}, u32[]{:S(2)}) %collective-permute-start.18) | collective-permute-done | bytes 1441824 | tf_op jit(solution)/shard_map/ppermute | solution.py:140
  331.8 10.0 %multiply_convert_fusion.1 = (bf16[1536,704]{0,1:T(8,128)(2,1)}, bf16[1536,704]{0,1:T(8,128)(2,1)S(1)}) fusion(f32[1536,704]{0,1:T(8,128)S(1)} %fusion.284, f32[1536,704]{0,1:T(8,128)} %get-tuple-element.352, bf16[1536,2048]{1,0:T(8,128)(2,1)S(1)} %bitcast.453, bf16[704,2048]{1,0:T(8,128)(2,1)S(1)} %bitcast.405), kind=kOutput, calls=%fused_computation.145 | convolution fusion | flops 4443242496 | bytes 22151168 | tf_op jit(solution)/shard_map/dot_general | solution.py:33
  341.8 5.1 fusion.285
  347.0 8.7 %add_convert_fusion = bf16[1536,2048]{1,0:T(8,128)(2,1)} fusion(f32[1536,2048]{1,0:T(8,128)S(1)} %fusion.285, bf16[1536,704]{0,1:T(8,128)(2,1)} %get-tuple-element.134, bf16[2048,704]{0,1:T(8,128)(2,1)S(1)} %copy-done.40), kind=kOutput, calls=%fused_computation.56 | convolution fusion | flops 4435476480 | bytes 23920640 | tf_op jit(solution)/shard_map/dot_general | solution.py:33
  356.3 2.8 dynamic-slice_bitcast_fusion
  360.1 10.4 %convolution_convert_fusion.2 = bf16[2048,704]{0,1:T(8,128)(2,1)} fusion(bf16[1536,704]{0,1:T(8,128)(2,1)S(1)} %copy-done.94, bf16[1536,2048]{1,0:T(8,128)(2,1)} %all-gather.6.cloned.1.call-done), kind=kOutput, calls=%fused_computation.168 | convolution fusion | flops 4430626816 | bytes 11337728 | tf_op jit(solution)/shard_map/dot_general | solution.py:33
  370.5 4.8 convolution_convert_fusion.3
  379.8 7.0 convolution_convert_fusion
  386.8 7.1 collective-permute-done.20
  393.9 3.6 fusion.144
  397.6 25.1 %collective-permute-done.19 = bf16[1024,704]{0,1:T(8,128)(2,1)} collective-permute-done((bf16[1024,704]{0,1:T(8,128)(2,1)}, bf16[1024,704]{0,1:T(8,128)(2,1)}, u32[]{:S(2)}, u32[]{:S(2)}) %collective-permute-start.19) | collective-permute-done | bytes 1441824 | tf_op jit(solution)/shard_map/ppermute | solution.py:140
  422.7 3.1 add_convert_fusion.2
  429.5 3.4 multiply_reduce_fusion.2
  440.4 2.8 slice.122
  443.4 7.2 %collective-permute-done.21 = bf16[192,2048]{1,0:T(8,128)(2,1)} collective-permute-done((bf16[192,2048]{1,0:T(8,128)(2,1)}, bf16[192,2048]{1,0:T(8,128)(2,1)}, u32[]{:S(2)}, u32[]{:S(2)}) %collective-permute-start.21) | collective-permute-done | bytes 786464 | tf_op jit(solution)/shard_map/ppermute | solution.py:140
  450.6 3.0 pad_maximum_fusion.8
  463.0 7.3 %collective-permute-done.26 = bf16[176,2048]{1,0:T(8,128)(2,1)} collective-permute-done((bf16[176,2048]{1,0:T(8,128)(2,1)}, bf16[176,2048]{1,0:T(8,128)(2,1)}, u32[]{:S(2)}, u32[]{:S(2)}) %collective-permute-start.26) | collective-permute-done | bytes 720928 | tf_op jit(solution)/shard_map/ppermute | solution.py:140
  472.5 16.6 %collective-permute-done.25 = bf16[1024,704]{0,1:T(8,128)(2,1)} collective-permute-done((bf16[1024,704]{0,1:T(8,128)(2,1)}, bf16[1024,704]{0,1:T(8,128)(2,1)}, u32[]{:S(2)}, u32[]{:S(2)}) %collective-permute-start.25) | collective-permute-done | bytes 1441824 | tf_op jit(solution)/shard_map/ppermute | solution.py:140
  489.1 3.2 add_convert_fusion.1
  492.3 3.9 pad_maximum_fusion.1
  498.0 4.6 convolution_convert_fusion.8
  505.3 3.9 subtract_multiply_fusion
  512.7 3.2 convolution_convert_fusion.5
  515.9 3.2 convolution_convert_fusion.6
  519.1 3.2 convolution_convert_fusion.7
  522.3 6.7 fusion.141
  541.5 5.2 collective-permute-done.29
  558.1 19.0 %collective-permute-done.32 = bf16[2,64,2048]{2,1,0:T(8,128)(2,1)S(1)} collective-permute-done((bf16[2,64,2048]{2,1,0:T(8,128)(2,1)S(1)}, bf16[2,64,2048]{2,1,0:T(8,128)(2,1)S(1)}, u32[]{:S(2)}, u32[]{:S(2)}) %collective-permute-start.32) | collective-permute-done | bytes 524320 | tf_op jit(solution)/shard_map/ppermute | solution.py:140
  580.6 3.7 convert_add_fusion
  584.3 3.0 collective-permute-done.38
  590.4 3.7 collective-permute-start.36
  606.3 3.4 collective-permute-done.36
  619.8 9.6 %collective-permute-done.42 = bf16[256,512]{1,0:T(8,128)(2,1)S(1)} collective-permute-done((bf16[256,512]{1,0:T(8,128)(2,1)S(1)}, bf16[256,512]{1,0:T(8,128)(2,1)S(1)}, u32[]{:S(2)}, u32[]{:S(2)}) %collective-permute-start.42) | collective-permute-done | bytes 262176 | tf_op jit(solution)/shard_map/ppermute | solution.py:140
  631.3 4.9 collective-permute-done.41
  641.0 9.8 %collective-permute-done.46 = bf16[256,512]{1,0:T(8,128)(2,1)S(1)} collective-permute-done((bf16[256,512]{1,0:T(8,128)(2,1)S(1)}, bf16[256,512]{1,0:T(8,128)(2,1)S(1)}, u32[]{:S(2)}, u32[]{:S(2)}) %collective-permute-start.46) | collective-permute-done | bytes 262176 | tf_op jit(solution)/shard_map/ppermute | solution.py:140
  650.9 5.7 collective-permute-done.45
  659.9 12.1 %collective-permute-done.49 = bf16[256,512]{1,0:T(8,128)(2,1)S(1)} collective-permute-done((bf16[256,512]{1,0:T(8,128)(2,1)S(1)}, bf16[256,512]{1,0:T(8,128)(2,1)S(1)}, u32[]{:S(2)}, u32[]{:S(2)}) %collective-permute-start.49) | collective-permute-done | bytes 262176 | tf_op jit(solution)/shard_map/ppermute | solution.py:140
  687.0 3.5 copy.216
  699.5 5.4 fusion.11
  (522 shorter events, 205.7 us)
Async XLA Ops:
  7.2 143.8 %all-gather.4.cloned.1.call-start = ((), (), s32[]{:S(2)}) async-start(), calls=%async_computation.2 | async-start | bytes 13369344 | tf_op jit(solution)/shard_map/all_gather | solution.py:280
  16.1 281.6 %all-gather.8.cloned.1.call-start = ((), (), s32[]{:S(2)}) async-start(), calls=%async_computation.4 | async-start | bytes 7077888 | tf_op jit(solution)/shard_map/all_gather | solution.py:224
  17.2 28.7 %collective-permute-start = (bf16[64,2048]{1,0:T(8,128)(2,1)}, bf16[64,2048]{1,0:T(8,128)(2,1)}, u32[]{:S(2)}, u32[]{:S(2)}) collective-permute-start(bf16[64,2048]{1,0:T(8,128)(2,1)} %dynamic-slice_bitcast_fusion.19), channel_id=1, source_target_pairs={{0,8},{1,9},{2,10},{3,11},{4,12},{5,13},{6,14},{7,15},{8,0},{9,1},... | collective-permute-start | bytes 786440 | tf_op jit(solution)/shard_map/ppermute | solution.py:140
  21.2 59.6 %collective-permute-start.2 = (bf16[192,2048]{1,0:T(8,128)(2,1)S(1)}, bf16[192,2048]{1,0:T(8,128)(2,1)S(1)}, u32[]{:S(2)}, u32[]{:S(2)}) collective-permute-start(bf16[192,2048]{1,0:T(8,128)(2,1)S(1)} %bitcast.387), channel_id=1, source_target_pairs={{0,16},{1,17},{2,18},{3,19},{4,20},{5,21},{6,22},{7,23},{8,24},{9,... | collective-permute-start | bytes 2359304 | tf_op jit(solution)/shard_map/ppermute | solution.py:140
  32.4 36.6 %collective-permute-start.6 = (bf16[512,704]{0,1:T(8,128)(2,1)}, bf16[512,704]{0,1:T(8,128)(2,1)}, u32[]{:S(2)}, u32[]{:S(2)}) collective-permute-start(bf16[512,704]{0,1:T(8,128)(2,1)} %pad_maximum_fusion.18), channel_id=1, source_target_pairs={{0,1},{1,0},{2,3},{3,2},{4,5},{5,4},{6,7},{7,6},{8,9},{9,8},{10,11... | collective-permute-start | bytes 2162696 | tf_op jit(solution)/shard_map/ppermute | solution.py:140
  32.4 10.7 %collective-permute-start.4 = (s32[1,192]{1,0:T(1,128)}, s32[1,192]{1,0:T(1,128)}, u32[]{:S(2)}, u32[]{:S(2)}) collective-permute-start(s32[1,192]{1,0:T(1,128)} %param.14), channel_id=1, source_target_pairs={{0,16},{1,17},{2,18},{3,19},{4,20},{5,21},{6,22},{7,23},{8,24},{9,... | collective-permute-start | bytes 2312 | tf_op jit(solution)/shard_map/ppermute | solution.py:140
  43.8 1.2 collective-permute-start.5
  68.9 65.6 %copy-start.66 = (f32[1,2048]{1,0:T(1,128)}, f32[1,2048]{1,0:T(1,128)S(1)}, u32[]{:S(2)}) copy-start(f32[1,2048]{1,0:T(1,128)S(1)} %get-tuple-element.350) | copy-start | bytes 24580
  68.9 32.9 %collective-permute-start.1 = (bf16[2,64,2048]{2,1,0:T(8,128)(2,1)S(1)}, bf16[2,64,2048]{2,1,0:T(8,128)(2,1)S(1)}, u32[]{:S(2)}, u32[]{:S(2)}) collective-permute-start(bf16[2,64,2048]{2,1,0:T(8,128)(2,1)S(1)} %pad_maximum_fusion.23), channel_id=1, source_target_pairs={{0,4},{1,5},{2,6},{3,7},{4,0},{5,1},{6,2},{7,3},{8,12},{9,13},{10,... | collective-permute-start | bytes 1572872 | tf_op jit(solution)/shard_map/ppermute | solution.py:140
  79.7 34.7 %collective-permute-start.7 = (bf16[512,704]{0,1:T(8,128)(2,1)}, bf16[512,704]{0,1:T(8,128)(2,1)}, u32[]{:S(2)}, u32[]{:S(2)}) collective-permute-start(bf16[512,704]{0,1:T(8,128)(2,1)} %bitcast.432), channel_id=1, source_target_pairs={{0,2},{1,3},{2,0},{3,1},{4,6},{5,7},{6,4},{7,5},{8,10},{9,11},{10,... | collective-permute-start | bytes 2162696 | tf_op jit(solution)/shard_map/ppermute | solution.py:140
  82.1 50.5 %collective-permute-start.3 = (bf16[384,2048]{1,0:T(8,128)(2,1)}, bf16[384,2048]{1,0:T(8,128)(2,1)}, u32[]{:S(2)}, u32[]{:S(2)}) collective-permute-start(bf16[384,2048]{1,0:T(8,128)(2,1)} %pad_maximum_fusion.6), channel_id=1, source_target_pairs={{0,1},{1,0},{2,3},{3,2},{4,5},{5,4},{6,7},{7,6},{8,9},{9,8},{10,11... | collective-permute-start | bytes 4718600 | tf_op jit(solution)/shard_map/ppermute | solution.py:140
  102.0 39.2 %collective-permute-start.8 = (bf16[2,2,64,2048]{3,2,1,0:T(8,128)(2,1)S(1)}, bf16[2,2,64,2048]{3,2,1,0:T(8,128)(2,1)}, u32[]{:S(2)}, u32[]{:S(2)}) collective-permute-start(bf16[2,2,64,2048]{3,2,1,0:T(8,128)(2,1)S(1)} %pad_maximum_fusion.16), channel_id=1, source_target_pairs={{0,2},{1,3},{2,0},{3,1},{4,6},{5,7},{6,4},{7,5},{8,10},{9,11},{10,... | collective-permute-start | bytes 3145736 | tf_op jit(solution)/shard_map/ppermute | solution.py:140
  151.1 146.7 %all-gather.6.cloned.1.call-start = ((), (), s32[]{:S(2)}) async-start(), calls=%async_computation.3 | async-start | bytes 7077888 | tf_op jit(solution)/shard_map/all_gather | solution.py:224
  151.4 33.9 %collective-permute-start.9 = (bf16[512,704]{0,1:T(8,128)(2,1)}, bf16[512,704]{0,1:T(8,128)(2,1)}, u32[]{:S(2)}, u32[]{:S(2)}) collective-permute-start(bf16[512,704]{0,1:T(8,128)(2,1)} %bitcast.411), channel_id=1, source_target_pairs={{0,8},{1,9},{2,10},{3,11},{4,12},{5,13},{6,14},{7,15},{8,0},{9,1},... | collective-permute-start | bytes 2162696 | tf_op jit(solution)/shard_map/ppermute | solution.py:140
  187.7 3.8 collective-permute-start.10
  187.8 49.5 %collective-permute-start.14 = (bf16[1024,704]{0,1:T(8,128)(2,1)S(1)}, bf16[1024,704]{0,1:T(8,128)(2,1)}, u32[]{:S(2)}, u32[]{:S(2)}) collective-permute-start(bf16[1024,704]{0,1:T(8,128)(2,1)S(1)} %pad_maximum_fusion.10), channel_id=1, source_target_pairs={{0,4},{1,5},{2,6},{3,7},{4,0},{5,1},{6,2},{7,3},{8,12},{9,13},{10,... | collective-permute-start | bytes 4325384 | tf_op jit(solution)/shard_map/ppermute | solution.py:140
  187.8 47.3 %collective-permute-start.15 = (bf16[512,704]{0,1:T(8,128)(2,1)}, bf16[512,704]{0,1:T(8,128)(2,1)S(1)}, u32[]{:S(2)}, u32[]{:S(2)}) collective-permute-start(bf16[512,704]{0,1:T(8,128)(2,1)} %bitcast.409), channel_id=1, source_target_pairs={{0,8},{1,9},{2,10},{3,11},{4,12},{5,13},{6,14},{7,15},{8,0},{9,1},... | collective-permute-start | bytes 2162696 | tf_op jit(solution)/shard_map/ppermute | solution.py:140
  191.0 4.8 collective-permute-start.12
  194.2 46.4 %collective-permute-start.11 = (bf16[192,2048]{1,0:T(8,128)(2,1)S(1)}, bf16[192,2048]{1,0:T(8,128)(2,1)S(1)}, u32[]{:S(2)}, u32[]{:S(2)}) collective-permute-start(bf16[192,2048]{1,0:T(8,128)(2,1)S(1)} %slice.200), channel_id=1, source_target_pairs={{0,16},{1,17},{2,18},{3,19},{4,20},{5,21},{6,22},{7,23},{8,24},{9,... | collective-permute-start | bytes 2359304 | tf_op jit(solution)/shard_map/ppermute | solution.py:140
  195.8 18.2 %collective-permute-start.13 = (f32[1,192]{1,0:T(1,128)S(1)}, f32[1,192]{1,0:T(1,128)S(1)}, u32[]{:S(2)}, u32[]{:S(2)}) collective-permute-start(f32[1,192]{1,0:T(1,128)S(1)} %slice.146), channel_id=1, source_target_pairs={{0,16},{1,17},{2,18},{3,19},{4,20},{5,21},{6,22},{7,23},{8,24},{9,... | collective-permute-start | bytes 2312 | tf_op jit(solution)/shard_map/ppermute | solution.py:140
  246.0 179.7 %reduce-scatter.3.cloned.1.call-start = ((), (), s32[]{:S(2)}) async-start(), calls=%async_computation.5 | async-start | bytes 7077888 | tf_op jit(solution)/shard_map/reduce_scatter | solution.py:227
  246.1 49.8 %copy-start.24 = (bf16[1024,704]{0,1:T(8,128)(2,1)S(1)}, bf16[1024,704]{0,1:T(8,128)(2,1)}, u32[]{:S(2)}) copy-start(bf16[1024,704]{0,1:T(8,128)(2,1)} %pad_maximum_fusion.11) | copy-start | bytes 4325380
  246.1 34.4 %collective-permute-start.17 = (bf16[176,2048]{1,0:T(8,128)(2,1)}, bf16[176,2048]{1,0:T(8,128)(2,1)S(1)}, u32[]{:S(2)}, u32[]{:S(2)}) collective-permute-start(bf16[176,2048]{1,0:T(8,128)(2,1)} %dynamic-slice_bitcast_fusion.10), channel_id=1, source_target_pairs={{0,8},{1,9},{2,10},{3,11},{4,12},{5,13},{6,14},{7,15},{8,0},{9,1},... | collective-permute-start | bytes 2162696 | tf_op jit(solution)/shard_map/ppermute | solution.py:140
  248.5 47.3 %collective-permute-start.16 = (bf16[1024,704]{0,1:T(8,128)(2,1)}, bf16[1024,704]{0,1:T(8,128)(2,1)S(1)}, u32[]{:S(2)}, u32[]{:S(2)}) collective-permute-start(bf16[1024,704]{0,1:T(8,128)(2,1)} %pad_maximum_fusion.11), channel_id=1, source_target_pairs={{0,4},{1,5},{2,6},{3,7},{4,0},{5,1},{6,2},{7,3},{8,12},{9,13},{10,... | collective-permute-start | bytes 4325384 | tf_op jit(solution)/shard_map/ppermute | solution.py:140
  297.7 33.5 %collective-permute-start.18 = (bf16[2,176,2048]{2,1,0:T(8,128)(2,1)}, bf16[2,176,2048]{2,1,0:T(8,128)(2,1)S(1)}, u32[]{:S(2)}, u32[]{:S(2)}) collective-permute-start(bf16[2,176,2048]{2,1,0:T(8,128)(2,1)} %pad_maximum_fusion.12), channel_id=1, source_target_pairs={{0,4},{1,5},{2,6},{3,7},{4,0},{5,1},{6,2},{7,3},{8,12},{9,13},{10,... | collective-permute-start | bytes 4325384 | tf_op jit(solution)/shard_map/ppermute | solution.py:140
  355.7 175.3 %reduce-scatter.5.cloned.1.call-start = ((), (), s32[]{:S(2)}) async-start(), calls=%async_computation.6 | async-start | bytes 7077888 | tf_op jit(solution)/shard_map/reduce_scatter | solution.py:227
  359.1 34.8 %collective-permute-start.20 = (bf16[2,176,2048]{2,1,0:T(8,128)(2,1)}, bf16[2,176,2048]{2,1,0:T(8,128)(2,1)}, u32[]{:S(2)}, u32[]{:S(2)}) collective-permute-start(bf16[2,176,2048]{2,1,0:T(8,128)(2,1)} %dynamic-slice_bitcast_fusion), channel_id=1, source_target_pairs={{0,4},{1,5},{2,6},{3,7},{4,0},{5,1},{6,2},{7,3},{8,12},{9,13},{10,... | collective-permute-start | bytes 4325384 | tf_op jit(solution)/shard_map/ppermute | solution.py:140
  378.2 44.5 %collective-permute-start.19 = (bf16[1024,704]{0,1:T(8,128)(2,1)}, bf16[1024,704]{0,1:T(8,128)(2,1)}, u32[]{:S(2)}, u32[]{:S(2)}) collective-permute-start(bf16[1024,704]{0,1:T(8,128)(2,1)} %slice.149), channel_id=1, source_target_pairs={{0,4},{1,5},{2,6},{3,7},{4,0},{5,1},{6,2},{7,3},{8,12},{9,13},{10,... | collective-permute-start | bytes 4325384 | tf_op jit(solution)/shard_map/ppermute | solution.py:140
  432.8 17.7 %collective-permute-start.21 = (bf16[192,2048]{1,0:T(8,128)(2,1)}, bf16[192,2048]{1,0:T(8,128)(2,1)}, u32[]{:S(2)}, u32[]{:S(2)}) collective-permute-start(bf16[192,2048]{1,0:T(8,128)(2,1)} %get-tuple-element.271), channel_id=1, source_target_pairs={{0,16},{1,17},{2,18},{3,19},{4,20},{5,21},{6,22},{7,23},{8,24},{9,... | collective-permute-start | bytes 2359304 | tf_op jit(solution)/shard_map/ppermute | solution.py:140
  438.8 31.4 %collective-permute-start.26 = (bf16[176,2048]{1,0:T(8,128)(2,1)}, bf16[176,2048]{1,0:T(8,128)(2,1)}, u32[]{:S(2)}, u32[]{:S(2)}) collective-permute-start(bf16[176,2048]{1,0:T(8,128)(2,1)} %dynamic-slice_bitcast_fusion.9), channel_id=1, source_target_pairs={{0,8},{1,9},{2,10},{3,11},{4,12},{5,13},{6,14},{7,15},{8,0},{9,1},... | collective-permute-start | bytes 2162696 | tf_op jit(solution)/shard_map/ppermute | solution.py:140
  443.2 45.9 %collective-permute-start.25 = (bf16[1024,704]{0,1:T(8,128)(2,1)}, bf16[1024,704]{0,1:T(8,128)(2,1)}, u32[]{:S(2)}, u32[]{:S(2)}) collective-permute-start(bf16[1024,704]{0,1:T(8,128)(2,1)} %slice.122), channel_id=1, source_target_pairs={{0,4},{1,5},{2,6},{3,7},{4,0},{5,1},{6,2},{7,3},{8,12},{9,13},{10,... | collective-permute-start | bytes 4325384 | tf_op jit(solution)/shard_map/ppermute | solution.py:140
  453.6 38.7 %collective-permute-start.22 = (bf16[384,2048]{1,0:T(8,128)(2,1)}, bf16[384,2048]{1,0:T(8,128)(2,1)}, u32[]{:S(2)}, u32[]{:S(2)}) collective-permute-start(bf16[384,2048]{1,0:T(8,128)(2,1)} %pad_maximum_fusion.8), channel_id=1, source_target_pairs={{0,1},{1,0},{2,3},{3,2},{4,5},{5,4},{6,7},{7,6},{8,9},{9,8},{10,11... | collective-permute-start | bytes 4718600 | tf_op jit(solution)/shard_map/ppermute | solution.py:140
  454.2 8.5 %collective-permute-start.23 = (f32[1,2,192]{2,1,0:T(2,128)S(1)}, f32[1,2,192]{2,1,0:T(2,128)S(1)}, u32[]{:S(2)}, u32[]{:S(2)}) collective-permute-start(f32[1,2,192]{2,1,0:T(2,128)S(1)} %maximum_bitcast_fusion), channel_id=1, source_target_pairs={{0,16},{1,17},{2,18},{3,19},{4,20},{5,21},{6,22},{7,23},{8,24},{9,... | collective-permute-start | bytes 4616 | tf_op jit(solution)/shard_map/ppermute | solution.py:140
  462.6 9.8 %collective-permute-start.24 = (f32[2,2,192]{2,1,0:T(2,128)S(1)}, f32[2,2,192]{2,1,0:T(2,128)S(1)}, u32[]{:S(2)}, u32[]{:S(2)}) collective-permute-start(f32[2,2,192]{2,1,0:T(2,128)S(1)} %pad_maximum_fusion.32), channel_id=1, source_target_pairs={{0,1},{1,0},{2,3},{3,2},{4,5},{5,4},{6,7},{7,6},{8,9},{9,8},{10,11... | collective-permute-start | bytes 9224 | tf_op jit(solution)/shard_map/ppermute | solution.py:140
  496.4 32.6 %collective-permute-start.28 = (bf16[176,2048]{1,0:T(8,128)(2,1)}, bf16[176,2048]{1,0:T(8,128)(2,1)S(1)}, u32[]{:S(2)}, u32[]{:S(2)}) collective-permute-start(bf16[176,2048]{1,0:T(8,128)(2,1)} %fusion.173), channel_id=1, source_target_pairs={{0,16},{1,17},{2,18},{3,19},{4,20},{5,21},{6,22},{7,23},{8,24},{9,... | collective-permute-start | bytes 2162696 | tf_op jit(solution)/shard_map/ppermute | solution.py:140
  497.9 32.4 %collective-permute-start.27 = (bf16[512,704]{0,1:T(8,128)(2,1)S(1)}, bf16[512,704]{0,1:T(8,128)(2,1)S(1)}, u32[]{:S(2)}, u32[]{:S(2)}) collective-permute-start(bf16[512,704]{0,1:T(8,128)(2,1)S(1)} %slice.127), channel_id=1, source_target_pairs={{0,8},{1,9},{2,10},{3,11},{4,12},{5,13},{6,14},{7,15},{8,0},{9,1},... | collective-permute-start | bytes 2162696 | tf_op jit(solution)/shard_map/ppermute | solution.py:140
  504.1 34.8 %collective-permute-start.30 = (bf16[2,2,64,2048]{3,2,1,0:T(8,128)(2,1)}, bf16[2,2,64,2048]{3,2,1,0:T(8,128)(2,1)}, u32[]{:S(2)}, u32[]{:S(2)}) collective-permute-start(bf16[2,2,64,2048]{3,2,1,0:T(8,128)(2,1)} %get-tuple-element.294), channel_id=1, source_target_pairs={{0,2},{1,3},{2,0},{3,1},{4,6},{5,7},{6,4},{7,5},{8,10},{9,11},{10,... | collective-permute-start | bytes 3145736 | tf_op jit(solution)/shard_map/ppermute | solution.py:140
  535.3 11.4 %collective-permute-start.29 = (bf16[256,704]{0,1:T(8,128)(2,1)S(1)}, bf16[256,704]{0,1:T(8,128)(2,1)S(1)}, u32[]{:S(2)}, u32[]{:S(2)}) collective-permute-start(bf16[256,704]{0,1:T(8,128)(2,1)S(1)} %bitcast.436), channel_id=1, source_target_pairs={{0,2},{1,3},{2,0},{3,1},{4,6},{5,7},{6,4},{7,5},{8,10},{9,11},{10,... | collective-permute-start | bytes 1081352 | tf_op jit(solution)/shard_map/ppermute | solution.py:140
  537.7 40.3 %collective-permute-start.31 = (bf16[2,2,256,512]{3,2,1,0:T(8,128)(2,1)}, bf16[2,2,256,512]{3,2,1,0:T(8,128)(2,1)}, u32[]{:S(2)}, u32[]{:S(2)}) collective-permute-start(bf16[2,2,256,512]{3,2,1,0:T(8,128)(2,1)} %get-tuple-element.293), channel_id=1, source_target_pairs={{0,2},{1,3},{2,0},{3,1},{4,6},{5,7},{6,4},{7,5},{8,10},{9,11},{10,... | collective-permute-start | bytes 3145736 | tf_op jit(solution)/shard_map/ppermute | solution.py:140
  548.1 32.5 %collective-permute-start.34 = (bf16[384,2048]{1,0:T(8,128)(2,1)}, bf16[384,2048]{1,0:T(8,128)(2,1)}, u32[]{:S(2)}, u32[]{:S(2)}) collective-permute-start(bf16[384,2048]{1,0:T(8,128)(2,1)} %slice.130), channel_id=1, source_target_pairs={{0,1},{1,0},{2,3},{3,2},{4,5},{5,4},{6,7},{7,6},{8,9},{9,8},{10,11... | collective-permute-start | bytes 4718600 | tf_op jit(solution)/shard_map/ppermute | solution.py:140
  549.9 6.4 collective-permute-start.33
  551.5 25.6 %collective-permute-start.32 = (bf16[2,64,2048]{2,1,0:T(8,128)(2,1)S(1)}, bf16[2,64,2048]{2,1,0:T(8,128)(2,1)S(1)}, u32[]{:S(2)}, u32[]{:S(2)}) collective-permute-start(bf16[2,64,2048]{2,1,0:T(8,128)(2,1)S(1)} %dynamic-slice_bitcast_fusion.14), channel_id=1, source_target_pairs={{0,4},{1,5},{2,6},{3,7},{4,0},{5,1},{6,2},{7,3},{8,12},{9,13},{10,... | collective-permute-start | bytes 1572872 | tf_op jit(solution)/shard_map/ppermute | solution.py:140
  552.9 34.4 %collective-permute-start.38 = (bf16[512,704]{0,1:T(8,128)(2,1)S(1)}, bf16[512,704]{0,1:T(8,128)(2,1)S(1)}, u32[]{:S(2)}, u32[]{:S(2)}) collective-permute-start(bf16[512,704]{0,1:T(8,128)(2,1)S(1)} %get-tuple-element.306), channel_id=1, source_target_pairs={{0,8},{1,9},{2,10},{3,11},{4,12},{5,13},{6,14},{7,15},{8,0},{9,1},... | collective-permute-start | bytes 2162696 | tf_op jit(solution)/shard_map/ppermute | solution.py:140
  556.3 45.5 %collective-permute-start.35 = (bf16[2,2,256,512]{3,2,1,0:T(8,128)(2,1)}, bf16[2,2,256,512]{3,2,1,0:T(8,128)(2,1)}, u32[]{:S(2)}, u32[]{:S(2)}) collective-permute-start(bf16[2,2,256,512]{3,2,1,0:T(8,128)(2,1)} %get-tuple-element.290), channel_id=1, source_target_pairs={{0,2},{1,3},{2,0},{3,1},{4,6},{5,7},{6,4},{7,5},{8,10},{9,11},{10,... | collective-permute-start | bytes 3145736 | tf_op jit(solution)/shard_map/ppermute | solution.py:140
  589.2 16.9 %collective-permute-start.39 = (bf16[256,704]{0,1:T(8,128)(2,1)S(1)}, bf16[256,704]{0,1:T(8,128)(2,1)S(1)}, u32[]{:S(2)}, u32[]{:S(2)}) collective-permute-start(bf16[256,704]{0,1:T(8,128)(2,1)S(1)} %bitcast.433), channel_id=1, source_target_pairs={{0,2},{1,3},{2,0},{3,1},{4,6},{5,7},{6,4},{7,5},{8,10},{9,11},{10,... | collective-permute-start | bytes 1081352 | tf_op jit(solution)/shard_map/ppermute | solution.py:140
  590.2 15.2 %collective-permute-start.37 = (bf16[64,2048]{1,0:T(8,128)(2,1)S(1)}, bf16[64,2048]{1,0:T(8,128)(2,1)S(1)}, u32[]{:S(2)}, u32[]{:S(2)}) collective-permute-start(bf16[64,2048]{1,0:T(8,128)(2,1)S(1)} %dynamic-slice_bitcast_fusion.18), channel_id=1, source_target_pairs={{0,8},{1,9},{2,10},{3,11},{4,12},{5,13},{6,14},{7,15},{8,0},{9,1},... | collective-permute-start | bytes 786440 | tf_op jit(solution)/shard_map/ppermute | solution.py:140
  590.4 19.3 %collective-permute-start.36 = (bf16[2,256,512]{2,1,0:T(8,128)(2,1)S(1)}, bf16[2,256,512]{2,1,0:T(8,128)(2,1)S(1)}, u32[]{:S(2)}, u32[]{:S(2)}) collective-permute-start(bf16[2,256,512]{2,1,0:T(8,128)(2,1)S(1)} %dynamic-slice_bitcast_fusion.13), channel_id=1, source_target_pairs={{0,4},{1,5},{2,6},{3,7},{4,0},{5,1},{6,2},{7,3},{8,12},{9,13},{10,... | collective-permute-start | bytes 1572872 | tf_op jit(solution)/shard_map/ppermute | solution.py:140
  596.5 20.8 %collective-permute-start.44 = (bf16[192,2048]{1,0:T(8,128)(2,1)}, bf16[192,2048]{1,0:T(8,128)(2,1)}, u32[]{:S(2)}, u32[]{:S(2)}) collective-permute-start(bf16[192,2048]{1,0:T(8,128)(2,1)} %slice.199), channel_id=1, source_target_pairs={{0,16},{1,17},{2,18},{3,19},{4,20},{5,21},{6,22},{7,23},{8,24},{9,... | collective-permute-start | bytes 2359304 | tf_op jit(solution)/shard_map/ppermute | solution.py:140
  601.7 27.9 %collective-permute-start.40 = (bf16[2,2,256,512]{3,2,1,0:T(8,128)(2,1)}, bf16[2,2,256,512]{3,2,1,0:T(8,128)(2,1)}, u32[]{:S(2)}, u32[]{:S(2)}) collective-permute-start(bf16[2,2,256,512]{3,2,1,0:T(8,128)(2,1)} %get-tuple-element.289), channel_id=1, source_target_pairs={{0,2},{1,3},{2,0},{3,1},{4,6},{5,7},{6,4},{7,5},{8,10},{9,11},{10,... | collective-permute-start | bytes 3145736 | tf_op jit(solution)/shard_map/ppermute | solution.py:140
  610.6 28.9 %collective-permute-start.48 = (bf16[2,2,128,704]{2,3,1,0:T(8,128)(2,1)}, bf16[2,2,128,704]{2,3,1,0:T(8,128)(2,1)}, u32[]{:S(2)}, u32[]{:S(2)}) collective-permute-start(bf16[2,2,128,704]{2,3,1,0:T(8,128)(2,1)} %pad_maximum_fusion.20), channel_id=1, source_target_pairs={{0,16},{1,17},{2,18},{3,19},{4,20},{5,21},{6,22},{7,23},{8,24},{9,... | collective-permute-start | bytes 2162696 | tf_op jit(solution)/shard_map/ppermute | solution.py:140
  613.9 15.5 %collective-permute-start.43 = (bf16[2,128,704]{1,2,0:T(8,128)(2,1)S(1)}, bf16[2,128,704]{1,2,0:T(8,128)(2,1)S(1)}, u32[]{:S(2)}, u32[]{:S(2)}) collective-permute-start(bf16[2,128,704]{1,2,0:T(8,128)(2,1)S(1)} %bitcast.434), channel_id=1, source_target_pairs={{0,1},{1,0},{2,3},{3,2},{4,5},{5,4},{6,7},{7,6},{8,9},{9,8},{10,11... | collective-permute-start | bytes 1081352 | tf_op jit(solution)/shard_map/ppermute | solution.py:140
  614.0 15.3 %collective-permute-start.42 = (bf16[256,512]{1,0:T(8,128)(2,1)S(1)}, bf16[256,512]{1,0:T(8,128)(2,1)S(1)}, u32[]{:S(2)}, u32[]{:S(2)}) collective-permute-start(bf16[256,512]{1,0:T(8,128)(2,1)S(1)} %dynamic-slice_bitcast_fusion.17), channel_id=1, source_target_pairs={{0,8},{1,9},{2,10},{3,11},{4,12},{5,13},{6,14},{7,15},{8,0},{9,1},... | collective-permute-start | bytes 786440 | tf_op jit(solution)/shard_map/ppermute | solution.py:140
  617.3 18.9 %collective-permute-start.41 = (bf16[2,256,512]{2,1,0:T(8,128)(2,1)S(1)}, bf16[2,256,512]{2,1,0:T(8,128)(2,1)S(1)}, u32[]{:S(2)}, u32[]{:S(2)}) collective-permute-start(bf16[2,256,512]{2,1,0:T(8,128)(2,1)S(1)} %dynamic-slice_bitcast_fusion.12), channel_id=1, source_target_pairs={{0,4},{1,5},{2,6},{3,7},{4,0},{5,1},{6,2},{7,3},{8,12},{9,13},{10,... | collective-permute-start | bytes 1572872 | tf_op jit(solution)/shard_map/ppermute | solution.py:140
  636.4 3.0 collective-permute-start.47
  636.5 14.4 %collective-permute-start.46 = (bf16[256,512]{1,0:T(8,128)(2,1)S(1)}, bf16[256,512]{1,0:T(8,128)(2,1)S(1)}, u32[]{:S(2)}, u32[]{:S(2)}) collective-permute-start(bf16[256,512]{1,0:T(8,128)(2,1)S(1)} %dynamic-slice_bitcast_fusion.16), channel_id=1, source_target_pairs={{0,8},{1,9},{2,10},{3,11},{4,12},{5,13},{6,14},{7,15},{8,0},{9,1},... | collective-permute-start | bytes 786440 | tf_op jit(solution)/shard_map/ppermute | solution.py:140
  636.6 20.1 %collective-permute-start.45 = (bf16[2,256,512]{2,1,0:T(8,128)(2,1)S(1)}, bf16[2,256,512]{2,1,0:T(8,128)(2,1)S(1)}, u32[]{:S(2)}, u32[]{:S(2)}) collective-permute-start(bf16[2,256,512]{2,1,0:T(8,128)(2,1)S(1)} %dynamic-slice_bitcast_fusion.11), channel_id=1, source_target_pairs={{0,4},{1,5},{2,6},{3,7},{4,0},{5,1},{6,2},{7,3},{8,12},{9,13},{10,... | collective-permute-start | bytes 1572872 | tf_op jit(solution)/shard_map/ppermute | solution.py:140
  638.8 20.8 %collective-permute-start.52 = (bf16[2,2,128,704]{2,3,1,0:T(8,128)(2,1)S(1)}, bf16[2,2,128,704]{2,3,1,0:T(8,128)(2,1)S(1)}, u32[]{:S(2)}, u32[]{:S(2)}) collective-permute-start(bf16[2,2,128,704]{2,3,1,0:T(8,128)(2,1)S(1)} %pad_maximum_fusion.22), channel_id=1, source_target_pairs={{0,16},{1,17},{2,18},{3,19},{4,20},{5,21},{6,22},{7,23},{8,24},{9,... | collective-permute-start | bytes 2162696 | tf_op jit(solution)/shard_map/ppermute | solution.py:140
  656.9 2.6 collective-permute-start.50
  657.0 18.3 %collective-permute-start.53 = (bf16[64,2048]{1,0:T(8,128)(2,1)}, bf16[64,2048]{1,0:T(8,128)(2,1)S(1)}, u32[]{:S(2)}, u32[]{:S(2)}) collective-permute-start(bf16[64,2048]{1,0:T(8,128)(2,1)} %fusion.203), channel_id=1, source_target_pairs={{0,16},{1,17},{2,18},{3,19},{4,20},{5,21},{6,22},{7,23},{8,24},{9,... | collective-permute-start | bytes 786440 | tf_op jit(solution)/shard_map/ppermute | solution.py:140
  657.6 14.4 %collective-permute-start.49 = (bf16[256,512]{1,0:T(8,128)(2,1)S(1)}, bf16[256,512]{1,0:T(8,128)(2,1)S(1)}, u32[]{:S(2)}, u32[]{:S(2)}) collective-permute-start(bf16[256,512]{1,0:T(8,128)(2,1)S(1)} %dynamic-slice_bitcast_fusion.15), channel_id=1, source_target_pairs={{0,8},{1,9},{2,10},{3,11},{4,12},{5,13},{6,14},{7,15},{8,0},{9,1},... | collective-permute-start | bytes 786440 | tf_op jit(solution)/shard_map/ppermute | solution.py:140
  657.9 16.0 %collective-permute-start.56 = (bf16[2,1,128,512]{3,2,0,1:T(8,128)(2,1)S(1)}, bf16[2,1,128,512]{3,2,0,1:T(8,128)(2,1)S(1)}, u32[]{:S(2)}, u32[]{:S(2)}) collective-permute-start(bf16[2,1,128,512]{3,2,0,1:T(8,128)(2,1)S(1)} %pad_maximum_fusion.28), channel_id=1, source_target_pairs={{0,16},{1,17},{2,18},{3,19},{4,20},{5,21},{6,22},{7,23},{8,24},{9,... | collective-permute-start | bytes 786440 | tf_op jit(solution)/shard_map/ppermute | solution.py:140
  672.1 4.2 collective-permute-start.51
  672.2 21.2 %collective-permute-start.54 = (bf16[2,1,128,512]{3,2,0,1:T(8,128)(2,1)S(1)}, bf16[2,1,128,512]{3,2,0,1:T(8,128)(2,1)}, u32[]{:S(2)}, u32[]{:S(2)}) collective-permute-start(bf16[2,1,128,512]{3,2,0,1:T(8,128)(2,1)S(1)} %bitcast.413), channel_id=1, source_target_pairs={{0,16},{1,17},{2,18},{3,19},{4,20},{5,21},{6,22},{7,23},{8,24},{9,... | collective-permute-start | bytes 786440 | tf_op jit(solution)/shard_map/ppermute | solution.py:140
  678.2 16.7 %collective-permute-start.55 = (bf16[2,1,128,512]{3,2,0,1:T(8,128)(2,1)}, bf16[2,1,128,512]{3,2,0,1:T(8,128)(2,1)}, u32[]{:S(2)}, u32[]{:S(2)}) collective-permute-start(bf16[2,1,128,512]{3,2,0,1:T(8,128)(2,1)} %bitcast.121), channel_id=1, source_target_pairs={{0,16},{1,17},{2,18},{3,19},{4,20},{5,21},{6,22},{7,23},{8,24},{9,... | collective-permute-start | bytes 786440 | tf_op jit(solution)/shard_map/ppermute | solution.py:140
  (105 other events, 760.3 us)
Sparse Core Ops, SparseCore 0:
  16.2 134.7 all-gather.3
  152.9 44.8 all-gather.7
  246.2 44.8 all-gather.5
  355.8 60.6 reduce-scatter.2
  429.6 59.9 reduce-scatter.4
